TPU v7x, 32 devices: a whole 2x2x4 slice. The times are simulated.
32 devices in a mesh: seq: 4 (over z), exp: 2 (over x), tp: 4 (over y, core).
Axes of the slice: x: 2, y: 2, z: 4, core: 2. Of those that a mesh axis runs over, the one named last changes fastest.
Arguments:
- query_heads: bfloat16 [1024, 32, 128], P(('seq', 'exp'), 'tp'), may hold values from -10 to 10
- key_heads: bfloat16 [1024, 8, 128], P(('seq', 'exp'), 'tp'), may hold values from -10 to 10
- value_head_rows: bfloat16 [1024, 8, 128], P(('seq', 'exp'), 'tp'), may hold values from -6 to 6
- state_input: bfloat16 [1024, 4096], P(('seq', 'exp'), 'tp'), may hold values from -6 to 6
- state_gate: bfloat16 [1024, 4096], P(('seq', 'exp'), 'tp'), may hold values from -6 to 6
- state_inflow: bfloat16 [1024, 8, 128], P(('seq', 'exp'), 'tp'), may hold values from -6 to 6
- state_readout: bfloat16 [1024, 8, 128], P(('seq', 'exp'), 'tp'), may hold values from -6 to 6
- step_size: float32 [1024, 64], P(('seq', 'exp'), 'tp'), may hold values from 0.01 to 0.1
- log_decay: float32 [1024, 64], P(('seq', 'exp'), 'tp'), may hold values from -1 to 0
- skip_scale: float32 [64], P('tp'), may hold values from 0.5 to 2
- state_gain: float32 [4096], P('tp'), may hold values from 0.25 to 1.75
- hidden_in: bfloat16 [1024, 2048], P(('seq', 'exp')), may hold values from -400 to 400
- mlp_gain: float32 [2048], replicated, may hold values from 0.25 to 1.75
- router_weight: bfloat16 [2048, 8], replicated, may hold values from -0.125 to 0.125
- expert_ids: int32 [1024, 2], P(('seq', 'exp')), may hold values from 0 to 7, as said below
- slot_index: int32 [1024, 2], P(('seq', 'exp')), may hold values from -1 to 39, as said below
- gate_up: bfloat16 [8, 7168, 2, 2048], P('exp', ('seq', 'tp')), may hold values from -0.125 to 0.125
- down_proj: bfloat16 [8, 7168, 2048], P('exp', ('seq', 'tp')), may hold values from -0.0625 to 0.0625
Outputs:
- window_out: bfloat16 [1024, 32, 128], P(('seq', 'exp'), 'tp')
- state_out: bfloat16 [1024, 4096], P(('seq', 'exp'), 'tp')
- routed_out: bfloat16 [1024, 2048], P(('seq', 'exp'), 'tp')
Inputs may be any that keep to these rules, and one draw needn't show every extreme that they name: `expert_ids`: the 2 ids of a row differ. slot_index[t, k] is the place of the choice expert_ids[t, k] in that expert's buffer of 40 places for the 128 rows of the device block that holds row t (rows b * 128 to b * 128 + 127); the live places of one expert within one block are distinct; -1 marks a dropped choice.
All inputs are finite; a program needn't handle non-finite values.
Results may differ from a plain program's by a relative error of at most 0.02.
Values may be sent and summed in bfloat16 or wider, within the bound.
No kernel may reach another device: no remote copies, remote signals or barrier semaphores. Data moves between devices by JAX's collectives and lax.ppermute only.
A program may use at most 192 MiB of HBM per device.

v0:
```python
import math

import jax
import jax.numpy as jnp
from jax import lax
from jax.sharding import PartitionSpec as P

EXPERTS = 8
WINDOW = 4096
HP = 64
NS = 128
STRETCH = 128
CAP = 40


EPSILON = 1e-05


def from_behind(block, axis, distance):
    devices = range(lax.axis_size(axis))
    route = [(i - distance, i) for i in devices if i - distance in devices]
    return lax.ppermute(block, axis, route)


def carried_in(shard, axis, join, neutral):
    place = lax.axis_index(axis)
    gathered = jax.tree.map(
        lambda a, kind: lax.all_gather(a.astype(kind), axis),
        shard,
        jax.tree.map(lambda a: jnp.bfloat16 if a.dtype == jnp.float32 else a.dtype, shard),
    )
    state = jax.tree.map(lambda a, e: jnp.zeros_like(a) + jnp.asarray(e, a.dtype), shard, neutral)

    def one(lap, state):
        return join(
            state,
            jax.tree.map(
                lambda a, own: lax.dynamic_index_in_dim(a, lap, 0, False).astype(own.dtype),
                gathered,
                shard,
            ),
        )

    return lax.fori_loop(0, place, one, state)


def combine_states(earlier, later):
    earlier_decay, earlier_state = earlier
    later_decay, later_state = later
    return (earlier_decay * later_decay, later_decay[..., None, None] * earlier_state + later_state)


def attend_range(running, query_rows, query_pos, key_row_list, value_rows, key_start):
    total_keys = key_row_list.shape[0]
    block_width = math.gcd(total_keys, 1024)
    blocks = total_keys // block_width
    shared_heads = key_row_list.shape[1]
    head_dim = key_row_list.shape[2]
    score_scale = 1.0 / math.sqrt(head_dim)
    key_blocks = key_row_list.reshape(blocks, block_width, shared_heads, head_dim)
    value_blocks = value_rows.reshape(blocks, block_width, shared_heads, head_dim)

    def one_block(carried, packed):
        run_max, run_sum, accumulated = carried
        key_block, value_block, counter = packed
        scores = (
            jnp.einsum("qkgd,jkd->kgqj", query_rows, key_block, preferred_element_type=jnp.float32)
            * score_scale
        )
        key_pos = key_start + counter * block_width + jnp.arange(block_width, dtype=jnp.int32)
        visible = (
            (key_pos[None, :] <= query_pos[:, None])
            & (key_pos[None, :] > query_pos[:, None] - WINDOW)
            & (key_pos[None, :] >= 0)
        )
        scores = jnp.where(visible, scores, -jnp.inf)
        new_max = jnp.maximum(run_max, jnp.max(scores, axis=-1))
        safe_max = jnp.where(new_max == -jnp.inf, 0.0, new_max)
        weights = jnp.exp(scores - safe_max[..., None])
        rescale = jnp.exp(run_max - safe_max)
        run_sum = run_sum * rescale + jnp.sum(weights, axis=-1)
        accumulated = accumulated * rescale[..., None] + jnp.einsum(
            "kgqj,jkd->kgqd",
            weights.astype(jnp.bfloat16),
            value_block,
            preferred_element_type=jnp.float32,
        )
        return ((new_max, run_sum, accumulated), None)

    running, _ = lax.scan(
        one_block, running, (key_blocks, value_blocks, jnp.arange(blocks, dtype=jnp.int32))
    )
    return running


def attention(query_heads, key_heads, value_head_rows):
    row_count, query_count, head_dim = query_heads.shape
    shared_heads = key_heads.shape[1]
    group_width = query_count // shared_heads
    seq_count = lax.axis_size("seq")
    exp_count = lax.axis_size("exp")
    seq_index = lax.axis_index("seq")
    position = seq_index * exp_count + lax.axis_index("exp")
    query_pos = position * row_count + jnp.arange(row_count, dtype=jnp.int32)
    query_rows = query_heads.reshape(row_count, shared_heads, group_width, head_dim)
    running = (
        jnp.full((shared_heads, group_width, row_count), -jnp.inf, jnp.float32),
        jnp.zeros((shared_heads, group_width, row_count), jnp.float32),
        jnp.zeros((shared_heads, group_width, row_count, head_dim), jnp.float32),
    )
    relay_depth = min(-(-WINDOW // row_count), seq_count * exp_count - 1)
    stacked = jnp.stack((key_heads, value_head_rows))
    buffer = jnp.zeros((2, relay_depth) + key_heads.shape, jnp.bfloat16)

    def relay_block(counter, carried):
        moving, stored = carried
        moving = from_behind(moving, ("seq", "exp"), 1)
        stored = lax.dynamic_update_index_in_dim(stored, moving, relay_depth - 1 - counter, 1)
        return (moving, stored)

    stored = lax.fori_loop(0, relay_depth, relay_block, (stacked, buffer))[1]
    window_rows = stored.reshape(2, relay_depth * row_count, shared_heads, head_dim)
    running = attend_range(
        running,
        query_rows,
        query_pos,
        window_rows[0],
        window_rows[1],
        (position - relay_depth) * row_count,
    )
    running = attend_range(
        running, query_rows, query_pos, key_heads, value_head_rows, position * row_count
    )
    run_max, run_sum, accumulated = running
    outputs = accumulated / run_sum[..., None]
    outputs = jnp.transpose(outputs, (2, 0, 1, 3)).reshape(row_count, query_count, head_dim)
    return outputs.astype(jnp.bfloat16)


def state_space(
    state_input,
    state_gate,
    state_inflow,
    state_readout,
    step_size,
    log_decay,
    skip_scale,
    state_gain,
):
    row_count, channels = state_input.shape
    heads = step_size.shape[1]
    groups = state_inflow.shape[1]
    per_group = heads // groups
    stretch_count = row_count // STRETCH
    inputs = state_input.reshape(stretch_count, STRETCH, groups, per_group, HP)
    inflow = state_inflow.reshape(stretch_count, STRETCH, groups, NS)
    readout = state_readout.reshape(stretch_count, STRETCH, groups, NS)
    step_rows = step_size.reshape(stretch_count, STRETCH, groups, per_group)
    cumulative = jnp.cumsum(log_decay.reshape(stretch_count, STRETCH, groups, per_group), axis=1)
    read_write = jnp.einsum("cign,cjgn->cijg", readout, inflow, preferred_element_type=jnp.float32)
    causal = (jnp.arange(STRETCH)[:, None] >= jnp.arange(STRETCH)[None, :])[None, :, :, None, None]
    decay_gap = cumulative[:, :, None] - cumulative[:, None]
    decay_mat = jnp.where(causal, jnp.exp(jnp.where(causal, decay_gap, 0.0)), 0.0)
    mixing = (decay_mat * read_write[..., None] * step_rows[:, None]).astype(jnp.bfloat16)
    intra = jnp.einsum("cijgk,cjgkp->cigkp", mixing, inputs, preferred_element_type=jnp.float32)
    stretch_total = cumulative[:, -1]
    weight_in = jnp.exp(stretch_total[:, None] - cumulative) * step_rows
    weighted = (weight_in[..., None] * inflow[:, :, :, None, :]).astype(jnp.bfloat16)
    stretch_state = jnp.einsum(
        "cjgkn,cjgkp->cgknp", weighted, inputs, preferred_element_type=jnp.float32
    )

    def carry_stretch(carried, packed):
        stretch_decay, state_piece = packed
        return (stretch_decay[..., None, None] * carried + state_piece, carried)

    initial = jnp.zeros((groups, per_group, NS, HP), jnp.float32)
    device_state, entering_local = lax.scan(
        carry_stretch, initial, (jnp.exp(stretch_total), stretch_state)
    )
    device_decay = jnp.exp(jnp.sum(stretch_total, axis=0))
    summary = (device_decay, device_state)
    identity = (jnp.ones_like(device_decay), jnp.zeros_like(device_state))
    entering = carried_in(summary, ("seq", "exp"), combine_states, identity)[1]
    prefix = jnp.exp(jnp.cumsum(stretch_total, axis=0) - stretch_total)
    stretch_entering = entering_local + prefix[..., None, None] * entering[None]
    inter = jnp.exp(cumulative)[..., None] * jnp.einsum(
        "cign,cgknp->cigkp",
        readout.astype(jnp.float32),
        stretch_entering,
        precision=lax.Precision.HIGHEST,
    )
    skip_rows = skip_scale.reshape(groups, per_group)
    output = intra + inter + skip_rows[:, :, None] * inputs.astype(jnp.float32)
    gate_rows = state_gate.reshape(stretch_count, STRETCH, groups, per_group, HP).astype(
        jnp.float32
    )
    gated = output * jax.nn.silu(gate_rows)
    mean_square = jnp.mean(gated * gated, axis=(3, 4), keepdims=True)
    normed = gated * lax.rsqrt(mean_square + EPSILON)
    return (normed.reshape(row_count, channels) * state_gain).astype(jnp.bfloat16)


def routed(hidden_in, mlp_gain, router_weight, expert_ids, slot_index, gate_up, down_proj):
    row_count = hidden_in.shape[0]
    hidden = hidden_in.astype(jnp.float32)
    mean_square = jnp.mean(hidden * hidden, axis=-1, keepdims=True)
    normed = (hidden * lax.rsqrt(mean_square + EPSILON) * mlp_gain).astype(jnp.bfloat16)
    logits = jnp.dot(normed, router_weight, preferred_element_type=jnp.float32)
    gate_values = jax.nn.sigmoid(logits)
    one_hot = expert_ids[..., None] == jnp.arange(EXPERTS, dtype=jnp.int32)
    chosen = jnp.sum(jnp.where(one_hot, gate_values[:, None, :], 0.0), axis=-1)
    mixing = chosen / jnp.sum(chosen, axis=1, keepdims=True)
    is_live = slot_index >= 0
    target = jnp.where(is_live, expert_ids * CAP + slot_index, -1)
    tp_count = lax.axis_size("tp")
    tp_index = lax.axis_index("tp")
    quarter = CAP // tp_count
    place_ids = (
        jnp.arange(EXPERTS, dtype=jnp.int32)[None, :] * CAP
        + tp_index * quarter
        + jnp.arange(quarter, dtype=jnp.int32)[:, None]
    )
    picker = jnp.any(place_ids[:, :, None, None] == target[None, None], axis=-1)
    picker = picker.reshape(quarter * EXPERTS, row_count).astype(jnp.bfloat16)
    outgoing = jnp.dot(picker, normed, preferred_element_type=jnp.float32).astype(jnp.bfloat16)
    outgoing = outgoing.reshape(quarter, EXPERTS, normed.shape[1])
    received = lax.all_to_all(outgoing, "exp", split_axis=1, concat_axis=0, tiled=True)
    all_rows = lax.all_gather(received, "seq", axis=0, tiled=True)
    wide_gate_up, wide_down = (
        lax.all_gather(gate_up, "tp", axis=1, tiled=True),
        lax.all_gather(down_proj, "tp", axis=1, tiled=True),
    )
    projected = jnp.einsum(
        "rld,lfsd->srlf", all_rows, wide_gate_up, preferred_element_type=jnp.float32
    )
    hidden_units = (jax.nn.silu(projected[0]) * projected[1]).astype(jnp.bfloat16)
    summed = lax.psum_scatter(
        jnp.einsum(
            "rlf,lfd->rld", hidden_units, wide_down, preferred_element_type=jnp.float32
        ).astype(jnp.bfloat16),
        "seq",
        scatter_dimension=0,
        tiled=True,
    ).astype(jnp.float32)
    returned_rows = lax.all_to_all(
        summed.astype(jnp.bfloat16), "exp", split_axis=0, concat_axis=1, tiled=True
    ).astype(summed.dtype)
    flat_rows = returned_rows.reshape(quarter * EXPERTS, returned_rows.shape[2])
    in_quarter = is_live & (slot_index // quarter == tp_index)
    place = (slot_index - tp_index * quarter) * EXPERTS + expert_ids
    picked = flat_rows[jnp.where(in_quarter, place, 0)]
    partial_value = jnp.sum(jnp.where(in_quarter, mixing, 0.0)[..., None] * picked, axis=1)
    return lax.psum_scatter(
        partial_value.astype(jnp.bfloat16), "tp", scatter_dimension=1, tiled=True
    )


def local(
    query_heads,
    key_heads,
    value_head_rows,
    state_input,
    state_gate,
    state_inflow,
    state_readout,
    step_size,
    log_decay,
    skip_scale,
    state_gain,
    hidden_in,
    mlp_gain,
    router_weight,
    expert_ids,
    slot_index,
    gate_up,
    down_proj,
):
    window_out = attention(query_heads, key_heads, value_head_rows)
    state_out = state_space(
        state_input,
        state_gate,
        state_inflow,
        state_readout,
        step_size,
        log_decay,
        skip_scale,
        state_gain,
    )
    routed_out = routed(
        hidden_in, mlp_gain, router_weight, expert_ids, slot_index, gate_up, down_proj
    )
    return (window_out, state_out, routed_out)


def solution(mesh):
    return jax.shard_map(
        local,
        mesh=mesh,
        in_specs=(
            P(("seq", "exp"), "tp", None),
            P(("seq", "exp"), "tp", None),
            P(("seq", "exp"), "tp", None),
            P(("seq", "exp"), "tp"),
            P(("seq", "exp"), "tp"),
            P(("seq", "exp"), "tp", None),
            P(("seq", "exp"), "tp", None),
            P(("seq", "exp"), "tp"),
            P(("seq", "exp"), "tp"),
            P("tp"),
            P("tp"),
            P(("seq", "exp"), None),
            P(),
            P(),
            P(("seq", "exp"), None),
            P(("seq", "exp"), None),
            P("exp", ("seq", "tp"), None, None),
            P("exp", ("seq", "tp"), None),
        ),
        out_specs=(P(("seq", "exp"), "tp", None), P(("seq", "exp"), "tp"), P(("seq", "exp"), "tp")),
        check_vma=False,
    )
```

profile of v0, /device:TPU:0, one launch (start us, length us, event | category | flops | bytes accessed | tf_op | source)
XLA Modules:
  0.0 794.4 jit_solution(15744291993359428038)
XLA Ops:
  8.1 1.2 fusion.34
  9.3 1.4 fusion.33
  10.7 0.7 select_reduce_fusion
  11.4 0.7 divide_select_fusion
  12.1 0.7 compare_select_fusion.2
  12.9 1.4 fusion.18
  14.5 12.0 %all_to_all.27 = bf16[10,8,2048]{2,0,1:T(8,128)(2,1)S(1)} all-to-all(bf16[10,8,2048]{2,0,1:T(8,128)(2,1)S(1)} %copy.233), channel_id=1, replica_groups=mesh['seq'=4,'exp'=2,'tp'=4] {'exp'}, dimensions={1} | all-to-all | bytes 655360 | tf_op jit(solution)/shard_map/all_to_all | solution.py:228
  26.5 1.0 copy.260
  27.6 16.4 %copy.236 = bf16[4,448,2,2048]{3,1,2,0:T(8,128)(2,1)} copy(bf16[4,448,2,2048]{3,2,1,0:T(2,128)(2,1)} %param.40) | data formatting | bytes 29360128 | tf_op args[16]
  44.0 0.7 all-gather.11.cloned.1.call-update
  44.7 15.9 %all-gather.7.cloned.1.call-done = bf16[80,4,2048]{2,1,0:T(4,128)(2,1)} async-done(((bf16[20,4,2048]{2,1,0:T(4,128)(2,1)}), bf16[80,4,2048]{2,1,0:T(4,128)(2,1)}) %all-gather.7.cloned.1.call-update) | async-done | bytes 1310736 | tf_op jit(solution)/shard_map/all_gather | solution.py:229
  60.6 345.7 %all-gather.9.cloned.1.call-done = bf16[4,1792,2,2048]{3,1,2,0:T(8,128)(2,1)} async-done(((bf16[4,448,2,2048]{3,1,2,0:T(8,128)(2,1)}), bf16[4,1792,2,2048]{3,1,2,0:T(8,128)(2,1)}) %all-gather.9.cloned.1.call-update) | async-done | bytes 58720272 | tf_op jit(solution)/shard_map/all_gather | solution.py:231
  406.3 33.7 %convolution_bitcast_fusion = f32[2,80,4,1792]{3,1,0,2:T(8,128)} fusion(bf16[4,1792,2,2048]{3,1,2,0:T(8,128)(2,1)} %all-gather.9.cloned.1.call-done, bf16[80,4,2048,1]{2,1,0,3:T(4,128)(2,1)} %bitcast.148), kind=kOutput, calls=%fused_computation.31 | convolution fusion | flops 4697620480 | bytes 64618496 | tf_op jit(solution)/shard_map/rld,lfsd->srlf/dot_general | solution.py:234
  440.0 145.5 %all-gather.11.cloned.1.call-done = bf16[4,1792,2048]{2,1,0:T(8,128)(2,1)} async-done(((bf16[4,448,2048]{2,1,0:T(8,128)(2,1)}), bf16[4,1792,2048]{2,1,0:T(8,128)(2,1)}) %all-gather.11.cloned.1.call-update) | async-done | bytes 29360144 | tf_op jit(solution)/shard_map/all_gather | solution.py:232
  585.6 15.8 %fusion.15 = bf16[80,4,2048]{2,0,1:T(8,128)(2,1)S(1)} fusion(bf16[4,1792,2048]{2,1,0:T(8,128)(2,1)} %all-gather.11.cloned.1.call-done, f32[2,80,4,1792]{3,1,0,2:T(8,128)} %convolution_bitcast_fusion), kind=kOutput, calls=%fused_computation.33 | convolution fusion | flops 2352906240 | bytes 35258368 | tf_op jit(solution)/shard_map/rlf,lfd->rld/dot_general | solution.py:239
  601.4 2.1 copy.239
  604.4 0.6 subtract_exponential_fusion.4
  605.0 1.2 fusion.27
  606.8 72.6 %while.14 = (s32[]{:T(128)}, bf16[2,128,2,128]{3,2,1,0:T(2,128)(2,1)S(1)}, bf16[2,7,128,2,128]{4,2,3,1,0:T(8,128)(2,1)S(1)}, s32[]{:T(128)}, s32[]{:T(128)}, /*index=5*/s32[]{:T(128)}, s32[]{:T(128)}) while((s32[]{:T(128)}, bf16[2,128,2,128]{3,2,1,0:T(2,128)(2,1)S(1)}, bf16[2,7,128,2,128]{4,2,3,1,0:T(8,128)(2,1)S(1)}, s32[]{:T(128)}, ...), condition=%wide.region_1.2_spmd, body=%wide.region_0.1_spmd.sunk | while | flops 6 | bytes 1048743 | solution.py:121
  606.8 3.4 collective-permute-start
  610.2 3.1 collective-permute-done
  613.5 6.7 collective-permute-start
  620.2 2.5 collective-permute-done
  622.8 9.0 %collective-permute-start = (bf16[2,128,2,128]{3,2,1,0:T(2,128)(2,1)S(1)}, bf16[2,128,2,128]{3,2,1,0:T(2,128)(2,1)S(1)}, u32[]{:S(2)}, u32[]{:S(2)}) collective-permute-start(bf16[2,128,2,128]{3,2,1,0:T(2,128)(2,1)S(1)} %get-tuple-element.571), channel_id=1, source_target_pairs={{0,4},{4,8},{8,12},{12,16},{16,20},{20,24},{24,28},{1,5},{5,9},{9,... | collective-permute-start | bytes 393224 | tf_op jit(solution)/shard_map/while/body/eval_jaxpr/ppermute | solution.py:22
  631.9 2.5 collective-permute-done
  634.5 8.8 %collective-permute-start = (bf16[2,128,2,128]{3,2,1,0:T(2,128)(2,1)S(1)}, bf16[2,128,2,128]{3,2,1,0:T(2,128)(2,1)S(1)}, u32[]{:S(2)}, u32[]{:S(2)}) collective-permute-start(bf16[2,128,2,128]{3,2,1,0:T(2,128)(2,1)S(1)} %get-tuple-element.571), channel_id=1, source_target_pairs={{0,4},{4,8},{8,12},{12,16},{16,20},{20,24},{24,28},{1,5},{5,9},{9,... | collective-permute-start | bytes 393224 | tf_op jit(solution)/shard_map/while/body/eval_jaxpr/ppermute | solution.py:22
  643.3 2.5 collective-permute-done
  645.9 7.4 collective-permute-start
  653.4 2.5 collective-permute-done
  656.0 8.6 %collective-permute-start = (bf16[2,128,2,128]{3,2,1,0:T(2,128)(2,1)S(1)}, bf16[2,128,2,128]{3,2,1,0:T(2,128)(2,1)S(1)}, u32[]{:S(2)}, u32[]{:S(2)}) collective-permute-start(bf16[2,128,2,128]{3,2,1,0:T(2,128)(2,1)S(1)} %get-tuple-element.571), channel_id=1, source_target_pairs={{0,4},{4,8},{8,12},{12,16},{16,20},{20,24},{24,28},{1,5},{5,9},{9,... | collective-permute-start | bytes 393224 | tf_op jit(solution)/shard_map/while/body/eval_jaxpr/ppermute | solution.py:22
  664.7 5.4 collective-permute-done
  670.2 6.5 collective-permute-start
  676.7 2.5 collective-permute-done
  679.5 15.8 %while.57 = (s32[]{:T(128)}, f32[2,4,128]{2,1,0:T(4,128)S(1)}, f32[2,4,128]{2,1,0:T(4,128)S(1)}, f32[2,4,128,128]{3,2,1,0:T(8,128)S(1)}, s32[7]{0:T(128)S(1)}, /...) while((s32[]{:T(128)}, f32[2,4,128]{2,1,0:T(4,128)S(1)}, ...), condition=%wide.region_5.6_spmd.clone, body=%wide.region_2.5_spmd.clone.sunk | while | flops 68494976 | bytes 3120577 | solution.py:90
  679.5 0.6 dynamic_slice.68
  681.3 0.4 convolution_add_fusion.4
  681.8 0.6 dynamic_slice.68
  683.5 0.4 convolution_add_fusion.4
  684.0 0.6 dynamic_slice.68
  686.3 0.6 dynamic_slice.68
  688.5 0.6 dynamic_slice.68
  690.3 0.4 convolution_add_fusion.4
  690.8 0.6 dynamic_slice.68
  692.6 0.4 convolution_add_fusion.4
  693.0 0.6 dynamic_slice.68
  694.8 0.4 convolution_add_fusion.4
  695.3 0.9 copy.229
  697.2 0.9 copy.242
  698.1 1.0 copy.230
  699.2 0.8 copy.221
  700.0 0.6 mul.302
  701.0 0.7 dynamic-slice.3
  702.3 37.5 %all-gather = bf16[8,1,2,8]{3,2,1,0:T(2,128)(2,1)S(1)} all-gather(bf16[1,1,2,8]{3,2,1,0:T(2,128)(2,1)S(1)} %get-tuple-element.424), channel_id=2, replica_groups=mesh['seq'=4,'exp'=2,'tp'=4] {'seq','exp'}, dimensions={0}, use_global_device_ids=true | all-gather | bytes 288 | tf_op jit(solution)/shard_map/all_gather | solution.py:28
  739.8 0.6 iota_compare_fusion
  740.4 1.8 constant_dynamic-slice_fusion.1
  742.3 3.5 all-to-all-start.1
  745.9 5.3 all-to-all-done.1
  751.6 2.7 gather_fusion
  754.3 2.5 reshape.349
  756.8 3.9 multiply_reduce_fusion
  760.7 1.7 fusion.26
  762.5 1.9 multiply_reduce_fusion.1
  764.7 0.7 multiply_convert_fusion.4
  765.4 21.8 %reduce-scatter.2.cloned.1.call-done = bf16[128,512]{1,0:T(8,128)(2,1)} async-done(((bf16[128,2048]{1,0:T(8,128)(2,1)}), bf16[128,512]{1,0:T(8,128)(2,1)}) %reduce-scatter.2.cloned.1.call-update) | async-done | bytes 131088 | tf_op jit(solution)/shard_map/reduce_scatter | solution.py:254
  (159 shorter events, 9.3 us)
Async XLA Ops:
  8.0 691.1 %copy-start = (bf16[128,2,128]{2,1,0:T(2,128)(2,1)S(1)}, bf16[128,2,128]{2,1,0:T(2,128)(2,1)}, u32[]{:S(2)}) copy-start(bf16[128,2,128]{2,1,0:T(2,128)(2,1)} %param.30) | copy-start | bytes 196612
  8.0 52.6 %all-gather.7.cloned.1.call-start = ((), (), s32[]{:S(2)}) async-start(), calls=%async_computation.3 | async-start | bytes 1638400 | tf_op jit(solution)/shard_map/all_gather | solution.py:229
  27.5 378.8 %all-gather.9.cloned.1.call-start = ((), (), s32[]{:S(2)}) async-start(), calls=%async_computation.4 | async-start | bytes 73400320 | tf_op jit(solution)/shard_map/all_gather | solution.py:231
  43.9 541.6 %all-gather.11.cloned.1.call-start = ((), (), s32[]{:S(2)}) async-start(), calls=%async_computation.5 | async-start | bytes 36700160 | tf_op jit(solution)/shard_map/all_gather | solution.py:232
  44.7 695.8 %all-reduce.3.cloned.1.call-start = ((), (), s32[]{:S(2)}) async-start(), calls=%async_computation.8 | async-start | bytes 2621440
  601.4 2.4 copy-start.8
  601.4 2.7 copy-start.1
  601.4 2.9 copy-start.4
  601.4 3.5 copy-start.9
  603.5 2.8 copy-start.3
  603.5 2.9 copy-start.5
  603.5 2.9 copy-start.6
  603.5 142.3 %all-gather.13.cloned.1.call-start = ((), (), s32[]{:S(2)}) async-start(), calls=%async_computation.7 | async-start | bytes 2359296 | tf_op jit(solution)/shard_map/all_gather | solution.py:28
  606.8 6.5 collective-permute-start
  613.5 9.2 %collective-permute-start = (bf16[2,128,2,128]{3,2,1,0:T(2,128)(2,1)S(1)}, bf16[2,128,2,128]{3,2,1,0:T(2,128)(2,1)S(1)}, u32[]{:S(2)}, u32[]{:S(2)}) collective-permute-start(bf16[2,128,2,128]{3,2,1,0:T(2,128)(2,1)S(1)} %get-tuple-element.571), channel_id=1, source_target_pairs={{0,4},{4,8},{8,12},{12,16},{16,20},{20,24},{24,28},{1,5},{5,9},{9,... | collective-permute-start | bytes 393224 | tf_op jit(solution)/shard_map/while/body/eval_jaxpr/ppermute | solution.py:22
  622.8 11.5 %collective-permute-start = (bf16[2,128,2,128]{3,2,1,0:T(2,128)(2,1)S(1)}, bf16[2,128,2,128]{3,2,1,0:T(2,128)(2,1)S(1)}, u32[]{:S(2)}, u32[]{:S(2)}) collective-permute-start(bf16[2,128,2,128]{3,2,1,0:T(2,128)(2,1)S(1)} %get-tuple-element.571), channel_id=1, source_target_pairs={{0,4},{4,8},{8,12},{12,16},{16,20},{20,24},{24,28},{1,5},{5,9},{9,... | collective-permute-start | bytes 393224 | tf_op jit(solution)/shard_map/while/body/eval_jaxpr/ppermute | solution.py:22
  634.5 11.3 %collective-permute-start = (bf16[2,128,2,128]{3,2,1,0:T(2,128)(2,1)S(1)}, bf16[2,128,2,128]{3,2,1,0:T(2,128)(2,1)S(1)}, u32[]{:S(2)}, u32[]{:S(2)}) collective-permute-start(bf16[2,128,2,128]{3,2,1,0:T(2,128)(2,1)S(1)} %get-tuple-element.571), channel_id=1, source_target_pairs={{0,4},{4,8},{8,12},{12,16},{16,20},{20,24},{24,28},{1,5},{5,9},{9,... | collective-permute-start | bytes 393224 | tf_op jit(solution)/shard_map/while/body/eval_jaxpr/ppermute | solution.py:22
  645.9 9.9 %collective-permute-start = (bf16[2,128,2,128]{3,2,1,0:T(2,128)(2,1)S(1)}, bf16[2,128,2,128]{3,2,1,0:T(2,128)(2,1)S(1)}, u32[]{:S(2)}, u32[]{:S(2)}) collective-permute-start(bf16[2,128,2,128]{3,2,1,0:T(2,128)(2,1)S(1)} %get-tuple-element.571), channel_id=1, source_target_pairs={{0,4},{4,8},{8,12},{12,16},{16,20},{20,24},{24,28},{1,5},{5,9},{9,... | collective-permute-start | bytes 393224 | tf_op jit(solution)/shard_map/while/body/eval_jaxpr/ppermute | solution.py:22
  656.0 14.0 %collective-permute-start = (bf16[2,128,2,128]{3,2,1,0:T(2,128)(2,1)S(1)}, bf16[2,128,2,128]{3,2,1,0:T(2,128)(2,1)S(1)}, u32[]{:S(2)}, u32[]{:S(2)}) collective-permute-start(bf16[2,128,2,128]{3,2,1,0:T(2,128)(2,1)S(1)} %get-tuple-element.571), channel_id=1, source_target_pairs={{0,4},{4,8},{8,12},{12,16},{16,20},{20,24},{24,28},{1,5},{5,9},{9,... | collective-permute-start | bytes 393224 | tf_op jit(solution)/shard_map/while/body/eval_jaxpr/ppermute | solution.py:22
  670.2 9.0 %collective-permute-start = (bf16[2,128,2,128]{3,2,1,0:T(2,128)(2,1)S(1)}, bf16[2,128,2,128]{3,2,1,0:T(2,128)(2,1)S(1)}, u32[]{:S(2)}, u32[]{:S(2)}) collective-permute-start(bf16[2,128,2,128]{3,2,1,0:T(2,128)(2,1)S(1)} %get-tuple-element.571), channel_id=1, source_target_pairs={{0,4},{4,8},{8,12},{12,16},{16,20},{20,24},{24,28},{1,5},{5,9},{9,... | collective-permute-start | bytes 393224 | tf_op jit(solution)/shard_map/while/body/eval_jaxpr/ppermute | solution.py:22
  679.5 17.3 %copy-start.7 = (bf16[128,2,128]{2,1,0:T(2,128)(2,1)S(1)}, bf16[128,2,128]{2,1,0:T(2,128)(2,1)}, u32[]{:S(2)}) copy-start(bf16[128,2,128]{2,1,0:T(2,128)(2,1)} %param.26) | copy-start | bytes 196612
  696.2 1.9 copy-start.2
  696.7 3.3 copy-start.11
  696.7 4.2 copy-start.12
  742.3 9.0 %all-to-all-start.1 = ((bf16[20,4,2048]{2,1,0:T(4,128)(2,1)}), bf16[20,4,2048]{2,1,0:T(4,128)(2,1)S(1)}, u32[]{:S(2)}, u32[]{:S(2)}) async-start(bf16[20,4,2048]{2,1,0:T(4,128)(2,1)} %constant_dynamic-slice_fusion.1), calls=%async_computation.1 | async-start | bytes 655360 | tf_op jit(solution)/shard_map/all_to_all | solution.py:246
  745.7 41.5 %reduce-scatter.2.cloned.1.call-start = ((), (), s32[]{:S(2)}) async-start(), calls=%async_computation.6 | async-start | bytes 655360 | tf_op jit(solution)/shard_map/reduce_scatter | solution.py:254
  762.5 2.2 copy-start.10
Sparse Core Ops, SparseCore 0:
  27.6 32.9 all-gather.6
  62.2 344.0 all-gather.8
  407.9 177.6 all-gather.10
  603.6 93.2 all-reduce.2
  760.9 26.3 reduce-scatter.1
Sparse Core Ops, SparseCore 1:
  606.7 89.0 all-gather.12
where the time goes:
time: 795 us; the launch traced here: 794 us
  waiting for transfers between devices  556 us (70%)
  matrix products  62.9 us (8%)
  starting transfers between devices  54.3 us (7%)
  blocking collectives  49.5 us (6%)
  local copies, waits for them, and re-layouts  38.3 us (5%)
  between operations  16.4 us (2%)
  other arithmetic  11.7 us (1%)
    all_gather x1, waiting for transfers between devices, routed(): lax.all_gather(gate_up, 'tp', axis=1, tiled=True)  346 us
    all_gather x1, waiting for transfers between devices, routed(): lax.all_gather(down_proj, 'tp', axis=1, tiled=True)  146 us
    ppermute x7, starting transfers between devices, from_behind(): return lax.ppermute(block, axis, route)  50.4 us
    all_gather x1, blocking collectives, carried_in(): lax.all_gather(a.astype(kind), axis)  37.5 us
    dot_general x1, matrix products, routed(): jnp.einsum('rld,lfsd->srlf', all_rows, wide_gate_up, preferred_element_ty...  33.7 us
    reduce_scatter x1, waiting for transfers between devices, routed(): lax.psum_scatter(partial_value.astype(jnp.bfloat16), 'tp', scatter_dimens...  21.8 us
    ppermute x7, waiting for transfers between devices, from_behind(): return lax.ppermute(block, axis, route)  21 us
    unnamed x32, local copies, waits for them, and re-layouts  20 us
  transfers between devices with their start and end apart: 14, of which 12 were waited for; matrix products, arithmetic and copies ran while one was open for 10% of the time, Pallas kernels for 0%

commit v1 on v0

v1 whole, which is shorter than its diff:
```python
import functools
import math

import jax
import jax.numpy as jnp
from jax import lax
from jax.experimental import pallas as pl
from jax.experimental.pallas import tpu as pltpu
from jax.sharding import PartitionSpec as P

EXPERTS = 8
WINDOW = 4096
HP = 64
NS = 128
STRETCH = 128
CAP = 40
EPSILON = 1e-05
F32 = jnp.float32
BF16 = jnp.bfloat16


def bits_of(count):
    assert count & (count - 1) == 0
    return [1 << b for b in reversed(range(count.bit_length() - 1))]


def swap(block, axis, bit):
    return lax.ppermute(block, axis, [(i, i ^ bit) for i in range(lax.axis_size(axis))])


def spread(block, stages):
    for axis, bit in stages:
        block = jnp.stack([block, swap(block, axis, bit)])
    return block


def stages_of(axis, bits):
    return [(axis, bit) for bit in bits]


def offsets_of(bits):
    offsets = [0]
    for bit in bits:
        offsets = offsets + [o ^ bit for o in offsets]
    return offsets


def attention_kernel(place_ref, query_ref, kv_ref, out_ref, top_ref, sum_ref, acc_ref):
    step = pl.program_id(0)
    steps = pl.num_programs(0)
    rows, width = query_ref.shape
    keys = kv_ref.shape[0]
    shared = kv_ref.shape[1] // (2 * 128)
    group = width // 128 // shared
    mine = place_ref[0]
    other = place_ref[1 + step]

    @pl.when(step == 0)
    def _():
        top_ref[...] = jnp.full_like(top_ref, -jnp.inf)
        sum_ref[...] = jnp.zeros_like(sum_ref)
        acc_ref[...] = jnp.zeros_like(acc_ref)

    gap = (mine - other) * rows

    @pl.when((gap >= 0) & (gap - (keys - 1) < WINDOW))
    def _():
        scale = 1.0 / math.sqrt(128)
        for k in range(shared):
            key = kv_ref[:, k * 128 : (k + 1) * 128]
            value = kv_ref[:, (shared + k) * 128 : (shared + k + 1) * 128]
            query = jnp.concatenate(
                [query_ref[:, (k * group + g) * 128 : (k * group + g + 1) * 128] for g in range(group)],
                axis=0,
            )
            score = (
                lax.dot_general(query, key, (((1,), (1,)), ((), ())), preferred_element_type=F32)
                * scale
            )
            row = lax.rem(lax.broadcasted_iota(jnp.int32, score.shape, 0), rows)
            column = lax.broadcasted_iota(jnp.int32, score.shape, 1)
            behind = gap + row - column
            score = jnp.where((behind >= 0) & (behind < WINDOW), score, -jnp.inf)
            old = top_ref[k]
            new = jnp.maximum(old, jnp.max(score, axis=1, keepdims=True))
            safe = jnp.where(new == -jnp.inf, 0.0, new)
            weight = jnp.exp(score - safe[:, :1])
            shrink = jnp.exp(old - safe)
            top_ref[k] = new
            sum_ref[k] = sum_ref[k] * shrink + jnp.sum(weight, axis=1, keepdims=True)
            acc_ref[k] = acc_ref[k] * shrink[:, :1] + jnp.dot(
                weight.astype(BF16), value, preferred_element_type=F32
            )

    @pl.when(step == steps - 1)
    def _():
        for k in range(shared):
            done = acc_ref[k] / sum_ref[k][:, :1]
            for g in range(group):
                h = k * group + g
                out_ref[:, h * 128 : (h + 1) * 128] = done[g * rows : (g + 1) * rows].astype(BF16)


def attention(query, kv_all, place):
    rows, width = query.shape
    blocks, keys, kv_width = kv_all.shape
    shared = kv_width // 256
    tall = width // 128 // shared * rows
    return pl.pallas_call(
        attention_kernel,
        out_shape=jax.ShapeDtypeStruct((rows, width), BF16),
        grid_spec=pltpu.PrefetchScalarGridSpec(
            num_scalar_prefetch=1,
            grid=(blocks,),
            in_specs=[
                pl.BlockSpec((rows, width), lambda j, place: (0, 0)),
                pl.BlockSpec((None, keys, kv_width), lambda j, place: (j, 0, 0)),
            ],
            out_specs=pl.BlockSpec((rows, width), lambda j, place: (0, 0)),
            scratch_shapes=[
                pltpu.VMEM((shared, tall, 128), F32),
                pltpu.VMEM((shared, tall, 128), F32),
                pltpu.VMEM((shared, tall, 128), F32),
            ],
        ),
        name="attention",
    )(place, query, kv_all)


def expert_kernel(
    offsets,
    where_ref,
    info_ref,
    left_ref,
    right_ref,
    gate_up_ref,
    down_ref,
    keep0_ref,
    keep1_ref,
    send0_ref,
    send1_ref,
    rows_ref,
    hot_ref,
    weight_ref,
):
    expert = pl.program_id(1)
    experts = pl.num_programs(1)
    me = where_ref[0]
    first = where_ref[1]
    far, gx, nz, tokens, half = keep0_ref.shape
    parts = 2 * far
    local = rows_ref.shape[1]
    pairs = rows_ref.shape[0]

    def column(part, h):
        return pl.multiple_of((me ^ offsets[part]) * (2 * half) + h * half, 128)

    def pair_at(p):
        return (2 * p) // nz, (2 * p) % nz

    @pl.when(expert == 0)
    def _():
        for p in range(pairs):
            mx, mz = pair_at(p)
            info = jnp.concatenate([info_ref[mx, mz], info_ref[mx, mz + 1]], axis=1)
            info_id = info[0:2].astype(jnp.int32)
            info_slot = info[2:4].astype(jnp.int32)
            block = lax.broadcasted_iota(jnp.int32, (1, 2 * tokens), 1) // tokens
            row = lax.broadcasted_iota(jnp.int32, (2 * CAP, 2 * tokens), 0)
            for e in range(local):
                match = []
                for k in range(2):
                    live = (info_slot[k : k + 1] >= 0) & (info_id[k : k + 1] == first + e)
                    code = jnp.where(live, block * CAP + info_slot[k : k + 1], -1)
                    match.append(row == code)
                hot_ref[p, e] = (match[0] | match[1]).astype(F32).astype(BF16)
                share = jnp.where(match[0], info[4:5], 0.0) + jnp.where(match[1], info[5:6], 0.0)
                weight_ref[p, e] = jnp.broadcast_to(
                    jnp.sum(share, axis=1, keepdims=True), (2 * CAP, 128)
                )
            hot = hot_ref[p].reshape(local * 2 * CAP, 2 * tokens)
            for part in range(parts):
                core, high = part // far, part % far
                for h in range(2):
                    if h == 0:
                        piece = left_ref[core, high, mx, mz : mz + 2]
                    else:
                        piece = right_ref[core, mx, high, mz : mz + 2]
                    piece = piece.reshape(2 * tokens, half)
                    picked = jnp.dot(hot, piece, preferred_element_type=F32).astype(BF16)
                    rows_ref[p, :, :, pl.ds(column(part, h), half)] = picked.reshape(
                        local, 2 * CAP, half
                    )

    rows = rows_ref[:, expert].reshape(pairs * 2 * CAP, rows_ref.shape[3])
    nt = (((1,), (1,)), ((), ()))
    gate = lax.dot_general(rows, gate_up_ref[0], nt, preferred_element_type=F32)
    up = lax.dot_general(rows, gate_up_ref[1], nt, preferred_element_type=F32)
    hidden = (gate / (1.0 + jnp.exp(-gate)) * up).astype(BF16)
    value = jnp.dot(hidden, down_ref[...], preferred_element_type=F32)
    for p in range(pairs):
        scaled = value[p * 2 * CAP : (p + 1) * 2 * CAP] * weight_ref[p, expert][:, :1]
        rows_ref[p, expert] = scaled.astype(BF16)

    @pl.when(expert == experts - 1)
    def _():
        for p in range(pairs):
            mx, mz = pair_at(p)
            hot = hot_ref[p].reshape(local * 2 * CAP, 2 * tokens)
            for part in range(parts):
                core, high = part // far, part % far
                for h in range(2):
                    value = rows_ref[p, :, :, pl.ds(column(part, h), half)]
                    value = value.reshape(local * 2 * CAP, half)
                    total = lax.dot_general(
                        hot, value, (((0,), (0,)), ((), ())), preferred_element_type=F32
                    )
                    total = total.astype(BF16).reshape(2, tokens, half)
                    if h == 0:
                        target = send0_ref if core else keep0_ref
                        target[high, mx, mz : mz + 2] = total
                    else:
                        target = send1_ref if core else keep1_ref
                        target[mx, high, mz : mz + 2] = total


def experts_apply(offsets, where, info, left, right, gate_up, down):
    nx, nz = info.shape[:2]
    _, far, _, _, tokens, half = left.shape
    local, _, units, width = gate_up.shape
    gx = max(1, 8 // nz)
    pairs = gx * nz // 2
    once = pl.Buffered(1)
    shape0 = jax.ShapeDtypeStruct((far, nx, nz, tokens, half), BF16)
    shape1 = jax.ShapeDtypeStruct((nx, far, nz, tokens, half), BF16)
    spec0 = pl.BlockSpec((far, gx, nz, tokens, half), lambda g, e, w: (0, g, 0, 0, 0))
    spec1 = pl.BlockSpec((gx, far, nz, tokens, half), lambda g, e, w: (g, 0, 0, 0, 0))
    return pl.pallas_call(
        functools.partial(expert_kernel, offsets),
        out_shape=[shape0, shape1, shape0, shape1],
        grid_spec=pltpu.PrefetchScalarGridSpec(
            num_scalar_prefetch=1,
            grid=(nx // gx, local),
            in_specs=[
                pl.BlockSpec((gx, nz, 8, 128), lambda g, e, w: (g, 0, 0, 0)),
                pl.BlockSpec(
                    (2, far, gx, nz, tokens, half),
                    lambda g, e, w: (0, 0, g, 0, 0, 0),
                    pipeline_mode=once,
                ),
                pl.BlockSpec(
                    (2, gx, far, nz, tokens, half),
                    lambda g, e, w: (0, g, 0, 0, 0, 0),
                    pipeline_mode=once,
                ),
                pl.BlockSpec((None, 2, units, width), lambda g, e, w: (e, 0, 0, 0)),
                pl.BlockSpec((None, units, width), lambda g, e, w: (e, 0, 0)),
            ],
            out_specs=[spec0, spec1, spec0, spec1],
            scratch_shapes=[
                pltpu.VMEM((pairs, local, 2 * CAP, width), BF16),
                pltpu.VMEM((pairs, local, 2 * CAP, 2 * tokens), BF16),
                pltpu.VMEM((pairs, local, 2 * CAP, 128), F32),
            ],
        ),
        compiler_params=pltpu.CompilerParams(vmem_limit_bytes=60 * 1024 * 1024),
        name="experts",
    )(where, info, left, right, gate_up, down)


def state_local(state_input, state_inflow, state_readout, step_size, log_decay):
    rows = state_input.shape[0]
    heads = step_size.shape[1]
    groups = state_inflow.shape[1]
    per_group = heads // groups
    inputs = state_input.reshape(rows, groups, per_group, HP)
    step_rows = step_size.reshape(rows, groups, per_group)
    cumulative = jnp.cumsum(log_decay.reshape(rows, groups, per_group), axis=0)
    read_write = jnp.einsum(
        "ign,jgn->ijg", state_readout, state_inflow, preferred_element_type=F32
    )
    causal = (jnp.arange(rows)[:, None] >= jnp.arange(rows)[None, :])[:, :, None, None]
    gap = cumulative[:, None] - cumulative[None]
    decay = jnp.where(causal, jnp.exp(jnp.where(causal, gap, 0.0)), 0.0)
    mixing = (decay * read_write[..., None] * step_rows[None]).astype(BF16)
    intra = jnp.einsum("ijgk,jgkp->igkp", mixing, inputs, preferred_element_type=F32)
    total = cumulative[-1]
    weight = jnp.exp(total[None] - cumulative) * step_rows
    weighted = (weight[..., None] * state_inflow[:, :, None, :]).astype(BF16)
    state = jnp.einsum("jgkn,jgkp->gknp", weighted, inputs, preferred_element_type=F32)
    return cumulative, intra, total, state


def state_entering(state, totals):
    nx = lax.axis_size("exp")
    nz = lax.axis_size("seq")
    place = lax.axis_index("seq") * nx + lax.axis_index("exp")
    count = nx * nz
    offsets = jnp.arange(count, dtype=jnp.int32)
    entering = jnp.zeros_like(state)
    span = 1
    while span < count:
        axis, bit = ("exp", span) if span < nx else ("seq", span // nx)
        if span * 2 < count:
            pairs = [(i, i ^ bit) for i in range(lax.axis_size(axis))]
        else:
            pairs = [(i, i ^ bit) for i in range(lax.axis_size(axis)) if not i & bit]
        other = lax.ppermute(state.astype(BF16), axis, pairs).astype(F32)
        upper = (place & span) != 0
        near = totals[:span]
        before = ((place ^ offsets[:span]) < place)[:, None, None]
        lead = jnp.exp(jnp.sum(jnp.where(before, near, 0.0), axis=0))
        entering = jnp.where(upper, lead[..., None, None] * other + entering, entering)
        own = jnp.exp(jnp.sum(near, axis=0))[..., None, None]
        theirs = jnp.exp(jnp.sum(totals[span : 2 * span], axis=0))[..., None, None]
        state = jnp.where(upper, own * other + state, theirs * state + other)
        span *= 2
    return entering


def state_finish(
    cumulative, intra, entering, state_input, state_gate, state_readout, skip_scale, state_gain
):
    rows, channels = state_input.shape
    groups = state_readout.shape[1]
    per_group = cumulative.shape[2]
    inter = jnp.exp(cumulative)[..., None] * jnp.einsum(
        "ign,gknp->igkp", state_readout.astype(F32), entering, precision=lax.Precision.HIGHEST
    )
    inputs = state_input.reshape(rows, groups, per_group, HP).astype(F32)
    output = intra + inter + skip_scale.reshape(groups, per_group)[:, :, None] * inputs
    gate_rows = state_gate.reshape(rows, groups, per_group, HP).astype(F32)
    gated = output * jax.nn.silu(gate_rows)
    mean_square = jnp.mean(gated * gated, axis=(2, 3), keepdims=True)
    normed = gated * lax.rsqrt(mean_square + EPSILON)
    return (normed.reshape(rows, channels) * state_gain).astype(BF16)


def local(
    query_heads,
    key_heads,
    value_head_rows,
    state_input,
    state_gate,
    state_inflow,
    state_readout,
    step_size,
    log_decay,
    skip_scale,
    state_gain,
    hidden_in,
    mlp_gain,
    router_weight,
    expert_ids,
    slot_index,
    gate_up,
    down_proj,
):
    nz, nx, nt = lax.axis_size("seq"), lax.axis_size("exp"), lax.axis_size("tp")
    z, x, t = lax.axis_index("seq"), lax.axis_index("exp"), lax.axis_index("tp")
    rows, width = hidden_in.shape
    chunk = width // nt
    half = chunk // 2
    tp_bits = bits_of(nt)
    seq_stages = stages_of("seq", bits_of(nz))
    exp_stages = stages_of("exp", bits_of(nx))
    far_stages, core_stages = stages_of("tp", tp_bits[:-1]), stages_of("tp", tp_bits[-1:])

    hidden = hidden_in.astype(F32)
    mean_square = jnp.mean(hidden * hidden, axis=-1, keepdims=True)
    normed = (hidden * lax.rsqrt(mean_square + EPSILON) * mlp_gain).astype(BF16)
    own = lax.dynamic_slice_in_dim(normed, t * chunk, chunk, 1)

    logits = jnp.dot(normed, router_weight, preferred_element_type=F32)
    gate_values = jax.nn.sigmoid(logits)
    one_hot = expert_ids[..., None] == jnp.arange(EXPERTS, dtype=jnp.int32)
    chosen = jnp.sum(jnp.where(one_hot, gate_values[:, None, :], 0.0), axis=-1)
    mixing = chosen / jnp.sum(chosen, axis=1, keepdims=True)

    cumulative, intra, total, state = state_local(
        state_input, state_inflow, state_readout, step_size, log_decay
    )
    heads = step_size.shape[1]
    decay_row = jnp.pad(total.reshape(1, heads), ((0, 1), (0, rows - heads)))
    info = jnp.concatenate(
        [expert_ids.T.astype(F32), slot_index.T.astype(F32), mixing.T, decay_row], axis=0
    )

    piece = spread(own, seq_stages)
    info_all = spread(info, seq_stages + exp_stages)
    left = spread(piece[..., :half], exp_stages + far_stages + core_stages)
    right = spread(piece[..., half:], far_stages + exp_stages + core_stages)
    left = left.reshape(2, nt // 2, nx, nz, rows, half)
    right = right.reshape(2, nx, nt // 2, nz, rows, half)
    info_all = info_all.reshape(nx, nz, 8, rows)

    where = jnp.stack([t, x * gate_up.shape[0]]).astype(jnp.int32)
    keep0, keep1, send0, send1 = experts_apply(
        offsets_of(tp_bits), where, info_all, left, right, jnp.swapaxes(gate_up, 1, 2), down_proj
    )

    flat = lambda a: a.reshape(rows, a.shape[1] * a.shape[2])
    kv = jnp.concatenate([flat(key_heads), flat(value_head_rows)], axis=1)
    kv_all = spread(kv, seq_stages + exp_stages).reshape(nx * nz, rows, kv.shape[1])
    off_x, off_z = offsets_of(bits_of(nx)), offsets_of(bits_of(nz))
    offset_x = jnp.array(off_x, jnp.int32)[:, None]
    offset_z = jnp.array(off_z, jnp.int32)[None, :]
    places = ((z ^ offset_z) * nx + (x ^ offset_x)).reshape(-1)
    place = jnp.concatenate([(z * nx + x)[None], places]).astype(jnp.int32)
    window_out = attention(flat(query_heads), kv_all, place).reshape(query_heads.shape)

    groups = state_inflow.shape[1]
    totals = jnp.stack(
        [info_all[off_x.index(i), off_z.index(k), 6, :heads] for k in range(nz) for i in range(nx)]
    ).reshape(nz * nx, groups, heads // groups)
    entering = state_entering(state, totals)
    state_out = state_finish(
        cumulative, intra, entering, state_input, state_gate, state_readout, skip_scale, state_gain
    )

    def settle(kept, stages):
        for axis, bit in stages:
            count = kept.shape[0] // 2
            kept = kept[:count] + swap(kept[count:].astype(BF16), axis, bit).astype(F32)
        return kept

    def join(kept, sent):
        kept = kept.astype(F32) + swap(sent, *core_stages[0]).astype(F32)
        return kept.reshape(-1, rows, half)

    kept0 = settle(join(keep0, send0), far_stages[::-1] + exp_stages[::-1])
    kept1 = settle(join(keep1, send1), exp_stages[::-1] + far_stages[::-1])
    kept = settle(jnp.concatenate([kept0, kept1], axis=-1), seq_stages[::-1])
    routed_out = kept.reshape(rows, chunk).astype(BF16)
    return window_out, state_out, routed_out


def solution(mesh):
    block = ("seq", "exp")
    return jax.shard_map(
        local,
        mesh=mesh,
        in_specs=(
            P(block, "tp", None),
            P(block, "tp", None),
            P(block, "tp", None),
            P(block, "tp"),
            P(block, "tp"),
            P(block, "tp", None),
            P(block, "tp", None),
            P(block, "tp"),
            P(block, "tp"),
            P("tp"),
            P("tp"),
            P(block, None),
            P(),
            P(),
            P(block, None),
            P(block, None),
            P("exp", ("seq", "tp"), None, None),
            P("exp", ("seq", "tp"), None),
        ),
        out_specs=(P(block, "tp", None), P(block, "tp"), P(block, "tp")),
        check_vma=False,
    )
```

time: 795 us -> 169 us (0.21)
  waiting for transfers between devices: 556 us -> 45.7 us
  matrix products: 62.9 us -> 6.48 us
  blocking collectives: 49.5 us -> 0 us
  Pallas kernels: 0 us -> 27.3 us
  starting transfers between devices: 54.3 us -> 35.8 us
  other arithmetic: 11.7 us -> 26.8 us
  between operations: 16.4 us -> 1.3 us
  local copies, waits for them, and re-layouts: 38.3 us -> 23.4 us
    all_gather x4 -> x0, waiting for transfers between devices: 507 us -> none  [the longest x1 346 us: routed(): lax.all_gather(gate_up, 'tp', axis=1, tiled=True)]
    dot_general x24 -> x5, matrix products: 62.9 us -> 6.48 us  [the longest x1 2.32 us: state_local(): jnp.einsum('ijgk,jgkp->igkp', mixing, inputs, preferred_element_type=F32)]
    all_gather x1 -> x0, blocking collectives: 37.5 us -> none  [carried_in(): lax.all_gather(a.astype(kind), axis)]
    pallas_call x0 -> x2, Pallas kernels: none -> 27.3 us  [the longest x1 20.8 us: experts_apply(): pl.pallas_call(functools.partial(expert_kernel, offsets), out_shape=[shap...]
    ppermute x7 -> x25, waiting for transfers between devices: 21 us -> 45.7 us  [the longest x22 42 us: swap(): lax.ppermute(block, axis, [(i, i ^ bit) for i in range(lax.axis_size(axis...]
    reduce_scatter x1 -> x0, waiting for transfers between devices: 21.8 us -> none  [routed(): lax.psum_scatter(partial_value.astype(jnp.bfloat16), 'tp', scatter_dimens...]
    another operation x2 -> x18, other arithmetic: 0.32 us -> 15 us  [the longest x15 14.2 us: spread(): block = jnp.stack([block, swap(block, axis, bit)])]
    ppermute x7 -> x25, starting transfers between devices: 50.4 us -> 35.8 us  [the longest x22 25.8 us: swap(): lax.ppermute(block, axis, [(i, i ^ bit) for i in range(lax.axis_size(axis...]
  transfers between devices with their start and end apart: 14 -> 25, of which waited for: 12 -> 13; matrix products, arithmetic and copies ran while one was open for 10% -> 32% of each run, Pallas kernels for 0% -> 16%
where the time goes in v1:
time: 169 us; the launch traced here: 167 us
  waiting for transfers between devices  45.7 us (27%)
  starting transfers between devices  35.8 us (21%)
  Pallas kernels  27.3 us (16%)
  other arithmetic  26.8 us (16%)
  local copies, waits for them, and re-layouts  23.4 us (14%)
  matrix products  6.48 us (4%)
    ppermute x22, waiting for transfers between devices, swap(): lax.ppermute(block, axis, [(i, i ^ bit) for i in range(lax.axis_size(axis...  42 us
    ppermute x22, starting transfers between devices, swap(): lax.ppermute(block, axis, [(i, i ^ bit) for i in range(lax.axis_size(axis...  25.8 us
    pallas_call x1, Pallas kernels, experts_apply(): pl.pallas_call(functools.partial(expert_kernel, offsets), out_shape=[shap...  20.8 us
    unnamed x60, local copies, waits for them, and re-layouts  19.9 us
    another operation x15, other arithmetic, spread(): block = jnp.stack([block, swap(block, axis, bit)])  14.2 us
    ppermute x3, starting transfers between devices, state_entering(): other = lax.ppermute(state.astype(BF16), axis, pairs).astype(F32)  9.96 us
    pallas_call x1, Pallas kernels, attention(): pl.pallas_call(attention_kernel, out_shape=jax.ShapeDtypeStruct((rows, wi...  6.49 us
    ppermute x3, waiting for transfers between devices, state_entering(): other = lax.ppermute(state.astype(BF16), axis, pairs).astype(F32)  3.65 us
  transfers between devices with their start and end apart: 25, of which 13 were waited for; matrix products, arithmetic and copies ran while one was open for 32% of the time, Pallas kernels for 16%

profile of v1, /device:TPU:0, one launch (start us, length us, event | category | flops | bytes accessed | tf_op | source)
XLA Modules:
  0.0 166.7 jit_solution(12472646496240449039)
XLA Ops:
  0.7 1.3 fusion.7
  2.0 1.2 fusion.9
  3.3 4.1 %collective-permute-start.9 = (bf16[128,512]{1,0:T(8,128)(2,1)S(1)}, bf16[128,512]{1,0:T(8,128)(2,1)S(1)}, u32[]{:S(2)}, u32[]{:S(2)}) collective-permute-start(bf16[128,512]{1,0:T(8,128)(2,1)S(1)} %constant_dynamic-slice_fusion), channel_id=1, source_target_pairs={{0,16},{8,24},{16,0},{24,8},{1,17},{9,25},{17,1},{25,9},{2,18},{10... | collective-permute-start | bytes 393224 | tf_op jit(solution)/shard_map/ppermute | solution.py:28
  7.4 1.0 fusion.6
  9.2 0.7 fusion.57
  10.2 1.3 fusion.59
  11.4 1.8 %collective-permute-start.6 = (bf16[2,8,128,64]{2,3,1,0:T(8,128)(2,1)}, bf16[2,8,128,64]{2,3,1,0:T(8,128)(2,1)}, u32[]{:S(2)}, u32[]{:S(2)}) collective-permute-start(bf16[2,8,128,64]{2,3,1,0:T(8,128)(2,1)} %get-tuple-element.42), channel_id=1, source_target_pairs={{0,4},{4,0},{1,5},{5,1},{2,6},{6,2},{3,7},{7,3},{8,12},{12,8},{9,1... | collective-permute-start | bytes 786440 | tf_op jit(solution)/shard_map/ppermute | solution.py:308
  13.2 0.6 bitcast_dynamic-update-slice_fusion.1
  14.0 1.6 collective-permute-start.10
  15.6 0.6 bitcast_dynamic-update-slice_fusion
  16.2 2.6 %collective-permute-start = (bf16[128,512]{1,0:T(8,128)(2,1)}, bf16[128,512]{1,0:T(8,128)(2,1)}, u32[]{:S(2)}, u32[]{:S(2)}) collective-permute-start(bf16[128,512]{1,0:T(8,128)(2,1)} %bitcast_dynamic-update-slice_fusion), channel_id=1, source_target_pairs={{0,16},{8,24},{16,0},{24,8},{1,17},{9,25},{17,1},{25,9},{2,18},{10... | collective-permute-start | bytes 393224 | tf_op jit(solution)/shard_map/ppermute | solution.py:28
  19.0 5.1 %collective-permute-done.10 = bf16[2,128,512]{2,1,0:T(8,128)(2,1)S(1)} collective-permute-done((bf16[2,128,512]{2,1,0:T(8,128)(2,1)S(1)}, bf16[2,128,512]{2,1,0:T(8,128)(2,1)S(1)}, u32[]{:S(2)}, u32[]{:S(2)}) %collective-permute-start.10) | collective-permute-done | bytes 262176 | tf_op jit(solution)/shard_map/ppermute | solution.py:28
  24.2 1.5 collective-permute-start.14
  25.7 1.4 collective-permute-start.11
  27.1 3.5 %collective-permute-done.14 = bf16[2,2,128,256]{3,2,1,0:T(8,128)(2,1)S(1)} collective-permute-done((bf16[2,2,128,256]{3,2,1,0:T(8,128)(2,1)S(1)}, bf16[2,2,128,256]{3,2,1,0:T(8,128)(2,1)S(1)}, u32[]{:S(2)}, u32[]{:S(2)}) %collective-permute-start.14) | collective-permute-done | bytes 262176 | tf_op jit(solution)/shard_map/ppermute | solution.py:28
  30.6 0.9 fusion.54
  31.5 1.9 %collective-permute-start.15 = (bf16[2,2,2,128,256]{4,3,2,1,0:T(8,128)(2,1)}, bf16[2,2,2,128,256]{4,3,2,1,0:T(8,128)(2,1)S(1)}, u32[]{:S(2)}, u32[]{:S(2)}) collective-permute-start(bf16[2,2,2,128,256]{4,3,2,1,0:T(8,128)(2,1)} %get-tuple-element.19), channel_id=1, source_target_pairs={{0,4},{4,0},{1,5},{5,1},{2,6},{6,2},{3,7},{7,3},{8,12},{12,8},{9,1... | collective-permute-start | bytes 1572872 | tf_op jit(solution)/shard_map/ppermute | solution.py:28
  33.4 1.4 collective-permute-done.11
  34.8 0.9 fusion.55
  36.4 2.3 %convolution_bitcast_fusion.1 = f32[128,2,8,64]{0,3,2,1:T(8,128)} fusion(bf16[128,2,8,64]{0,3,2,1:T(8,128)(2,1)} %bitcast.133, f32[128,2,8]{0,2,1:T(8,128)S(1)} %bitcast.157, f32[128,128,2]{1,0,2:T(8,128)S(1)} %copy.57, f32[128,2,8]{0,2,1:T(8,128)S(1)} %copy.53, pred[128,128]{1,0:T(8,128)(4,1)S(1)} %iota_compare_fusion), kind=kOutput, calls=%fused_computation.8 | convolution fusion | flops 35127296 | bytes 950272 | tf_op jit(solution)/shard_map/ijgk,jgkp->igkp/dot_general | solution.py:286
  38.7 4.0 %collective-permute-done.15 = bf16[2,2,2,128,256]{4,3,2,1,0:T(8,128)(2,1)S(1)} collective-permute-done((bf16[2,2,2,128,256]{4,3,2,1,0:T(8,128)(2,1)}, bf16[2,2,2,128,256]{4,3,2,1,0:T(8,128)(2,1)S(1)}, u32[]{:S(2)}, u32[]{:S(2)}) %collective-permute-start.15) | collective-permute-done | bytes 524320 | tf_op jit(solution)/shard_map/ppermute | solution.py:28
  42.7 1.1 pad_maximum_fusion.4
  43.8 1.3 collective-permute-done.12
  45.2 1.0 pad_maximum_fusion.3
  46.3 0.6 pad_add_fusion.1.where_ref
  47.0 2.9 %collective-permute-done.4 = f32[2,8,128]{2,1,0:T(8,128)S(1)} collective-permute-done((f32[2,8,128]{2,1,0:T(8,128)S(1)}, f32[2,8,128]{2,1,0:T(8,128)S(1)}, u32[]{:S(2)}, u32[]{:S(2)}) %collective-permute-start.4) | collective-permute-done | bytes 8224 | tf_op jit(solution)/shard_map/ppermute | solution.py:28
  50.0 1.4 collective-permute-start.5
  51.4 0.6 pad_add_fusion.place_ref
  52.1 16.5 %copy.86 = bf16[4,448,2,2048]{3,1,2,0:T(8,128)(2,1)} copy(bf16[4,448,2,2048]{3,2,1,0:T(2,128)(2,1)} %param.36) | data formatting | bytes 29360128 | tf_op args[16]
  68.7 0.9 copy.64
  69.7 0.8 copy.87
  70.5 0.6 pad_maximum_fusion.12.info_ref
  71.1 2.8 %pad_maximum_fusion.1.right_ref = bf16[2,2,2,4,128,256]{5,4,3,2,1,0:T(8,128)(2,1)} fusion(bf16[1,2,2,4,128,256]{5,4,3,2,1,0:T(8,128)(2,1)} %bitcast.53, bf16[1,1,2,4,128,256]{5,4,3,2,1,0:T(8,128)(2,1)S(1)} %bitcast.124, bf16[1,1,1,4,128,256]{5,4,3,2,1,0:T(8,128)(2,1)S(1)} %bitcast.131, bf16[1,1,1,4,128,256]{5,4,3,2,1,0:T(8,128)(2,1)S(1)} %bitcast.121), kind=kLoop, calls=%fused_computation.2 | loop fusion | flops 3145728 | bytes 4194304 | tf_op jit(solution)/shard_map/stack | solution.py:33
  73.9 2.8 %pad_maximum_fusion.left_ref = bf16[2,2,2,4,128,256]{5,4,3,2,1,0:T(8,128)(2,1)} fusion(bf16[1,2,2,4,128,256]{5,4,3,2,1,0:T(8,128)(2,1)} %bitcast.45, bf16[1,1,2,4,128,256]{5,4,3,2,1,0:T(8,128)(2,1)S(1)} %bitcast.126, bf16[1,1,1,4,128,256]{5,4,3,2,1,0:T(8,128)(2,1)S(1)} %bitcast.129, bf16[1,1,1,4,128,256]{5,4,3,2,1,0:T(8,128)(2,1)S(1)} %bitcast.119), kind=kLoop, calls=%fused_computation.1 | loop fusion | flops 3145728 | bytes 4194304 | tf_op jit(solution)/shard_map/stack | solution.py:33
  76.7 20.8 %experts.1 = (bf16[2,2,4,128,256]{4,3,2,1,0:T(8,128)(2,1)}, bf16[2,2,4,128,256]{4,3,2,1,0:T(8,128)(2,1)}, bf16[2,2,4,128,256]{4,3,2,1,0:T(8,128)(2,1)}, bf16[2,2,4,128,256]{4,3,2,1,0:T(8,128)(2,1)}) custom-call(s32[2]{0:T(128)} %pad_add_fusion.1.where_ref, f32[2,4,8,128]{3,2,1,0:T(8,128)} %pad_maximum_fusion.12.info_ref, ...), custom_call_target="tpu_custom_call" | custom-call | tf_op jit(solution)/shard_map/experts/pallas_call | solution.py:238
  97.7 1.0 fusion.53
  98.8 0.6 collective-permute-start.17
  99.4 1.1 fusion.39
  100.5 1.7 %collective-permute-start.7 = (bf16[2,8,128,64]{2,3,1,0:T(8,128)(2,1)S(1)}, bf16[2,8,128,64]{2,3,1,0:T(8,128)(2,1)S(1)}, u32[]{:S(2)}, u32[]{:S(2)}) collective-permute-start(bf16[2,8,128,64]{2,3,1,0:T(8,128)(2,1)S(1)} %fusion.39), channel_id=1, source_target_pairs={{0,8},{8,0},{16,24},{24,16},{1,9},{9,1},{17,25},{25,17},{2,10},{10... | collective-permute-start | bytes 786440 | tf_op jit(solution)/shard_map/ppermute | solution.py:308
  102.9 5.1 %collective-permute-done.1 = bf16[2,128,512]{2,1,0:T(8,128)(2,1)S(1)} collective-permute-done((bf16[2,128,512]{2,1,0:T(8,128)(2,1)S(1)}, bf16[2,128,512]{2,1,0:T(8,128)(2,1)S(1)}, u32[]{:S(2)}, u32[]{:S(2)}) %collective-permute-start.1) | collective-permute-done | bytes 262176 | tf_op jit(solution)/shard_map/ppermute | solution.py:28
  108.0 0.9 fusion.56
  108.8 0.6 collective-permute-start.2
  109.5 3.6 %collective-permute-done.7 = bf16[2,8,128,64]{2,3,1,0:T(8,128)(2,1)S(1)} collective-permute-done((bf16[2,8,128,64]{2,3,1,0:T(8,128)(2,1)S(1)}, bf16[2,8,128,64]{2,3,1,0:T(8,128)(2,1)S(1)}, u32[]{:S(2)}, u32[]{:S(2)}) %collective-permute-start.7) | collective-permute-done | bytes 262176 | tf_op jit(solution)/shard_map/ppermute | solution.py:308
  113.1 1.3 fusion.15
  114.5 6.4 %collective-permute-start.8 = (bf16[2,8,128,64]{2,3,1,0:T(8,128)(2,1)S(1)}, bf16[2,8,128,64]{2,3,1,0:T(8,128)(2,1)S(1)}, u32[]{:S(2)}, u32[]{:S(2)}) collective-permute-start(bf16[2,8,128,64]{2,3,1,0:T(8,128)(2,1)S(1)} %fusion.15), channel_id=1, source_target_pairs={{0,16},{8,24},{1,17},{9,25},{2,18},{10,26},{3,19},{11,27},{4,20},{... | collective-permute-start | bytes 786440 | tf_op jit(solution)/shard_map/ppermute | solution.py:308
  120.9 1.6 convert_add_fusion
  122.6 1.1 collective-permute-start.21
  123.7 1.6 convert_add_fusion.1
  125.4 1.6 collective-permute-start.18
  127.0 1.7 %multiply_reduce_fusion = (f32[128,2]{0,1:T(2,128)S(1)}, f32[128,2,8,64]{0,3,2,1:T(8,128)S(1)}) fusion(f32[128,2,8,64]{0,3,2,1:T(8,128)S(1)} %bitcast.137, bf16[128,2,8,64]{0,3,2,1:T(8,128)(2,1)S(1)} %bitcast.134, f32[2,8]{1,0:T(2,128)S(1)} %mul.203, f32[128,2,8,64]{0,3,2,1:T(8,128)S(1)} %copy-done.26, bf16[128,2,128,1]{2,1,0,3:T(2,128)(2,1)S(1)} %bitcast.115, ...), kind=kOutput, calls=%fused_computation.61 | convolution fusion | flops 204340992 | bytes 2696451 | tf_op jit(solution)/shard_map/ign,gknp->igkp/dot_general | solution.py:327
  128.8 7.4 %collective-permute-done.21 = bf16[8,128,256]{2,1,0:T(8,128)(2,1)S(1)} collective-permute-done((bf16[8,128,256]{2,1,0:T(8,128)(2,1)S(1)}, bf16[8,128,256]{2,1,0:T(8,128)(2,1)S(1)}, u32[]{:S(2)}, u32[]{:S(2)}) %collective-permute-start.21) | collective-permute-done | bytes 524320 | tf_op jit(solution)/shard_map/ppermute | solution.py:28
  136.4 1.6 collective-permute-start.22
  138.0 1.6 collective-permute-done.18
  139.7 0.9 collective-permute-start.19
  140.6 3.7 %collective-permute-done.22 = bf16[4,128,256]{2,1,0:T(8,128)(2,1)S(1)} collective-permute-done((bf16[4,128,256]{2,1,0:T(8,128)(2,1)S(1)}, bf16[4,128,256]{2,1,0:T(8,128)(2,1)S(1)}, u32[]{:S(2)}, u32[]{:S(2)}) %collective-permute-start.22) | collective-permute-done | bytes 262176 | tf_op jit(solution)/shard_map/ppermute | solution.py:28
  144.4 1.7 %collective-permute-done.19 = bf16[4,128,256]{2,1,0:T(8,128)(2,1)S(1)} collective-permute-done((bf16[4,128,256]{2,1,0:T(8,128)(2,1)S(1)}, bf16[4,128,256]{2,1,0:T(8,128)(2,1)S(1)}, u32[]{:S(2)}, u32[]{:S(2)}) %collective-permute-start.19) | collective-permute-done | bytes 262176 | tf_op jit(solution)/shard_map/ppermute | solution.py:28
  146.3 1.4 collective-permute-start.23
  147.9 0.7 multiply_convert_fusion.4
  148.7 4.0 %collective-permute-done.23 = bf16[2,128,512]{2,1,0:T(8,128)(2,1)S(1)} collective-permute-done((bf16[2,128,512]{2,1,0:T(8,128)(2,1)S(1)}, bf16[2,128,512]{2,1,0:T(8,128)(2,1)S(1)}, u32[]{:S(2)}, u32[]{:S(2)}) %collective-permute-start.23) | collective-permute-done | bytes 262176 | tf_op jit(solution)/shard_map/ppermute | solution.py:28
  152.8 2.9 %collective-permute-start.24 = (bf16[1,128,512]{2,1,0:T(8,128)(2,1)S(1)}, bf16[1,128,512]{2,1,0:T(8,128)(2,1)S(1)}, u32[]{:S(2)}, u32[]{:S(2)}) collective-permute-start(bf16[1,128,512]{2,1,0:T(8,128)(2,1)S(1)} %slice.192), channel_id=1, source_target_pairs={{0,16},{8,24},{16,0},{24,8},{1,17},{9,25},{17,1},{25,9},{2,18},{10... | collective-permute-start | bytes 393224 | tf_op jit(solution)/shard_map/ppermute | solution.py:28
  155.7 2.1 %pad_maximum_fusion.2 = bf16[2,2,2,128,512]{4,3,2,1,0:T(8,128)(2,1)} fusion(bf16[1,2,2,128,512]{4,3,2,1,0:T(8,128)(2,1)} %bitcast.6, bf16[1,2,2,128,512]{4,3,2,1,0:T(8,128)(2,1)S(1)} %get-tuple-element.24), kind=kLoop, calls=%fused_computation.23 | loop fusion | flops 524288 | bytes 2097152 | tf_op jit(solution)/shard_map/stack | solution.py:33
  157.8 6.5 %attention.1 = bf16[128,1024]{1,0:T(8,128)(2,1)} custom-call(s32[9]{0:T(128)} %pad_add_fusion.place_ref, bf16[128,1024]{1,0:T(8,128)(2,1)} %bitcast.135, bf16[8,128,512]{2,1,0:T(8,128)(2,1)} %bitcast.117), custom_call_target="tpu_custom_call" | custom-call | tf_op jit(solution)/shard_map/attention/pallas_call | solution.py:109
  164.3 1.7 %copy.73 = bf16[16,8,8,128]{3,2,1,0:T(8,128)(2,1)} copy(bf16[16,8,8,128]{3,1,2,0:T(8,128)(2,1)} %bitcast.136) | data formatting | bytes 524288
  166.0 0.7 fusion.40
  (138 shorter events, 4.1 us)
Async XLA Ops:
  0.6 18.2 %copy-start = (bf16[128,2,128]{2,1,0:T(2,128)(2,1)S(1)}, bf16[128,2,128]{2,1,0:T(2,128)(2,1)}, u32[]{:S(2)}) copy-start(bf16[128,2,128]{2,1,0:T(2,128)(2,1)} %param.26) | copy-start | bytes 196612
  0.6 7.8 %copy-start.19 = (f32[128,16]{0,1:T(8,128)S(1)}, f32[128,16]{0,1:T(8,128)}, u32[]{:S(2)}) copy-start(f32[128,16]{0,1:T(8,128)} %param.28) | copy-start | bytes 24580
  0.7 8.2 %copy-start.22 = (s32[128,2]{0,1:T(2,128)S(1)}, s32[128,2]{0,1:T(2,128)}, u32[]{:S(2)}) copy-start(s32[128,2]{0,1:T(2,128)} %param.34) | copy-start | bytes 3076
  0.7 8.2 %copy-start.23 = (s32[128,2]{0,1:T(2,128)S(1)}, s32[128,2]{0,1:T(2,128)}, u32[]{:S(2)}) copy-start(s32[128,2]{0,1:T(2,128)} %param.35) | copy-start | bytes 3076
  0.7 8.3 %copy-start.20 = (f32[128,16]{0,1:T(8,128)S(1)}, f32[128,16]{0,1:T(8,128)}, u32[]{:S(2)}) copy-start(f32[128,16]{0,1:T(8,128)} %param.27) | copy-start | bytes 24580
  0.7 9.2 %copy-start.14 = (bf16[128,1024]{1,0:T(8,128)(2,1)S(1)}, bf16[128,1024]{1,0:T(8,128)(2,1)}, u32[]{:S(2)}) copy-start(bf16[128,1024]{1,0:T(8,128)(2,1)} %param.23) | copy-start | bytes 786436
  0.7 9.4 %copy-start.16 = (bf16[128,2,128]{2,1,0:T(2,128)(2,1)S(1)}, bf16[128,2,128]{2,1,0:T(2,128)(2,1)}, u32[]{:S(2)}) copy-start(bf16[128,2,128]{2,1,0:T(2,128)(2,1)} %param.25) | copy-start | bytes 196612
  3.3 10.0 %copy-start.17 = (bf16[128,2,128]{2,1,0:T(2,128)(2,1)S(1)}, bf16[128,2,128]{2,1,0:T(2,128)(2,1)}, u32[]{:S(2)}) copy-start(bf16[128,2,128]{2,1,0:T(2,128)(2,1)} %param.21) | copy-start | bytes 196612
  3.3 10.6 %collective-permute-start.9 = (bf16[128,512]{1,0:T(8,128)(2,1)S(1)}, bf16[128,512]{1,0:T(8,128)(2,1)S(1)}, u32[]{:S(2)}, u32[]{:S(2)}) collective-permute-start(bf16[128,512]{1,0:T(8,128)(2,1)S(1)} %constant_dynamic-slice_fusion), channel_id=1, source_target_pairs={{0,16},{8,24},{16,0},{24,8},{1,17},{9,25},{17,1},{25,9},{2,18},{10... | collective-permute-start | bytes 393224 | tf_op jit(solution)/shard_map/ppermute | solution.py:28
  8.6 7.0 %copy-start.18 = (bf16[128,2,128]{2,1,0:T(2,128)(2,1)S(1)}, bf16[128,2,128]{2,1,0:T(2,128)(2,1)}, u32[]{:S(2)}) copy-start(bf16[128,2,128]{2,1,0:T(2,128)(2,1)} %param.22) | copy-start | bytes 196612
  8.9 37.3 %collective-permute-start.3 = (f32[8,128]{1,0:T(8,128)S(1)}, f32[8,128]{1,0:T(8,128)S(1)}, u32[]{:S(2)}, u32[]{:S(2)}) collective-permute-start(f32[8,128]{1,0:T(8,128)S(1)} %get-tuple-element.41), channel_id=1, source_target_pairs={{0,16},{8,24},{16,0},{24,8},{1,17},{9,25},{17,1},{25,9},{2,18},{10... | collective-permute-start | bytes 12296 | tf_op jit(solution)/shard_map/ppermute | solution.py:28
  10.1 3.8 %copy-start.7 = (bf16[128,1024]{0,1:T(8,128)(2,1)}, bf16[128,1024]{0,1:T(8,128)(2,1)S(1)}, u32[]{:S(2)}) copy-start(bf16[128,1024]{0,1:T(8,128)(2,1)S(1)} %copy.58) | copy-start | bytes 786436
  10.1 16.9 %copy-start.25 = (s32[4]{0:T(128)S(1)}, s32[4]{0:T(128)}, u32[]{:S(2)}) copy-start(s32[4]{0:T(128)} %constant.49.clone) | copy-start | bytes 52
  11.4 87.9 %collective-permute-start.6 = (bf16[2,8,128,64]{2,3,1,0:T(8,128)(2,1)}, bf16[2,8,128,64]{2,3,1,0:T(8,128)(2,1)}, u32[]{:S(2)}, u32[]{:S(2)}) collective-permute-start(bf16[2,8,128,64]{2,3,1,0:T(8,128)(2,1)} %get-tuple-element.42), channel_id=1, source_target_pairs={{0,4},{4,0},{1,5},{5,1},{2,6},{6,2},{3,7},{7,3},{8,12},{12,8},{9,1... | collective-permute-start | bytes 786440 | tf_op jit(solution)/shard_map/ppermute | solution.py:308
  14.0 10.2 %collective-permute-start.10 = (bf16[2,128,512]{2,1,0:T(8,128)(2,1)S(1)}, bf16[2,128,512]{2,1,0:T(8,128)(2,1)S(1)}, u32[]{:S(2)}, u32[]{:S(2)}) collective-permute-start(bf16[2,128,512]{2,1,0:T(8,128)(2,1)S(1)} %get-tuple-element.26), channel_id=1, source_target_pairs={{0,8},{8,0},{16,24},{24,16},{1,9},{9,1},{17,25},{25,17},{2,10},{10... | collective-permute-start | bytes 786440 | tf_op jit(solution)/shard_map/ppermute | solution.py:28
  16.2 81.4 %collective-permute-start = (bf16[128,512]{1,0:T(8,128)(2,1)}, bf16[128,512]{1,0:T(8,128)(2,1)}, u32[]{:S(2)}, u32[]{:S(2)}) collective-permute-start(bf16[128,512]{1,0:T(8,128)(2,1)} %bitcast_dynamic-update-slice_fusion), channel_id=1, source_target_pairs={{0,16},{8,24},{16,0},{24,8},{1,17},{9,25},{17,1},{25,9},{2,18},{10... | collective-permute-start | bytes 393224 | tf_op jit(solution)/shard_map/ppermute | solution.py:28
  24.2 6.4 %collective-permute-start.14 = (bf16[2,2,128,256]{3,2,1,0:T(8,128)(2,1)S(1)}, bf16[2,2,128,256]{3,2,1,0:T(8,128)(2,1)S(1)}, u32[]{:S(2)}, u32[]{:S(2)}) collective-permute-start(bf16[2,2,128,256]{3,2,1,0:T(8,128)(2,1)S(1)} %get-tuple-element.20), channel_id=1, source_target_pairs={{0,2},{1,3},{2,0},{3,1},{4,6},{5,7},{6,4},{7,5},{8,10},{9,11},{10,... | collective-permute-start | bytes 786440 | tf_op jit(solution)/shard_map/ppermute | solution.py:28
  25.7 9.2 %collective-permute-start.11 = (bf16[2,2,128,256]{3,2,1,0:T(8,128)(2,1)S(1)}, bf16[2,2,128,256]{3,2,1,0:T(8,128)(2,1)S(1)}, u32[]{:S(2)}, u32[]{:S(2)}) collective-permute-start(bf16[2,2,128,256]{3,2,1,0:T(8,128)(2,1)S(1)} %get-tuple-element.21), channel_id=1, source_target_pairs={{0,4},{4,0},{1,5},{5,1},{2,6},{6,2},{3,7},{7,3},{8,12},{12,8},{9,1... | collective-permute-start | bytes 786440 | tf_op jit(solution)/shard_map/ppermute | solution.py:28
  30.6 5.2 %copy-start.5 = (bf16[2,2,128,256]{3,2,1,0:T(8,128)(2,1)}, bf16[2,2,128,256]{3,2,1,0:T(8,128)(2,1)S(1)}, u32[]{:S(2)}) copy-start(bf16[2,2,128,256]{3,2,1,0:T(8,128)(2,1)S(1)} %collective-permute-done.14) | copy-start | bytes 786436
  31.5 11.2 %collective-permute-start.15 = (bf16[2,2,2,128,256]{4,3,2,1,0:T(8,128)(2,1)}, bf16[2,2,2,128,256]{4,3,2,1,0:T(8,128)(2,1)S(1)}, u32[]{:S(2)}, u32[]{:S(2)}) collective-permute-start(bf16[2,2,2,128,256]{4,3,2,1,0:T(8,128)(2,1)} %get-tuple-element.19), channel_id=1, source_target_pairs={{0,4},{4,0},{1,5},{5,1},{2,6},{6,2},{3,7},{7,3},{8,12},{12,8},{9,1... | collective-permute-start | bytes 1572872 | tf_op jit(solution)/shard_map/ppermute | solution.py:28
  34.8 0.9 copy-start.3
  35.8 9.4 %collective-permute-start.12 = (bf16[2,2,2,128,256]{4,3,2,1,0:T(8,128)(2,1)}, bf16[2,2,2,128,256]{4,3,2,1,0:T(8,128)(2,1)S(1)}, u32[]{:S(2)}, u32[]{:S(2)}) collective-permute-start(bf16[2,2,2,128,256]{4,3,2,1,0:T(8,128)(2,1)} %get-tuple-element.23), channel_id=1, source_target_pairs={{0,2},{1,3},{2,0},{3,1},{4,6},{5,7},{6,4},{7,5},{8,10},{9,11},{10,... | collective-permute-start | bytes 1572872 | tf_op jit(solution)/shard_map/ppermute | solution.py:28
  43.8 27.3 %collective-permute-start.16 = (bf16[2,2,2,2,128,256]{5,4,3,2,1,0:T(8,128)(2,1)}, bf16[2,2,2,2,128,256]{5,4,3,2,1,0:T(8,128)(2,1)}, u32[]{:S(2)}, u32[]{:S(2)}) collective-permute-start(bf16[2,2,2,2,128,256]{5,4,3,2,1,0:T(8,128)(2,1)} %pad_maximum_fusion.4), channel_id=1, source_target_pairs={{0,1},{1,0},{2,3},{3,2},{4,5},{5,4},{6,7},{7,6},{8,9},{9,8},{10,11... | collective-permute-start | bytes 3145736 | tf_op jit(solution)/shard_map/ppermute | solution.py:28
  46.2 27.7 %collective-permute-start.13 = (bf16[2,2,2,2,128,256]{5,4,3,2,1,0:T(8,128)(2,1)}, bf16[2,2,2,2,128,256]{5,4,3,2,1,0:T(8,128)(2,1)}, u32[]{:S(2)}, u32[]{:S(2)}) collective-permute-start(bf16[2,2,2,2,128,256]{5,4,3,2,1,0:T(8,128)(2,1)} %pad_maximum_fusion.3), channel_id=1, source_target_pairs={{0,1},{1,0},{2,3},{3,2},{4,5},{5,4},{6,7},{7,6},{8,9},{9,8},{10,11... | collective-permute-start | bytes 3145736 | tf_op jit(solution)/shard_map/ppermute | solution.py:28
  46.3 3.7 %collective-permute-start.4 = (f32[2,8,128]{2,1,0:T(8,128)S(1)}, f32[2,8,128]{2,1,0:T(8,128)S(1)}, u32[]{:S(2)}, u32[]{:S(2)}) collective-permute-start(f32[2,8,128]{2,1,0:T(8,128)S(1)} %get-tuple-element.39), channel_id=1, source_target_pairs={{0,8},{8,0},{16,24},{24,16},{1,9},{9,1},{17,25},{25,17},{2,10},{10... | collective-permute-start | bytes 24584 | tf_op jit(solution)/shard_map/ppermute | solution.py:28
  50.0 20.5 %collective-permute-start.5 = (f32[2,2,8,128]{3,2,1,0:T(8,128)S(1)}, f32[2,2,8,128]{3,2,1,0:T(8,128)S(1)}, u32[]{:S(2)}, u32[]{:S(2)}) collective-permute-start(f32[2,2,8,128]{3,2,1,0:T(8,128)S(1)} %pad_maximum_fusion.13), channel_id=1, source_target_pairs={{0,4},{4,0},{1,5},{5,1},{2,6},{6,2},{3,7},{7,3},{8,12},{12,8},{9,1... | collective-permute-start | bytes 49160 | tf_op jit(solution)/shard_map/ppermute | solution.py:28
  52.0 16.6 %copy-start.12 = (f32[32,8,8]{2,1,0:T(8,128)S(1)}, f32[32,8,8]{2,1,0:T(8,128)}, u32[]{:S(2)}) copy-start(f32[32,8,8]{2,1,0:T(8,128)} %get-tuple-element.48) | copy-start | bytes 24580
  52.0 16.7 %copy-start.13 = (bf16[128,1024]{1,0:T(8,128)(2,1)S(1)}, bf16[128,1024]{1,0:T(8,128)(2,1)}, u32[]{:S(2)}) copy-start(bf16[128,1024]{1,0:T(8,128)(2,1)} %param.24) | copy-start | bytes 786436
  52.0 17.6 %copy-start.24 = (f32[16]{0:T(128)S(1)}, f32[16]{0:T(128)}, u32[]{:S(2)}) copy-start(f32[16]{0:T(128)} %param.29) | copy-start | bytes 196
  52.0 17.7 %copy-start.15 = (bf16[128,8,128]{2,1,0:T(8,128)(2,1)S(1)}, bf16[128,8,128]{2,1,0:T(8,128)(2,1)}, u32[]{:S(2)}) copy-start(bf16[128,8,128]{2,1,0:T(8,128)(2,1)} %param.20) | copy-start | bytes 786436
  52.0 19.1 %copy-start.6 = (bf16[2,2,128,256]{3,2,1,0:T(8,128)(2,1)S(1)}, bf16[2,2,128,256]{3,2,1,0:T(8,128)(2,1)}, u32[]{:S(2)}) copy-start(bf16[2,2,128,256]{3,2,1,0:T(8,128)(2,1)} %copy-done.5) | copy-start | bytes 786436
  71.1 2.8 %copy-start.4 = (bf16[2,2,128,256]{3,2,1,0:T(8,128)(2,1)S(1)}, bf16[2,2,128,256]{3,2,1,0:T(8,128)(2,1)}, u32[]{:S(2)}) copy-start(bf16[2,2,128,256]{3,2,1,0:T(8,128)(2,1)} %copy-done.3) | copy-start | bytes 786436
  97.5 23.4 %collective-permute-start.20 = (bf16[2,2,4,128,256]{4,3,2,1,0:T(8,128)(2,1)}, bf16[2,2,4,128,256]{4,3,2,1,0:T(8,128)(2,1)}, u32[]{:S(2)}, u32[]{:S(2)}) collective-permute-start(bf16[2,2,4,128,256]{4,3,2,1,0:T(8,128)(2,1)} %get-tuple-element.10), channel_id=1, source_target_pairs={{0,1},{1,0},{2,3},{3,2},{4,5},{5,4},{6,7},{7,6},{8,9},{9,8},{10,11... | collective-permute-start | bytes 3145736 | tf_op jit(solution)/shard_map/ppermute | solution.py:28
  98.7 22.2 %copy-start.10 = (bf16[2,2,4,128,256]{4,3,2,1,0:T(8,128)(2,1)S(1)}, bf16[2,2,4,128,256]{4,3,2,1,0:T(8,128)(2,1)}, u32[]{:S(2)}) copy-start(bf16[2,2,4,128,256]{4,3,2,1,0:T(8,128)(2,1)} %get-tuple-element.9) | copy-start | bytes 3145732
  98.7 9.2 %collective-permute-start.1 = (bf16[2,128,512]{2,1,0:T(8,128)(2,1)S(1)}, bf16[2,128,512]{2,1,0:T(8,128)(2,1)S(1)}, u32[]{:S(2)}, u32[]{:S(2)}) collective-permute-start(bf16[2,128,512]{2,1,0:T(8,128)(2,1)S(1)} %get-tuple-element.29), channel_id=1, source_target_pairs={{0,8},{8,0},{16,24},{24,16},{1,9},{9,1},{17,25},{25,17},{2,10},{10... | collective-permute-start | bytes 786440 | tf_op jit(solution)/shard_map/ppermute | solution.py:28
  98.8 24.9 %collective-permute-start.17 = (bf16[2,2,4,128,256]{4,3,2,1,0:T(8,128)(2,1)}, bf16[2,2,4,128,256]{4,3,2,1,0:T(8,128)(2,1)}, u32[]{:S(2)}, u32[]{:S(2)}) collective-permute-start(bf16[2,2,4,128,256]{4,3,2,1,0:T(8,128)(2,1)} %get-tuple-element.8), channel_id=1, source_target_pairs={{0,1},{1,0},{2,3},{3,2},{4,5},{5,4},{6,7},{7,6},{8,9},{9,8},{10,11... | collective-permute-start | bytes 3145736 | tf_op jit(solution)/shard_map/ppermute | solution.py:28
  100.5 12.6 %collective-permute-start.7 = (bf16[2,8,128,64]{2,3,1,0:T(8,128)(2,1)S(1)}, bf16[2,8,128,64]{2,3,1,0:T(8,128)(2,1)S(1)}, u32[]{:S(2)}, u32[]{:S(2)}) collective-permute-start(bf16[2,8,128,64]{2,3,1,0:T(8,128)(2,1)S(1)} %fusion.39), channel_id=1, source_target_pairs={{0,8},{8,0},{16,24},{24,16},{1,9},{9,1},{17,25},{25,17},{2,10},{10... | collective-permute-start | bytes 786440 | tf_op jit(solution)/shard_map/ppermute | solution.py:308
  108.8 46.9 %collective-permute-start.2 = (bf16[2,2,128,512]{3,2,1,0:T(8,128)(2,1)}, bf16[2,2,128,512]{3,2,1,0:T(8,128)(2,1)}, u32[]{:S(2)}, u32[]{:S(2)}) collective-permute-start(bf16[2,2,128,512]{3,2,1,0:T(8,128)(2,1)} %get-tuple-element.25), channel_id=1, source_target_pairs={{0,4},{4,0},{1,5},{5,1},{2,6},{6,2},{3,7},{7,3},{8,12},{12,8},{9,1... | collective-permute-start | bytes 1572872 | tf_op jit(solution)/shard_map/ppermute | solution.py:28
  114.5 12.5 %collective-permute-start.8 = (bf16[2,8,128,64]{2,3,1,0:T(8,128)(2,1)S(1)}, bf16[2,8,128,64]{2,3,1,0:T(8,128)(2,1)S(1)}, u32[]{:S(2)}, u32[]{:S(2)}) collective-permute-start(bf16[2,8,128,64]{2,3,1,0:T(8,128)(2,1)S(1)} %fusion.15), channel_id=1, source_target_pairs={{0,16},{8,24},{1,17},{9,25},{2,18},{10,26},{3,19},{11,27},{4,20},{... | collective-permute-start | bytes 786440 | tf_op jit(solution)/shard_map/ppermute | solution.py:308
  120.9 2.8 %copy-start.9 = (bf16[2,2,4,128,256]{4,3,2,1,0:T(8,128)(2,1)S(1)}, bf16[2,2,4,128,256]{4,3,2,1,0:T(8,128)(2,1)}, u32[]{:S(2)}) copy-start(bf16[2,2,4,128,256]{4,3,2,1,0:T(8,128)(2,1)} %get-tuple-element.7) | copy-start | bytes 3145732
  122.5 6.3 %copy-start.1 = (f32[2,2,4,128,256]{4,3,2,1,0:T(8,128)}, f32[2,2,4,128,256]{4,3,2,1,0:T(8,128)S(1)}, u32[]{:S(2)}) copy-start(f32[2,2,4,128,256]{4,3,2,1,0:T(8,128)S(1)} %convert_add_fusion) | copy-start | bytes 6291460
  122.6 13.6 %collective-permute-start.21 = (bf16[8,128,256]{2,1,0:T(8,128)(2,1)S(1)}, bf16[8,128,256]{2,1,0:T(8,128)(2,1)S(1)}, u32[]{:S(2)}, u32[]{:S(2)}) collective-permute-start(bf16[8,128,256]{2,1,0:T(8,128)(2,1)S(1)} %bitcast.138), channel_id=1, source_target_pairs={{0,4},{4,0},{1,5},{5,1},{2,6},{6,2},{3,7},{7,3},{8,12},{12,8},{9,1... | collective-permute-start | bytes 1572872 | tf_op jit(solution)/shard_map/ppermute | solution.py:28
  123.7 3.3 %copy-start.8 = (bf16[128,1024]{0,1:T(8,128)(2,1)S(1)}, bf16[128,1024]{0,1:T(8,128)(2,1)}, u32[]{:S(2)}) copy-start(bf16[128,1024]{0,1:T(8,128)(2,1)} %copy-done.7) | copy-start | bytes 786436
  123.7 3.3 %copy-start.11 = (f32[128,1024]{0,1:T(8,128)S(1)}, f32[128,1024]{0,1:T(8,128)}, u32[]{:S(2)}) copy-start(f32[128,1024]{0,1:T(8,128)} %copy.64) | copy-start | bytes 1572868
  123.7 3.3 %copy-start.26 = (f32[128,2,8,64]{0,3,2,1:T(8,128)S(1)}, f32[128,2,8,64]{0,3,2,1:T(8,128)}, u32[]{:S(2)}) copy-start(f32[128,2,8,64]{0,3,2,1:T(8,128)} %convolution_bitcast_fusion.1) | copy-start | bytes 1572868
  125.3 3.4 %copy-start.2 = (f32[2,2,4,128,256]{4,3,2,1,0:T(8,128)}, f32[2,2,4,128,256]{4,3,2,1,0:T(8,128)S(1)}, u32[]{:S(2)}) copy-start(f32[2,2,4,128,256]{4,3,2,1,0:T(8,128)S(1)} %convert_add_fusion.1) | copy-start | bytes 6291460
  125.4 14.2 %collective-permute-start.18 = (bf16[8,128,256]{2,1,0:T(8,128)(2,1)S(1)}, bf16[8,128,256]{2,1,0:T(8,128)(2,1)S(1)}, u32[]{:S(2)}, u32[]{:S(2)}) collective-permute-start(bf16[8,128,256]{2,1,0:T(8,128)(2,1)S(1)} %bitcast.139), channel_id=1, source_target_pairs={{0,2},{1,3},{2,0},{3,1},{4,6},{5,7},{6,4},{7,5},{8,10},{9,11},{10,... | collective-permute-start | bytes 1572872 | tf_op jit(solution)/shard_map/ppermute | solution.py:28
  128.8 7.5 %slice-start = ((f32[2,2,4,128,256]{4,3,2,1,0:T(8,128)}), f32[1,2,4,128,256]{4,3,2,1,0:T(8,128)S(1)}, s32[]{:S(2)}) async-start(f32[2,2,4,128,256]{4,3,2,1,0:T(8,128)} %copy-done.1), calls=%async_computation | async-start | bytes 2097152 | tf_op jit(solution)/shard_map/slice | solution.py:424
  128.8 10.8 %slice-start.1 = ((f32[2,2,4,128,256]{4,3,2,1,0:T(8,128)}), f32[1,2,4,128,256]{4,3,2,1,0:T(8,128)S(1)}, s32[]{:S(2)}) async-start(f32[2,2,4,128,256]{4,3,2,1,0:T(8,128)} %copy-done.2), calls=%async_computation.1 | async-start | bytes 2097152 | tf_op jit(solution)/shard_map/slice | solution.py:424
  136.4 8.0 %collective-permute-start.22 = (bf16[4,128,256]{2,1,0:T(8,128)(2,1)S(1)}, bf16[4,128,256]{2,1,0:T(8,128)(2,1)S(1)}, u32[]{:S(2)}, u32[]{:S(2)}) collective-permute-start(bf16[4,128,256]{2,1,0:T(8,128)(2,1)S(1)} %slice.190), channel_id=1, source_target_pairs={{0,2},{1,3},{2,0},{3,1},{4,6},{5,7},{6,4},{7,5},{8,10},{9,11},{10,... | collective-permute-start | bytes 786440 | tf_op jit(solution)/shard_map/ppermute | solution.py:28
  139.7 6.4 %collective-permute-start.19 = (bf16[4,128,256]{2,1,0:T(8,128)(2,1)S(1)}, bf16[4,128,256]{2,1,0:T(8,128)(2,1)S(1)}, u32[]{:S(2)}, u32[]{:S(2)}) collective-permute-start(bf16[4,128,256]{2,1,0:T(8,128)(2,1)S(1)} %slice.191), channel_id=1, source_target_pairs={{0,4},{4,0},{1,5},{5,1},{2,6},{6,2},{3,7},{7,3},{8,12},{12,8},{9,1... | collective-permute-start | bytes 786440 | tf_op jit(solution)/shard_map/ppermute | solution.py:28
  144.4 3.5 %copy-start.21 = (f32[1024]{0:T(1024)S(1)}, f32[1024]{0:T(1024)}, u32[]{:S(2)}) copy-start(f32[1024]{0:T(1024)} %param.30) | copy-start | bytes 12292
  146.3 6.4 %collective-permute-start.23 = (bf16[2,128,512]{2,1,0:T(8,128)(2,1)S(1)}, bf16[2,128,512]{2,1,0:T(8,128)(2,1)S(1)}, u32[]{:S(2)}, u32[]{:S(2)}) collective-permute-start(bf16[2,128,512]{2,1,0:T(8,128)(2,1)S(1)} %fusion.19), channel_id=1, source_target_pairs={{0,8},{8,0},{16,24},{24,16},{1,9},{9,1},{17,25},{25,17},{2,10},{10... | collective-permute-start | bytes 786440 | tf_op jit(solution)/shard_map/ppermute | solution.py:28
  152.8 13.2 %collective-permute-start.24 = (bf16[1,128,512]{2,1,0:T(8,128)(2,1)S(1)}, bf16[1,128,512]{2,1,0:T(8,128)(2,1)S(1)}, u32[]{:S(2)}, u32[]{:S(2)}) collective-permute-start(bf16[1,128,512]{2,1,0:T(8,128)(2,1)S(1)} %slice.192), channel_id=1, source_target_pairs={{0,16},{8,24},{16,0},{24,8},{1,17},{9,25},{17,1},{25,9},{2,18},{10... | collective-permute-start | bytes 393224 | tf_op jit(solution)/shard_map/ppermute | solution.py:28

commit v2 on v1

v2 whole, which is shorter than its diff:
```python
import functools
import math

import jax
import jax.numpy as jnp
from jax import lax
from jax.experimental import pallas as pl
from jax.experimental.pallas import tpu as pltpu
from jax.sharding import PartitionSpec as P

SEQ, EXP, TP = "seq", "exp", "tp"
WINDOW = 4096
HP = 64
NS = 128
STRETCH = 128
CAP = 40
EPSILON = 1e-05
F32 = jnp.float32
BF16 = jnp.bfloat16


def bits_of(count):
    assert count & (count - 1) == 0
    return [1 << b for b in reversed(range(count.bit_length() - 1))]


def swap(block, axis, bit):
    return lax.ppermute(block, axis, [(i, i ^ bit) for i in range(lax.axis_size(axis))])


def spread(block, stages):
    for axis, bit in stages:
        block = jnp.stack([block, swap(block, axis, bit)])
    return block


def stages_of(axis, bits):
    return [(axis, bit) for bit in bits]


def offsets_of(bits):
    offsets = [0]
    for bit in bits:
        offsets = offsets + [o ^ bit for o in offsets]
    return offsets


def staged_call(body, scalars, near, arrays, out_shape, scratch=(), vmem=20):
    count, outs = len(arrays), len(out_shape)

    def kernel(*refs):
        inside = list(refs)
        first, inside = inside[: len(scalars) + len(near)], inside[len(scalars) + len(near) :]
        sources, inside = inside[:count], inside[count:]
        results, inside = inside[:outs], inside[outs:]
        targets, inside = inside[:count], inside[count:]
        sem, extra = inside[0], inside[1:]
        copies = [
            pltpu.make_async_copy(source, target, sem.at[i])
            for i, (source, target) in enumerate(zip(sources, targets))
        ]
        for copy in copies:
            copy.start()
        for copy in copies:
            copy.wait()
        body(*first, *targets, *results, *extra)

    smem = pl.BlockSpec(memory_space=pltpu.SMEM)
    local = pl.BlockSpec(memory_space=pltpu.VMEM)
    return pl.pallas_call(
        kernel,
        out_shape=out_shape,
        in_specs=[smem] * len(scalars)
        + [local] * len(near)
        + [pl.BlockSpec(memory_space=pltpu.HBM)] * count,
        out_specs=[local] * outs,
        scratch_shapes=[pltpu.VMEM(a.shape, a.dtype) for a in arrays]
        + [pltpu.SemaphoreType.DMA((count,))]
        + list(scratch),
        compiler_params=pltpu.CompilerParams(vmem_limit_bytes=vmem * 1024 * 1024),
    )(*scalars, *near, *[pltpu.with_memory_space_constraint(a, pltpu.HBM) for a in arrays])


def attention_kernel(offsets, where_ref, query_ref, *refs):
    kv_refs, (out_ref, score_ref, top_ref, sum_ref, acc_ref) = refs[:-5], refs[-5:]
    total, size = query_ref.shape
    shared = 2
    wide = kv_refs[0].shape[1] // 2
    keys = wide // shared
    heads = total // keys
    mine = where_ref[2]
    scale = 1.0 / math.sqrt(size)
    row = lax.broadcasted_iota(jnp.int32, (total, keys), 0)
    column = lax.broadcasted_iota(jnp.int32, (total, keys), 1)
    lower = lax.rem(row, heads) < heads // shared
    behind = row // heads - column
    source = lax.broadcasted_iota(jnp.int32, (wide, wide), 0)
    target = lax.broadcasted_iota(jnp.int32, (wide, wide), 1)
    apart = target == lax.rem(source, keys) * shared + source // keys
    apart = apart.astype(F32).astype(BF16)
    part = lambda rows: jnp.dot(apart, rows, preferred_element_type=F32).astype(BF16)
    blocks = [(kv_ref, b) for kv_ref in kv_refs for b in range(kv_ref.shape[0])]
    gaps = [(mine - (mine ^ offset)) * keys for offset in offsets]
    seen = [(gap >= 0) & (gap - (keys - 1) < WINDOW) for gap in gaps]
    top_ref[...] = jnp.full_like(top_ref, -jnp.inf)
    sum_ref[...] = jnp.zeros_like(sum_ref)
    acc_ref[...] = jnp.zeros_like(acc_ref)

    def scores(at):
        kv_ref, b = blocks[at]
        score = lax.dot_general(
            query_ref[...],
            part(kv_ref[b, :wide]),
            (((1,), (1,)), ((), ())),
            preferred_element_type=F32,
        )
        return jnp.where(lower, score[:, :keys], score[:, keys:]) * scale

    for at, gap in enumerate(gaps):
        inside = (gap >= keys - 1) & (gap + keys - 1 < WINDOW)

        @pl.when(inside)
        def _(at=at):
            score = scores(at)
            score_ref[at] = score
            top_ref[...] = jnp.maximum(top_ref[...], score)

        @pl.when(seen[at] & jnp.logical_not(inside))
        def _(at=at, gap=gap):
            distance = behind + gap
            score = jnp.where((distance >= 0) & (distance < WINDOW), scores(at), -jnp.inf)
            score_ref[at] = score
            top_ref[...] = jnp.maximum(top_ref[...], score)

    top = jnp.max(top_ref[...], axis=1, keepdims=True)
    top_ref[...] = jnp.broadcast_to(top, (total, keys))

    for at, (kv_ref, b) in enumerate(blocks):

        @pl.when(seen[at])
        def _(at=at, kv_ref=kv_ref, b=b):
            weight = jnp.exp(score_ref[at] - top_ref[...])
            sum_ref[...] += weight
            weight = jnp.concatenate(
                [jnp.where(lower, weight, 0.0), jnp.where(lower, 0.0, weight)], axis=1
            )
            acc_ref[...] += jnp.dot(
                weight.astype(BF16), part(kv_ref[b, wide:]), preferred_element_type=F32
            )

    out_ref[...] = (acc_ref[...] / jnp.sum(sum_ref[...], axis=1, keepdims=True)).astype(BF16)


def attention(query, kv_parts, offsets, where):
    rows, heads, size = query.shape
    assert kv_parts[0].shape[1] == 4 * rows and size == rows
    total = rows * heads
    vmem = pl.BlockSpec(memory_space=pltpu.VMEM)
    out = pl.pallas_call(
        functools.partial(attention_kernel, offsets),
        out_shape=jax.ShapeDtypeStruct((total, size), BF16),
        in_specs=[pl.BlockSpec(memory_space=pltpu.SMEM), vmem] + [vmem] * len(kv_parts),
        out_specs=vmem,
        scratch_shapes=[pltpu.VMEM((len(offsets), total, rows), F32)]
        + [pltpu.VMEM((total, rows), F32)] * 2
        + [pltpu.VMEM((total, size), F32)],
        compiler_params=pltpu.CompilerParams(
            vmem_limit_bytes=(len(offsets) + 40) * total * rows * 4
        ),
        name="attention",
    )(where, query.reshape(total, size), *kv_parts)
    return out.reshape(rows, heads, size)


def norm_kernel(
    where_ref, hidden_ref, gain_ref, router_ref, id_ref, slot_ref, log_ref, own_ref, normed_ref
):
    rows, _ = hidden_ref.shape
    chunk = own_ref.shape[1]
    hidden = hidden_ref[...].astype(F32)
    mean_square = jnp.mean(hidden * hidden, axis=1, keepdims=True)
    normed = (hidden * lax.rsqrt(mean_square + EPSILON) * gain_ref[...]).astype(BF16)
    normed_ref[...] = normed
    start = pl.multiple_of(where_ref[0] * chunk, 128)
    own_ref[0:rows, :] = normed_ref[:, pl.ds(start, chunk)]
    logits = lax.dot_general(
        router_ref[...], normed, (((1,), (1,)), ((), ())), preferred_element_type=F32
    )
    gates = 1.0 / (1.0 + jnp.exp(-logits))
    expert = lax.broadcasted_iota(jnp.int32, gates.shape, 0)
    chosen = [
        jnp.sum(jnp.where(id_ref[k : k + 1] == expert, gates, 0.0), axis=0, keepdims=True)
        for k in range(2)
    ]
    both = chosen[0] + chosen[1]
    decay = jnp.sum(log_ref[...], axis=1, keepdims=True)
    head = lax.broadcasted_iota(jnp.int32, log_ref.shape, 0)
    lane = lax.broadcasted_iota(jnp.int32, log_ref.shape, 1)
    decay = jnp.sum(jnp.where(head == lane, decay, 0.0), axis=0, keepdims=True)
    info = jnp.concatenate(
        [
            id_ref[...].astype(F32),
            slot_ref[...].astype(F32),
            chosen[0] / both,
            chosen[1] / both,
            decay,
            jnp.zeros_like(decay),
        ],
        axis=0,
    )
    parts = []
    for _ in range(3):
        part = info.astype(BF16).astype(F32)
        parts.append(part)
        info = info - part
    tail = jnp.concatenate(
        [
            jnp.concatenate([parts[0], parts[1]], axis=1),
            jnp.concatenate([parts[2], jnp.zeros_like(info)], axis=1),
        ],
        axis=0,
    )
    tail = jnp.concatenate([tail, jnp.zeros((16, chunk - 256), F32)], axis=1)
    own_ref[rows:, :] = tail.astype(BF16)


def info_of(block):
    block = block.astype(F32)
    return block[0:8, 0:128] + block[0:8, 128:256] + block[8:16, 0:128]


def norm_share(where, chunk, hidden, gain, router, ids, slots, log_decay):
    rows, width = hidden.shape
    assert rows == 128 and chunk >= 512
    return staged_call(
        norm_kernel,
        (where,),
        (),
        (hidden, gain, router, ids, slots, log_decay),
        [jax.ShapeDtypeStruct((rows + 16, chunk), BF16)],
        [pltpu.VMEM((rows, width), BF16)],
    )[0]


def expert_kernel(
    offsets,
    where_ref,
    info_ref,
    left_ref,
    right_ref,
    gate_up_ref,
    down_ref,
    keep0_ref,
    keep1_ref,
    send0_ref,
    send1_ref,
    rows_ref,
    hot_ref,
    weight_ref,
):
    expert = pl.program_id(1)
    experts = pl.num_programs(1)
    me = where_ref[0]
    first = where_ref[1]
    far, _, nz, tokens, half = keep0_ref.shape
    parts = 2 * far
    local = rows_ref.shape[1]
    pairs = rows_ref.shape[0]

    def column(part, h):
        return pl.multiple_of((me ^ offsets[part]) * (2 * half) + h * half, 128)

    def pair_at(p):
        return (2 * p) // nz, (2 * p) % nz

    @pl.when(expert == 0)
    def _():
        for p in range(pairs):
            mx, mz = pair_at(p)
            info = jnp.concatenate([info_of(info_ref[mx, mz]), info_of(info_ref[mx, mz + 1])], axis=1)
            info_id = info[0:2].astype(jnp.int32)
            info_slot = info[2:4].astype(jnp.int32)
            block = lax.broadcasted_iota(jnp.int32, (1, 2 * tokens), 1) // tokens
            row = lax.broadcasted_iota(jnp.int32, (2 * CAP, 2 * tokens), 0)
            for e in range(local):
                match = []
                for k in range(2):
                    live = (info_slot[k : k + 1] >= 0) & (info_id[k : k + 1] == first + e)
                    code = jnp.where(live, block * CAP + info_slot[k : k + 1], -1)
                    match.append(row == code)
                hot_ref[p, e] = (match[0] | match[1]).astype(F32).astype(BF16)
                share = jnp.where(match[0], info[4:5], 0.0) + jnp.where(match[1], info[5:6], 0.0)
                weight_ref[p, e] = jnp.broadcast_to(
                    jnp.sum(share, axis=1, keepdims=True), (2 * CAP, 128)
                )
            hot = hot_ref[p].reshape(local * 2 * CAP, 2 * tokens)
            for part in range(parts):
                core, high = part // far, part % far
                for h in range(2):
                    if h == 0:
                        piece = left_ref[core, high, mx, mz : mz + 2]
                    else:
                        piece = right_ref[core, mx, high, mz : mz + 2]
                    piece = piece.reshape(2 * tokens, half)
                    picked = jnp.dot(hot, piece, preferred_element_type=F32).astype(BF16)
                    rows_ref[p, :, :, pl.ds(column(part, h), half)] = picked.reshape(
                        local, 2 * CAP, half
                    )

    rows = rows_ref[:, expert].reshape(pairs * 2 * CAP, rows_ref.shape[3])
    nt = (((1,), (1,)), ((), ()))
    gate = lax.dot_general(rows, gate_up_ref[0], nt, preferred_element_type=F32)
    up = lax.dot_general(rows, gate_up_ref[1], nt, preferred_element_type=F32)
    hidden = (gate / (1.0 + jnp.exp(-gate)) * up).astype(BF16)
    value = jnp.dot(hidden, down_ref[...], preferred_element_type=F32)
    for p in range(pairs):
        scaled = value[p * 2 * CAP : (p + 1) * 2 * CAP] * weight_ref[p, expert][:, :1]
        rows_ref[p, expert] = scaled.astype(BF16)

    @pl.when(expert == experts - 1)
    def _():
        for p in range(pairs):
            mx, mz = pair_at(p)
            hot = hot_ref[p].reshape(local * 2 * CAP, 2 * tokens)
            for part in range(parts):
                core, high = part // far, part % far
                for h in range(2):
                    value = rows_ref[p, :, :, pl.ds(column(part, h), half)]
                    value = value.reshape(local * 2 * CAP, half)
                    total = lax.dot_general(
                        hot, value, (((0,), (0,)), ((), ())), preferred_element_type=F32
                    )
                    total = total.astype(BF16).reshape(2, tokens, half)
                    if h == 0:
                        target = send0_ref if core else keep0_ref
                        target[high, mx, mz : mz + 2] = total
                    else:
                        target = send1_ref if core else keep1_ref
                        target[mx, high, mz : mz + 2] = total


def experts_apply(offsets, where, info, left, right, gate_up, down):
    nx, nz = info.shape[:2]
    _, far, _, _, tokens, half = left.shape
    local, _, units, width = gate_up.shape
    gx = max(1, 8 // nz)
    pairs = gx * nz // 2
    once = pl.Buffered(1)
    shape0 = jax.ShapeDtypeStruct((far, nx, nz, tokens, half), BF16)
    shape1 = jax.ShapeDtypeStruct((nx, far, nz, tokens, half), BF16)
    spec0 = pl.BlockSpec((far, gx, nz, tokens, half), lambda g, e, w: (0, g, 0, 0, 0))
    spec1 = pl.BlockSpec((gx, far, nz, tokens, half), lambda g, e, w: (g, 0, 0, 0, 0))
    return pl.pallas_call(
        functools.partial(expert_kernel, offsets),
        out_shape=[shape0, shape1, shape0, shape1],
        grid_spec=pltpu.PrefetchScalarGridSpec(
            num_scalar_prefetch=1,
            grid=(nx // gx, local),
            in_specs=[
                pl.BlockSpec((gx, nz, 16, 256), lambda g, e, w: (g, 0, 0, 0)),
                pl.BlockSpec(
                    (2, far, gx, nz, tokens, half),
                    lambda g, e, w: (0, 0, g, 0, 0, 0),
                    pipeline_mode=once,
                ),
                pl.BlockSpec(
                    (2, gx, far, nz, tokens, half),
                    lambda g, e, w: (0, g, 0, 0, 0, 0),
                    pipeline_mode=once,
                ),
                pl.BlockSpec((None, 2, units, width), lambda g, e, w: (e, 0, 0, 0)),
                pl.BlockSpec((None, units, width), lambda g, e, w: (e, 0, 0)),
            ],
            out_specs=[spec0, spec1, spec0, spec1],
            scratch_shapes=[
                pltpu.VMEM((pairs, local, 2 * CAP, width), BF16),
                pltpu.VMEM((pairs, local, 2 * CAP, 2 * tokens), BF16),
                pltpu.VMEM((pairs, local, 2 * CAP, 128), F32),
            ],
        ),
        compiler_params=pltpu.CompilerParams(vmem_limit_bytes=60 * 1024 * 1024),
        name="experts",
    )(where, info, left, right, gate_up, down)


def matches(info_ref, blocks, first, local):
    info = jnp.concatenate([info_of(info_ref[b]) for b in blocks], axis=1)
    tokens = info_ref.shape[2] // 2
    ids, slots = info[0:2].astype(jnp.int32), info[2:4].astype(jnp.int32)
    block = lax.broadcasted_iota(jnp.int32, (1, 2 * tokens), 1) // tokens
    row = lax.broadcasted_iota(jnp.int32, (2 * CAP, 2 * tokens), 0)
    for e in range(local):
        found = []
        for k in range(2):
            live = (slots[k : k + 1] >= 0) & (ids[k : k + 1] == first + e)
            found.append(row == jnp.where(live, block * CAP + slots[k : k + 1], -1))
        share = jnp.where(found[0], info[4:5], 0.0) + jnp.where(found[1], info[5:6], 0.0)
        yield (found[0] | found[1]).astype(F32).astype(BF16), jnp.sum(share, axis=1, keepdims=True)


def column_of(me, offset, h, half):
    return pl.multiple_of((me ^ offset) * (2 * half) + h * half, 128)


def combine(me, offsets, hot, value_of, keep_ref, send_ref, xo):
    tokens, half = keep_ref.shape[-2:]
    for core in range(2):
        for yi in range(2):
            for h in range(2):
                value = value_of(column_of(me, offsets[core][yi], h, half), half)
                total = lax.dot_general(
                    hot, value, (((0,), (0,)), ((), ())), preferred_element_type=F32
                )
                target = send_ref if core else keep_ref
                place = (h, yi, xo) if h == 0 else (h, xo, yi)
                target[place] = total.astype(BF16).reshape(2, tokens, half)


def paired(both):
    count, width = both.shape
    lane = lax.broadcasted_iota(jnp.int32, (count, 128), 1)
    low = lane < 64
    even = jnp.where(low, 2 * lane, 2 * lane - 128)
    take = lambda a, i: jnp.take_along_axis(a, i, axis=1, mode="promise_in_bounds")
    hidden = []
    for c in range(0, width, 256):
        one = both[:, c : c + 128]
        two = both[:, c + 128 : c + 256] if c + 128 < width else one
        gate = jnp.where(low, take(one, even), take(two, even))
        up = jnp.where(low, take(one, even + 1), take(two, even + 1))
        unit = (gate / (1.0 + jnp.exp(-gate)) * up).astype(BF16)
        hidden.append(unit[:, : (width - c) // 2] if width - c < 256 else unit)
    return jnp.concatenate(hidden, axis=1)


def gather_kernel(offsets, *refs):
    where_ref, gate_up_ref, down_ref = refs[:3]
    pieces = refs[3:19]
    results = refs[19:23]
    all_ref, rows_ref, hot_ref, weight_ref, wide_ref, tall_ref, info_ref = refs[23:30]
    piece_sem, wide_sem, tall_sem, info_sem = refs[30:]
    me, first = where_ref[0], where_ref[1]
    pairs, local, places, width = rows_ref.shape
    tokens, half = all_ref.shape[2], pieces[0].shape[-1]
    units = down_ref.shape[1]
    count = pairs * places

    def fetch(e, slot):
        return (
            pltpu.make_async_copy(gate_up_ref.at[e], wide_ref.at[slot], wide_sem.at[slot]),
            pltpu.make_async_copy(down_ref.at[e], tall_ref.at[slot], tall_sem.at[slot]),
        )

    copies = []
    for p in range(pairs):
        g, xo = p // 2, p % 2
        for core in range(2):
            for yi in range(2):
                for h in range(2):
                    if h == 0:
                        source = pieces[8 * g + 2 * core + yi].at[xo, :, 0:tokens]
                    else:
                        source = pieces[8 * g + 4 + 2 * core + xo].at[yi]
                    column = column_of(me, offsets[core][yi], h, half)
                    copies.append(
                        pltpu.make_async_copy(
                            source,
                            all_ref.at[p, :, :, pl.ds(column, half)],
                            piece_sem.at[len(copies)],
                        )
                    )
    notes = [
        pltpu.make_async_copy(
            pieces[b // 4 * 8].at[b // 2 % 2, b % 2, tokens : tokens + 16],
            info_ref.at[b],
            info_sem.at[b],
        )
        for b in range(2 * pairs)
    ]
    for copy in notes + copies:
        copy.start()
    for slot in range(2):
        if slot < local:
            for copy in fetch(slot, slot):
                copy.start()
    for copy in notes:
        copy.wait()
    for p in range(pairs):
        for e, (hot, weight) in enumerate(matches(info_ref, (2 * p, 2 * p + 1), first, local)):
            hot_ref[p, e] = hot
            weight_ref[p, e] = jnp.broadcast_to(weight, (places, 128))
    for p in range(pairs):
        for copy in copies[8 * p : 8 * p + 8]:
            copy.wait()
        hot = hot_ref[p].reshape(local * places, 2 * tokens)
        picked = jnp.dot(
            hot, all_ref[p].reshape(2 * tokens, width), preferred_element_type=F32
        ).astype(BF16)
        rows_ref[p] = picked.reshape(local, places, width)

    def one_expert(e, _):
        slot = lax.rem(e, 2)
        for copy in fetch(e, slot):
            copy.wait()
        rows = rows_ref[:, e].reshape(count, width)
        wide = wide_ref[slot].reshape(2 * units, width)
        both = lax.dot_general(
            rows, wide, (((1,), (1,)), ((), ())), preferred_element_type=F32
        )
        value = jnp.dot(paired(both), tall_ref[slot], preferred_element_type=F32)
        for p in range(pairs):
            scaled = value[p * places : (p + 1) * places] * weight_ref[p, e][:, :1]
            rows_ref[p, e] = scaled.astype(BF16)

        @pl.when(e + 2 < local)
        def _():
            for copy in fetch(e + 2, slot):
                copy.start()

        return 0

    lax.fori_loop(0, local, one_expert, 0)
    for p in range(pairs):
        combine(
            me,
            offsets,
            hot_ref[p].reshape(local * places, 2 * tokens),
            lambda column, half: rows_ref[p, :, :, pl.ds(column, half)].reshape(
                local * places, half
            ),
            *results[p // 2 * 2 : p // 2 * 2 + 2],
            p % 2,
        )


def experts_gather(offsets, where, pieces, gate_up, down):
    half = pieces[0].shape[-1]
    tokens = pieces[4].shape[-2]
    local, units, _, width = gate_up.shape
    pairs, places = 4, 2 * CAP
    result = jax.ShapeDtypeStruct((2, 2, 2, 2, tokens, half), BF16)
    smem = pl.BlockSpec(memory_space=pltpu.SMEM)
    vmem = pl.BlockSpec(memory_space=pltpu.VMEM)
    hbm = pl.BlockSpec(memory_space=pl.ANY)
    return pl.pallas_call(
        functools.partial(gather_kernel, offsets),
        out_shape=[result] * 4,
        in_specs=[smem, hbm, hbm] + [hbm] * len(pieces),
        out_specs=[vmem] * 4,
        scratch_shapes=[
            pltpu.VMEM((pairs, 2, tokens, width), BF16),
            pltpu.VMEM((pairs, local, places, width), BF16),
            pltpu.VMEM((pairs, local, places, 2 * tokens), BF16),
            pltpu.VMEM((pairs, local, places, 128), F32),
            pltpu.VMEM((2, units, 2, width), BF16),
            pltpu.VMEM((2, units, width), BF16),
            pltpu.VMEM((2 * pairs, 16, 2 * 128), BF16),
            pltpu.SemaphoreType.DMA((8 * pairs,)),
            pltpu.SemaphoreType.DMA((2,)),
            pltpu.SemaphoreType.DMA((2,)),
            pltpu.SemaphoreType.DMA((2 * pairs,)),
        ],
        compiler_params=pltpu.CompilerParams(vmem_limit_bytes=44 * 1024 * 1024),
        name="experts",
    )(where, gate_up, down, *pieces)


def group_bits():
    far, near = bits_of(lax.axis_size(SEQ))
    (side,) = bits_of(lax.axis_size(EXP))
    high, core = bits_of(lax.axis_size(TP))
    return far, near, side, high, core


def spread_near(block):
    _, _, side, high, core = group_bits()
    half = block.shape[-1] // 2
    left, right = block[..., :half], block[..., :-16, half:]
    left = jnp.stack([left, swap(left, EXP, side)])
    right = jnp.stack([right, swap(right, TP, high)])
    left2 = swap(left, TP, high)
    right2 = swap(right, EXP, side)
    first = [swap(left, TP, core), swap(right, TP, core)]
    second = [swap(left2, TP, core), swap(right2, TP, core)]
    return [left, left2, first[0], second[0], right, right2, first[1], second[1]]


def fold(kept, sent, axis, bit):
    return kept + swap(sent.astype(BF16), axis, bit).astype(F32)


HIGHEST = lax.Precision.HIGHEST


def running_sum(log_ref, rows, columns):
    i = lax.broadcasted_iota(jnp.int32, (rows, rows), 0)
    j = lax.broadcasted_iota(jnp.int32, (rows, rows), 1)
    decay = log_ref[...]
    if columns:
        ones = (j <= i).astype(F32)
        return lax.dot_general(
            ones, decay, (((1,), (1,)), ((), ())), precision=HIGHEST, preferred_element_type=F32
        )
    ones = (i <= j).astype(F32)
    return jnp.dot(decay, ones, precision=HIGHEST, preferred_element_type=F32)


def group_rows(ref, g, groups):
    count = ref.shape[0]
    row = lax.broadcasted_iota(jnp.int32, (count // groups, count), 0)
    column = lax.broadcasted_iota(jnp.int32, (count // groups, count), 1)
    pick = (column == row * groups + g).astype(F32).astype(BF16)
    return jnp.dot(pick, ref[...], preferred_element_type=F32)


def state_kernel(input_ref, inflow_ref, readout_ref, step_ref, log_ref, intra_ref, state_ref, sent_ref):
    rows = input_ref.shape[0]
    heads = step_ref.shape[0]
    groups = inflow_ref.shape[0] // rows
    per_group = heads // groups
    across = running_sum(log_ref, rows, False)
    down = running_sum(log_ref, rows, True)
    step = step_ref[...]
    i = lax.broadcasted_iota(jnp.int32, (rows, rows), 0)
    j = lax.broadcasted_iota(jnp.int32, (rows, rows), 1)
    causal = j <= i
    weight = jnp.transpose(jnp.exp(across[:, rows - 1 :] - across) * step)
    for g in range(groups):
        wide = group_rows(inflow_ref, g, groups)
        both = lax.dot_general(
            group_rows(readout_ref, g, groups).astype(BF16),
            wide.astype(BF16),
            (((1,), (1,)), ((), ())),
            preferred_element_type=F32,
        )
        for pair in range(0, per_group, 2):
            first = g * per_group + pair
            columns = slice(first * HP, (first + 2) * HP)
            inputs = input_ref[:, columns]
            intra, state = [], []
            for h in (first, first + 1):
                gap = jnp.where(causal, down[:, h : h + 1] - across[h : h + 1], 0.0)
                decay = jnp.where(causal, jnp.exp(gap), 0.0)
                mixing = (decay * both * step[h : h + 1]).astype(BF16)
                intra.append(jnp.dot(mixing, inputs, preferred_element_type=F32))
                weighted = (weight[:, h : h + 1] * wide).astype(BF16)
                state.append(
                    lax.dot_general(
                        weighted, inputs, (((0,), (0,)), ((), ())), preferred_element_type=F32
                    )
                )
            left = lax.broadcasted_iota(jnp.int32, (rows, 2 * HP), 1) < HP
            intra_ref[:, columns] = jnp.where(left, intra[0], intra[1])
            left = lax.broadcasted_iota(jnp.int32, (NS, 2 * HP), 1) < HP
            block = jnp.where(left, state[0], state[1])
            state_ref[:, columns] = block
            sent_ref[:, columns] = block.astype(BF16)


def state_local(inputs, inflow, readout, step, log_decay):
    rows, channels = inputs.shape
    assert rows == STRETCH
    return staged_call(
        state_kernel,
        (),
        (),
        (inputs, inflow, readout, step, log_decay),
        [
            jax.ShapeDtypeStruct((rows, channels), F32),
            jax.ShapeDtypeStruct((NS, channels), F32),
            jax.ShapeDtypeStruct((NS, channels), BF16),
        ],
    )


def lanes_of(factors, heads):
    left = lax.broadcasted_iota(jnp.int32, (1, 2 * HP), 1) < HP
    return jnp.concatenate(
        [
            jnp.where(left, factors[:, h : h + 1], factors[:, h + 1 : h + 2])
            for h in range(0, heads, 2)
        ],
        axis=1,
    )


def decay_between(place, total_ref, order, span, heads):
    row = lambda m: info_of(total_ref[order[m]])[6:7]
    upper = (place & span) != 0
    lead = own = jnp.zeros_like(row(0))
    theirs = jnp.zeros_like(own)
    for m in range(span):
        lead = lead + jnp.where((place ^ m) < place, row(m), 0.0)
        own = own + row(m)
        theirs = theirs + row(span + m)
    lead, own, theirs = jnp.exp(lead), jnp.exp(own), jnp.exp(theirs)
    return (
        lanes_of(jnp.where(upper, lead, 0.0), heads),
        lanes_of(jnp.where(upper, own, 1.0), heads),
        lanes_of(jnp.where(upper, 1.0, theirs), heads),
    )


def scan_kernel(order, span, heads, where_ref, total_ref, other_ref, state_ref, *refs):
    entering_ref = refs[0] if len(refs) == 4 else None
    new_entering_ref, new_state_ref, sent_ref = refs[-3:]
    lead, own, theirs = decay_between(where_ref[2], total_ref, order, span, heads)
    other = other_ref[...].astype(F32)
    entering = lead * other
    if entering_ref is not None:
        entering = entering + entering_ref[...]
    new_entering_ref[...] = entering
    state = own * other + theirs * state_ref[...]
    new_state_ref[...] = state
    sent_ref[...] = state.astype(BF16)


def scan_step(order, span, heads, where, totals, other, state, *entering):
    vmem = pl.BlockSpec(memory_space=pltpu.VMEM)
    smem = pl.BlockSpec(memory_space=pltpu.SMEM)
    like = jax.ShapeDtypeStruct(state.shape, F32)
    return pl.pallas_call(
        functools.partial(scan_kernel, order, span, heads),
        out_shape=[like, like, jax.ShapeDtypeStruct(state.shape, BF16)],
        in_specs=[smem] + [vmem] * (3 + len(entering)),
        out_specs=[vmem] * 3,
        compiler_params=pltpu.CompilerParams(vmem_limit_bytes=20 * 1024 * 1024),
    )(where, totals, other, state, *entering)


def span_route(span):
    nx, nz = lax.axis_size(EXP), lax.axis_size(SEQ)
    axis, bit = (EXP, span) if span < nx else (SEQ, span // nx)
    both = span * 2 < nx * nz
    pairs = [(i, i ^ bit) for i in range(lax.axis_size(axis)) if both or not i & bit]
    return axis, pairs


def finish_kernel(
    order, span, where_ref, total_ref, other_ref, entering_ref, intra_ref, readout_ref, log_ref, input_ref, gate_ref, skip_ref, gain_ref, out_ref
):
    rows, channels = input_ref.shape
    heads = log_ref.shape[0]
    groups = readout_ref.shape[0] // rows
    width = channels // groups
    grown = jnp.exp(running_sum(log_ref, rows, True))
    lead, _, _ = decay_between(where_ref[2], total_ref, order, span, heads)
    left = lax.broadcasted_iota(jnp.int32, (rows, 2 * HP), 1) < HP
    for g in range(groups):
        columns = slice(g * width, (g + 1) * width)
        inter = jnp.dot(
            group_rows(readout_ref, g, groups),
            lead[:, columns] * other_ref[:, columns].astype(F32) + entering_ref[:, columns],
            precision=HIGHEST,
            preferred_element_type=F32,
        )
        first = g * (heads // groups)
        factor = jnp.concatenate(
            [
                jnp.where(left, grown[:, h : h + 1], grown[:, h + 1 : h + 2])
                for h in range(first, first + heads // groups, 2)
            ],
            axis=1,
        )
        mixed = (
            intra_ref[:, columns]
            + factor * inter
            + skip_ref[:, columns] * input_ref[:, columns].astype(F32)
        )
        gate = gate_ref[:, columns].astype(F32)
        gated = mixed * (gate / (1.0 + jnp.exp(-gate)))
        mean_square = jnp.mean(gated * gated, axis=1, keepdims=True)
        normed = gated * lax.rsqrt(mean_square + EPSILON)
        out_ref[:, columns] = (normed * gain_ref[:, columns]).astype(BF16)


def state_finish(order, span, where, totals, other, entering, intra, *arrays):
    return staged_call(
        functools.partial(finish_kernel, order, span),
        (where,),
        (totals, other, entering, intra),
        arrays,
        [jax.ShapeDtypeStruct(arrays[2].shape, BF16)],
    )[0]


def routed_in_general(own, gate_up, down_proj):
    nz, nx, nt = lax.axis_size(SEQ), lax.axis_size(EXP), lax.axis_size(TP)
    x, t = lax.axis_index(EXP), lax.axis_index(TP)
    info, own = own[-16:, :256], own[:-16]
    rows, chunk = own.shape
    half = chunk // 2
    tp_bits = bits_of(nt)
    seq_stages = stages_of(SEQ, bits_of(nz))
    exp_stages = stages_of(EXP, bits_of(nx))
    far_stages, core_stages = stages_of(TP, tp_bits[:-1]), stages_of(TP, tp_bits[-1:])

    piece = spread(own, seq_stages)
    info_all = spread(info, seq_stages + exp_stages)
    left = spread(piece[..., :half], exp_stages + far_stages + core_stages)
    right = spread(piece[..., half:], far_stages + exp_stages + core_stages)
    left = left.reshape(2, nt // 2, nx, nz, rows, half)
    right = right.reshape(2, nx, nt // 2, nz, rows, half)
    info_all = info_all.reshape(nx, nz, 16, 256)

    where = jnp.stack([t, x * gate_up.shape[0]]).astype(jnp.int32)
    keep0, keep1, send0, send1 = experts_apply(
        offsets_of(tp_bits), where, info_all, left, right, jnp.swapaxes(gate_up, 1, 2), down_proj
    )

    def settle(kept, stages):
        for axis, bit in stages:
            count = kept.shape[0] // 2
            kept = kept[:count] + swap(kept[count:].astype(BF16), axis, bit).astype(F32)
        return kept

    def join(kept, sent):
        kept = kept.astype(F32) + swap(sent, *core_stages[0]).astype(F32)
        return kept.reshape(-1, rows, half)

    kept0 = settle(join(keep0, send0), far_stages[::-1] + exp_stages[::-1])
    kept1 = settle(join(keep1, send1), exp_stages[::-1] + far_stages[::-1])
    kept = settle(jnp.concatenate([kept0, kept1], axis=-1), seq_stages[::-1])
    routed_out = kept.reshape(rows, chunk).astype(BF16)
    order = [
        offsets_of(bits_of(nx)).index(i) * nz + offsets_of(bits_of(nz)).index(k)
        for k in range(nz)
        for i in range(nx)
    ]
    return routed_out, info_all.reshape(-1, 16, 256), order


def local(
    query_heads,
    key_heads,
    value_head_rows,
    state_input,
    state_gate,
    state_inflow,
    state_readout,
    step_size,
    log_decay,
    skip_scale,
    state_gain,
    hidden_in,
    mlp_gain,
    router_weight,
    expert_ids,
    slot_index,
    gate_up,
    down_proj,
):
    nz, nx, nt = lax.axis_size(SEQ), lax.axis_size(EXP), lax.axis_size(TP)
    z, x, t = lax.axis_index(SEQ), lax.axis_index(EXP), lax.axis_index(TP)
    _, width = hidden_in.shape
    chunk = width // nt
    seq_stages = stages_of(SEQ, bits_of(nz))
    exp_stages = stages_of(EXP, bits_of(nx))

    where = jnp.stack([t, x * gate_up.shape[0], z * nx + x]).astype(jnp.int32)
    own = norm_share(
        where,
        chunk,
        hidden_in,
        mlp_gain[None],
        router_weight.T,
        expert_ids.T,
        slot_index.T,
        log_decay.T,
    )
    flat = lambda a: a.reshape(-1, a.shape[2])
    heads = step_size.shape[1]
    inflow, readout = flat(state_inflow), flat(state_readout)
    intra, state, sent = state_local(state_input, inflow, readout, step_size.T, log_decay.T)
    kv = jnp.concatenate([flat(key_heads), flat(value_head_rows)], axis=0)
    finish_args = (
        intra,
        readout,
        log_decay.T,
        state_input,
        state_gate,
        jnp.repeat(skip_scale, HP)[None],
        state_gain[None],
    )

    if (nz, nx, nt) != (4, 2, 4):
        routed_out, info_all, order = routed_in_general(own, gate_up, down_proj)
        stages = seq_stages + exp_stages
        kv_own = spread(kv, stages[:-1])
        kv_parts = [a.reshape(-1, *kv.shape) for a in (kv_own, swap(kv_own, *stages[-1]))]
        far = [o * nx for o in offsets_of(bits_of(nz))]
        window_out = attention(
            query_heads, kv_parts, [i ^ o for i in offsets_of(bits_of(nx)) for o in far], where
        )
        entering, span = (), 1
        while span * 2 < nx * nz:
            other = lax.ppermute(sent, *span_route(span))
            *entering, state, sent = scan_step(
                order, span, heads, where, info_all, other, state, *entering
            )
            span *= 2
        other = lax.ppermute(sent, *span_route(span))
        state_out = state_finish(order, span, where, info_all, other, *entering, *finish_args)
        return window_out, state_out, routed_out

    return in_groups(
        where, own, kv, sent, state, query_heads, finish_args, gate_up, down_proj
    )


def in_groups(where, own, kv, sent, state, query_heads, finish_args, gate_up, down_proj):
    nz, nx = lax.axis_size(SEQ), lax.axis_size(EXP)
    heads = finish_args[2].shape[0]
    far, near, side, high, core = group_bits()
    order = [(k >> 1 << 2) | (i << 1) | (k & 1) for k in range(nz) for i in range(nx)]
    beyond = swap(own, SEQ, far)
    beside = swap(own, SEQ, near)
    here = jnp.stack([own, beside])
    kv_own = jnp.stack([kv, swap(kv, EXP, side)])
    kv_own = jnp.stack([kv_own, swap(kv_own, SEQ, far)])
    there = jnp.stack([beyond, swap(beyond, SEQ, near)])
    pieces_a = spread_near(here)
    pieces_b = spread_near(there)
    info_all = jnp.concatenate(
        [p[0][..., -16:, :256].reshape(-1, 16, 256) for p in (pieces_a, pieces_b)], axis=0
    )
    other = lax.ppermute(sent, *span_route(1))
    *entering, state, sent = scan_step(order, 1, heads, where, info_all, other, state)
    other2 = lax.ppermute(sent, *span_route(2))
    kv_other = swap(kv_own, SEQ, near)

    offsets = ((0, high), (core, core ^ high))
    keep_a, send_a, keep_b, send_b = experts_gather(
        offsets, where, pieces_a + pieces_b, gate_up, down_proj
    )

    kept_b = fold(keep_b.astype(F32), send_b, TP, core)
    kept_a = fold(keep_a.astype(F32), send_a, TP, core)
    *entering, state, sent = scan_step(order, 2, heads, where, info_all, other2, state, *entering)
    other4 = lax.ppermute(sent, *span_route(4))
    firsts, routed = [], []
    for name, kept in (("b", kept_b), ("a", kept_a)):
        left = fold(kept[0, 0], kept[0, 1], TP, high)
        right = fold(kept[1, 0], kept[1, 1], EXP, side)
        firsts.append((name, left, right))
    kv_parts = [a.reshape(-1, *kv.shape) for a in (kv_own, kv_other)]
    kv_offsets = [n * nx ^ f * nx ^ i for n in (0, near) for f in (0, far) for i in (0, side)]
    window_out = attention(query_heads, kv_parts, kv_offsets, where)
    state_out = state_finish(order, 4, where, info_all, other4, *entering, *finish_args)
    for name, left, right in firsts:
        left = fold(left[0], left[1], EXP, side)
        right = fold(right[0], right[1], TP, high)
        both = jnp.concatenate([left, right], axis=-1)
        routed.append(fold(both[0], both[1], SEQ, near))
    routed_out = fold(routed[1], routed[0], SEQ, far).astype(BF16)
    return window_out, state_out, routed_out


def solution(mesh):
    block = (SEQ, EXP)
    program = jax.shard_map(
        local,
        mesh=mesh,
        in_specs=(
            P(block, TP, None),
            P(block, TP, None),
            P(block, TP, None),
            P(block, TP),
            P(block, TP),
            P(block, TP, None),
            P(block, TP, None),
            P(block, TP),
            P(block, TP),
            P(TP),
            P(TP),
            P(block, None),
            P(),
            P(),
            P(block, None),
            P(block, None),
            P(EXP, (SEQ, TP), None, None),
            P(EXP, (SEQ, TP), None),
        ),
        out_specs=(P(block, TP, None), P(block, TP), P(block, TP)),
        check_vma=False,
    )
    if tuple(mesh.shape[a] for a in (SEQ, EXP, TP)) != (4, 2, 4):
        return program
    return program
```

time: 169 us -> 136 us (0.80)
  the two profiles are of different devices: /device:TPU:0 before, /device:TPU:24 now
where the time goes in v2:
time: 136 us
  waiting for transfers between devices  59.2 us (44%)
  Pallas kernels  36.7 us (27%)
  starting transfers between devices  33.5 us (25%)
  other arithmetic  4.5 us (3%)
    ppermute x35, waiting for transfers between devices, swap(): lax.ppermute(block, axis, [(i, i ^ bit) for i in range(lax.axis_size(axis...  47.8 us
    ppermute x35, starting transfers between devices, swap(): lax.ppermute(block, axis, [(i, i ^ bit) for i in range(lax.axis_size(axis...  29.7 us
    pallas_call x1, Pallas kernels, experts_gather(): pl.pallas_call(functools.partial(gather_kernel, offsets), out_shape=[resu...  17.5 us
    pallas_call x1, Pallas kernels, attention(): pl.pallas_call(functools.partial(attention_kernel, offsets), out_shape=ja...  8.52 us
    pallas_call x3, Pallas kernels, staged_call(): pl.pallas_call(kernel, out_shape=out_shape, in_specs=[smem] * len(scalars...  8.2 us
    ppermute x1, waiting for transfers between devices, in_groups(): other = lax.ppermute(sent, *span_route(1))  5.91 us
    ppermute x1, waiting for transfers between devices, in_groups(): other2 = lax.ppermute(sent, *span_route(2))  5.48 us
  transfers between devices with their start and end apart: 38, of which 20 were waited for; matrix products, arithmetic and copies ran while one was open for 3% of the time, Pallas kernels for 12%

profile of v2, /device:TPU:24, one launch (start us, length us, event | category | flops | bytes accessed | tf_op | source)
XLA Modules:
  0.0 135.8 jit_solution(7622777465939638045)
XLA Ops:
  0.6 0.1 pad_add_fusion.where_ref.refs_0_
  0.7 2.2 %shard_map.193 = bf16[144,512]{1,0:T(8,128)(2,1)S(1)} custom-call(s32[3]{0:T(128)S(1)} %pad_add_fusion.where_ref.refs_0_, bf16[128,2048]{1,0:T(8,128)(2,1)} %refs_1_.2, f32[1,2048]{1,0:T(1,128)} %bitcast.147, bf16[8,2048]{1,0:T(8,128)(2,1)} %bitcast.146, s32[2,128]{1,0:T(2,128)} %bitcast.150, s32[2,128]{1,0:T(2,128)} %bitcast.151, f32[16,128]{1,0:T(8,128)} %bitcast.140), custom_call_target="tpu_custom_call" | custom-call | tf_op jit(solution)/shard_map/pallas_call | solution.py:70
  2.9 0.5 collective-permute-start.3
  3.4 7.1 %collective-permute-done.3 = bf16[144,512]{1,0:T(8,128)(2,1)S(1)} collective-permute-done((bf16[144,512]{1,0:T(8,128)(2,1)S(1)}, bf16[144,512]{1,0:T(8,128)(2,1)S(1)}, u32[]{:S(2)}, u32[]{:S(2)}) %collective-permute-start.3) | collective-permute-done | bytes 147488 | tf_op jit(solution)/shard_map/ppermute | solution.py:28
  10.5 1.6 %collective-permute-start.14 = (bf16[2,128,256]{2,1,0:T(8,128)(2,1)S(1)}, bf16[2,128,256]{2,1,0:T(8,128)(2,1)S(1)}, u32[]{:S(2)}, u32[]{:S(2)}) collective-permute-start(bf16[2,128,256]{2,1,0:T(8,128)(2,1)S(1)} %pad_maximum_fusion.9), channel_id=1, source_target_pairs={{0,2},{1,3},{2,0},{3,1},{4,6},{5,7},{6,4},{7,5},{8,10},{9,11},{10,... | collective-permute-start | bytes 393224 | tf_op jit(solution)/shard_map/ppermute | solution.py:28
  12.1 0.7 collective-permute-done.5
  12.8 1.6 %collective-permute-start.4 = (bf16[2,144,256]{2,1,0:T(8,128)(2,1)S(1)}, bf16[2,144,256]{2,1,0:T(8,128)(2,1)S(1)}, u32[]{:S(2)}, u32[]{:S(2)}) collective-permute-start(bf16[2,144,256]{2,1,0:T(8,128)(2,1)S(1)} %fusion.20), channel_id=1, source_target_pairs={{0,4},{4,0},{1,5},{5,1},{2,6},{6,2},{3,7},{7,3},{8,12},{12,8},{9,1... | collective-permute-start | bytes 442376 | tf_op jit(solution)/shard_map/ppermute | solution.py:28
  14.4 1.1 collective-permute-done.14
  15.6 1.6 %collective-permute-start.15 = (bf16[2,2,128,256]{3,2,1,0:T(8,128)(2,1)S(1)}, bf16[2,2,128,256]{3,2,1,0:T(8,128)(2,1)S(1)}, u32[]{:S(2)}, u32[]{:S(2)}) collective-permute-start(bf16[2,2,128,256]{3,2,1,0:T(8,128)(2,1)S(1)} %pad_maximum_fusion.6.refs_7_), channel_id=1, source_target_pairs={{0,4},{4,0},{1,5},{5,1},{2,6},{6,2},{3,7},{7,3},{8,12},{12,8},{9,1... | collective-permute-start | bytes 786440 | tf_op jit(solution)/shard_map/ppermute | solution.py:28
  17.1 0.8 collective-permute-done.6
  18.0 1.6 %collective-permute-start.7 = (bf16[2,144,256]{2,1,0:T(8,128)(2,1)S(1)}, bf16[2,144,256]{2,1,0:T(8,128)(2,1)S(1)}, u32[]{:S(2)}, u32[]{:S(2)}) collective-permute-start(bf16[2,144,256]{2,1,0:T(8,128)(2,1)S(1)} %fusion.19), channel_id=1, source_target_pairs={{0,4},{4,0},{1,5},{5,1},{2,6},{6,2},{3,7},{7,3},{8,12},{12,8},{9,1... | collective-permute-start | bytes 442376 | tf_op jit(solution)/shard_map/ppermute | solution.py:28
  19.6 1.5 %collective-permute-start.21 = (bf16[2,128,256]{2,1,0:T(8,128)(2,1)S(1)}, bf16[2,128,256]{2,1,0:T(8,128)(2,1)S(1)}, u32[]{:S(2)}, u32[]{:S(2)}) collective-permute-start(bf16[2,128,256]{2,1,0:T(8,128)(2,1)S(1)} %pad_maximum_fusion.8), channel_id=1, source_target_pairs={{0,2},{1,3},{2,0},{3,1},{4,6},{5,7},{6,4},{7,5},{8,10},{9,11},{10,... | collective-permute-start | bytes 393224 | tf_op jit(solution)/shard_map/ppermute | solution.py:28
  21.2 0.6 collective-permute-start.11
  21.7 4.7 %collective-permute-done.7 = bf16[2,144,256]{2,1,0:T(8,128)(2,1)S(1)} collective-permute-done((bf16[2,144,256]{2,1,0:T(8,128)(2,1)S(1)}, bf16[2,144,256]{2,1,0:T(8,128)(2,1)S(1)}, u32[]{:S(2)}, u32[]{:S(2)}) %collective-permute-start.7) | collective-permute-done | bytes 147488 | tf_op jit(solution)/shard_map/ppermute | solution.py:28
  26.5 1.6 %collective-permute-start.18 = (bf16[2,2,144,256]{3,2,1,0:T(8,128)(2,1)S(1)}, bf16[2,2,144,256]{3,2,1,0:T(8,128)(2,1)S(1)}, u32[]{:S(2)}, u32[]{:S(2)}) collective-permute-start(bf16[2,2,144,256]{3,2,1,0:T(8,128)(2,1)S(1)} %pad_maximum_fusion.2.refs_11_), channel_id=1, source_target_pairs={{0,2},{1,3},{2,0},{3,1},{4,6},{5,7},{6,4},{7,5},{8,10},{9,11},{10,... | collective-permute-start | bytes 884744 | tf_op jit(solution)/shard_map/ppermute | solution.py:28
  28.1 1.6 %collective-permute-start.22 = (bf16[2,2,128,256]{3,2,1,0:T(8,128)(2,1)S(1)}, bf16[2,2,128,256]{3,2,1,0:T(8,128)(2,1)S(1)}, u32[]{:S(2)}, u32[]{:S(2)}) collective-permute-start(bf16[2,2,128,256]{3,2,1,0:T(8,128)(2,1)S(1)} %pad_maximum_fusion.7.refs_15_), channel_id=1, source_target_pairs={{0,4},{4,0},{1,5},{5,1},{2,6},{6,2},{3,7},{7,3},{8,12},{12,8},{9,1... | collective-permute-start | bytes 786440 | tf_op jit(solution)/shard_map/ppermute | solution.py:28
  29.7 0.1 collective-permute-done.11.refs_4_
  29.8 0.4 collective-permute-start.19
  30.2 0.1 collective-permute-start.13
  30.3 5.7 %collective-permute-done.18.refs_12_ = bf16[2,2,144,256]{3,2,1,0:T(8,128)(2,1)S(1)} collective-permute-done((bf16[2,2,144,256]{3,2,1,0:T(8,128)(2,1)S(1)}, bf16[2,2,144,256]{3,2,1,0:T(8,128)(2,1)S(1)}, u32[]{:S(2)}, u32[]{:S(2)}) %collective-permute-start.18) | collective-permute-done | bytes 294944 | tf_op jit(solution)/shard_map/ppermute | solution.py:28
  36.0 0.6 collective-permute-done.22.refs_16_
  36.6 0.5 collective-permute-start.24
  37.1 1.0 collective-permute-done.17.refs_10_
  38.2 0.4 collective-permute-done.24.refs_18_
  38.5 17.5 %experts.1 = (bf16[2,2,2,2,128,256]{5,4,3,2,1,0:T(8,128)(2,1)S(1)}, bf16[2,2,2,2,128,256]{5,4,3,2,1,0:T(8,128)(2,1)S(1)}, bf16[2,2,2,2,128,256]{5,4,3,2,1,0:T(8,...) custom-call(s32[3]{0:T(128)S(1)} %pad_add_fusion.where_ref.refs_0_, bf16[4,448,2,2048]{3,2,1,0:T(2,128)(2,1)} %refs_1_.3, ...), custom_call_target="tpu_custom_call" | custom-call | tf_op jit(solution)/shard_map/experts/pallas_call | solution.py:545
  56.1 0.2 collective-permute-start.25
  56.3 1.6 %collective-permute-start = (bf16[512,128]{1,0:T(8,128)(2,1)S(1)}, bf16[512,128]{1,0:T(8,128)(2,1)S(1)}, u32[]{:S(2)}, u32[]{:S(2)}) collective-permute-start(bf16[512,128]{1,0:T(8,128)(2,1)S(1)} %get-tuple-element.42), channel_id=1, source_target_pairs={{0,4},{4,0},{1,5},{5,1},{2,6},{6,2},{3,7},{7,3},{8,12},{12,8},{9,1... | collective-permute-start | bytes 393224 | tf_op jit(solution)/shard_map/ppermute | solution.py:28
  57.9 2.6 %shard_map.194 = (f32[128,1024]{1,0:T(8,128)S(1)}, f32[128,1024]{1,0:T(8,128)S(1)}, bf16[128,1024]{1,0:T(8,128)(2,1)S(1)}) custom-call(bf16[128,1024]{1,0:T(8,128)(2,1)} %refs_7_.1, bf16[256,128]{1,0:T(8,128)(2,1)} %bitcast.143, bf16[256,128]{1,0:T(8,128)(2,1)} %bitcast.131, f32[16,128]{1,0:T(8,128)} %bitcast.148, f32[16,128]{1,0:T(8,128)} %bitcast.141), custom_call_target="tpu_custom_call" | custom-call | tf_op jit(solution)/shard_map/pallas_call | solution.py:70
  60.5 0.6 collective-permute-start.8
  61.1 1.1 collective-permute-done
  62.2 0.7 collective-permute-start.1
  62.9 5.9 %collective-permute-done.8.other_ref = bf16[128,1024]{1,0:T(8,128)(2,1)S(1)} collective-permute-done((bf16[128,1024]{1,0:T(8,128)(2,1)S(1)}, bf16[128,1024]{1,0:T(8,128)(2,1)S(1)}, u32[]{:S(2)}, u32[]{:S(2)}) %collective-permute-start.8) | collective-permute-done | bytes 262176 | tf_op jit(solution)/shard_map/ppermute | solution.py:927
  68.8 0.8 shard_map.195
  69.6 1.8 %collective-permute-start.9 = (bf16[128,1024]{1,0:T(8,128)(2,1)S(1)}, bf16[128,1024]{1,0:T(8,128)(2,1)S(1)}, u32[]{:S(2)}, u32[]{:S(2)}) collective-permute-start(bf16[128,1024]{1,0:T(8,128)(2,1)S(1)} %get-tuple-element.17), channel_id=1, source_target_pairs={{0,8},{8,0},{16,24},{24,16},{1,9},{9,1},{17,25},{25,17},{2,10},{10... | collective-permute-start | bytes 786440 | tf_op jit(solution)/shard_map/ppermute | solution.py:929
  71.4 5.2 %collective-permute-done.1 = bf16[2,512,128]{2,1,0:T(8,128)(2,1)S(1)} collective-permute-done((bf16[2,512,128]{2,1,0:T(8,128)(2,1)S(1)}, bf16[2,512,128]{2,1,0:T(8,128)(2,1)S(1)}, u32[]{:S(2)}, u32[]{:S(2)}) %collective-permute-start.1) | collective-permute-done | bytes 262176 | tf_op jit(solution)/shard_map/ppermute | solution.py:28
  76.7 5.5 %collective-permute-done.9.other_ref = bf16[128,1024]{1,0:T(8,128)(2,1)S(1)} collective-permute-done((bf16[128,1024]{1,0:T(8,128)(2,1)S(1)}, bf16[128,1024]{1,0:T(8,128)(2,1)S(1)}, u32[]{:S(2)}, u32[]{:S(2)}) %collective-permute-start.9) | collective-permute-done | bytes 262176 | tf_op jit(solution)/shard_map/ppermute | solution.py:929
  82.2 1.6 %shard_map.196 = (f32[128,1024]{1,0:T(8,128)S(1)}, f32[128,1024]{1,0:T(8,128)}, bf16[128,1024]{1,0:T(8,128)(2,1)S(1)}) custom-call(s32[3]{0:T(128)S(1)} %pad_add_fusion.where_ref.refs_0_, bf16[8,16,256]{2,1,0:T(8,128)(2,1)S(1)} %pad_maximum_fusion.11.total_ref.refs_1_, bf16[128,1024]{1,0:T(8,128)(2,1)S(1)} %collective-permute-done.9.other_ref, ...), custom_call_target="tpu_custom_call" | custom-call | tf_op jit(solution)/shard_map/pallas_call | solution.py:722
  83.8 1.5 %collective-permute-start.10 = (bf16[128,1024]{1,0:T(8,128)(2,1)S(1)}, bf16[128,1024]{1,0:T(8,128)(2,1)S(1)}, u32[]{:S(2)}, u32[]{:S(2)}) collective-permute-start(bf16[128,1024]{1,0:T(8,128)(2,1)S(1)} %get-tuple-element.20), channel_id=1, source_target_pairs={{0,16},{8,24},{1,17},{9,25},{2,18},{10,26},{3,19},{11,27},{4,20},{... | collective-permute-start | bytes 786440 | tf_op jit(solution)/shard_map/ppermute | solution.py:940
  85.3 0.3 fusion.31
  85.7 0.9 collective-permute-start.28
  86.6 1.5 %collective-permute-start.26 = (bf16[2,2,128,256]{3,2,1,0:T(8,128)(2,1)S(1)}, bf16[2,2,128,256]{3,2,1,0:T(8,128)(2,1)S(1)}, u32[]{:S(2)}, u32[]{:S(2)}) collective-permute-start(bf16[2,2,128,256]{3,2,1,0:T(8,128)(2,1)S(1)} %get-tuple-element.38), channel_id=1, source_target_pairs={{0,2},{1,3},{2,0},{3,1},{4,6},{5,7},{6,4},{7,5},{8,10},{9,11},{10,... | collective-permute-start | bytes 786440 | tf_op jit(solution)/shard_map/ppermute | solution.py:28
  88.1 0.3 fusion.32
  88.5 1.2 collective-permute-start.34
  89.6 5.3 %collective-permute-done.28 = bf16[2,2,128,256]{3,2,1,0:T(8,128)(2,1)S(1)} collective-permute-done((bf16[2,2,128,256]{3,2,1,0:T(8,128)(2,1)S(1)}, bf16[2,2,128,256]{3,2,1,0:T(8,128)(2,1)S(1)}, u32[]{:S(2)}, u32[]{:S(2)}) %collective-permute-start.28) | collective-permute-done | bytes 262176 | tf_op jit(solution)/shard_map/ppermute | solution.py:28
  95.0 1.3 collective-permute-start.32
  96.3 0.1 fusion.2
  96.5 1.0 collective-permute-start.27
  97.5 2.0 %collective-permute-done.34 = bf16[2,2,128,256]{3,2,1,0:T(8,128)(2,1)S(1)} collective-permute-done((bf16[2,2,128,256]{3,2,1,0:T(8,128)(2,1)S(1)}, bf16[2,2,128,256]{3,2,1,0:T(8,128)(2,1)S(1)}, u32[]{:S(2)}, u32[]{:S(2)}) %collective-permute-start.34) | collective-permute-done | bytes 262176 | tf_op jit(solution)/shard_map/ppermute | solution.py:28
  99.5 2.1 %collective-permute-start.29 = (bf16[2,128,256]{2,1,0:T(8,128)(2,1)S(1)}, bf16[2,128,256]{2,1,0:T(8,128)(2,1)S(1)}, u32[]{:S(2)}, u32[]{:S(2)}) collective-permute-start(bf16[2,128,256]{2,1,0:T(8,128)(2,1)S(1)} %fusion.22), channel_id=1, source_target_pairs={{0,2},{1,3},{2,0},{3,1},{4,6},{5,7},{6,4},{7,5},{8,10},{9,11},{10,... | collective-permute-start | bytes 393224 | tf_op jit(solution)/shard_map/ppermute | solution.py:28
  101.6 0.9 collective-permute-done.32
  102.4 0.1 fusion
  102.6 0.3 collective-permute-start.33
  103.0 4.7 %collective-permute-done.33 = bf16[2,128,256]{2,1,0:T(8,128)(2,1)S(1)} collective-permute-done((bf16[2,128,256]{2,1,0:T(8,128)(2,1)S(1)}, bf16[2,128,256]{2,1,0:T(8,128)(2,1)S(1)}, u32[]{:S(2)}, u32[]{:S(2)}) %collective-permute-start.33) | collective-permute-done | bytes 131104 | tf_op jit(solution)/shard_map/ppermute | solution.py:28
  107.6 1.5 %collective-permute-start.35 = (bf16[2,128,256]{2,1,0:T(8,128)(2,1)S(1)}, bf16[2,128,256]{2,1,0:T(8,128)(2,1)S(1)}, u32[]{:S(2)}, u32[]{:S(2)}) collective-permute-start(bf16[2,128,256]{2,1,0:T(8,128)(2,1)S(1)} %fusion.25), channel_id=1, source_target_pairs={{0,2},{1,3},{2,0},{3,1},{4,6},{5,7},{6,4},{7,5},{8,10},{9,11},{10,... | collective-permute-start | bytes 393224 | tf_op jit(solution)/shard_map/ppermute | solution.py:28
  109.2 3.4 %collective-permute-done.35 = bf16[2,128,256]{2,1,0:T(8,128)(2,1)S(1)} collective-permute-done((bf16[2,128,256]{2,1,0:T(8,128)(2,1)S(1)}, bf16[2,128,256]{2,1,0:T(8,128)(2,1)S(1)}, u32[]{:S(2)}, u32[]{:S(2)}) %collective-permute-start.35) | collective-permute-done | bytes 131104 | tf_op jit(solution)/shard_map/ppermute | solution.py:28
  112.8 0.7 fusion.23
  113.5 2.0 %collective-permute-start.30 = (bf16[128,512]{1,0:T(8,128)(2,1)}, bf16[128,512]{1,0:T(8,128)(2,1)}, u32[]{:S(2)}, u32[]{:S(2)}) collective-permute-start(bf16[128,512]{1,0:T(8,128)(2,1)} %fusion.23), channel_id=1, source_target_pairs={{0,8},{8,0},{16,24},{24,16},{1,9},{9,1},{17,25},{25,17},{2,10},{10... | collective-permute-start | bytes 393224 | tf_op jit(solution)/shard_map/ppermute | solution.py:28
  115.5 2.9 %collective-permute-done.36 = bf16[128,512]{1,0:T(8,128)(2,1)S(1)} collective-permute-done((bf16[128,512]{1,0:T(8,128)(2,1)S(1)}, bf16[128,512]{1,0:T(8,128)(2,1)S(1)}, u32[]{:S(2)}, u32[]{:S(2)}) %collective-permute-start.36) | collective-permute-done | bytes 131104 | tf_op jit(solution)/shard_map/ppermute | solution.py:28
  118.4 0.7 fusion.7
  119.1 2.3 %collective-permute-start.37 = (bf16[128,512]{1,0:T(8,128)(2,1)}, bf16[128,512]{1,0:T(8,128)(2,1)}, u32[]{:S(2)}, u32[]{:S(2)}) collective-permute-start(bf16[128,512]{1,0:T(8,128)(2,1)} %fusion.7), channel_id=1, source_target_pairs={{0,16},{8,24},{16,0},{24,8},{1,17},{9,25},{17,1},{25,9},{2,18},{10... | collective-permute-start | bytes 393224 | tf_op jit(solution)/shard_map/ppermute | solution.py:28
  121.4 0.7 broadcast_in_dim_reshape.3.refs_9_
  122.1 8.5 %attention.1 = bf16[1024,128]{1,0:T(8,128)(2,1)} custom-call(s32[3]{0:T(128)S(1)} %pad_add_fusion.where_ref.refs_0_, bf16[1024,128]{1,0:T(8,128)(2,1)S(1)} %bitcast.114, bf16[4,512,128]{2,1,0:T(8,128)(2,1)S(1)} %bitcast.112, bf16[4,512,128]{2,1,0:T(8,128)(2,1)S(1)} %bitcast.113), custom_call_target="tpu_custom_call" | custom-call | tf_op jit(solution)/shard_map/attention/pallas_call | solution.py:159
  130.6 3.5 %shard_map.197 = bf16[128,1024]{1,0:T(8,128)(2,1)} custom-call(s32[3]{0:T(128)S(1)} %pad_add_fusion.where_ref.refs_0_, bf16[8,16,256]{2,1,0:T(8,128)(2,1)S(1)} %pad_maximum_fusion.11.total_ref.refs_1_, bf16[128,1024]{1,0:T(8,128)(2,1)S(1)} %collective-permute-done.10.refs_2_, f32[128,1024]{1,0:T(8,128)S(1)} %get-tuple-element.21.refs_3_, ...), custom_call_target="tpu_custom_call" | custom-call | tf_op jit(solution)/shard_map/pallas_call | solution.py:70
  134.1 1.7 %fusion.12 = bf16[128,512]{1,0:T(8,128)(2,1)} fusion(f32[2,128,256]{2,1,0:T(8,128)S(1)} %fusion.18, f32[2,128,256]{2,1,0:T(8,128)S(1)} %fusion.17, bf16[128,512]{1,0:T(8,128)(2,1)} %collective-permute-done.37, bf16[128,512]{1,0:T(8,128)(2,1)} %collective-permute-done.30), kind=kLoop, calls=%fused_computation.33 | loop fusion | flops 393216 | bytes 917504 | tf_op jit(solution)/shard_map/convert_element_type | solution.py:955
  (66 shorter events, 0.9 us)
Async XLA Ops:
  2.9 7.6 %collective-permute-start.3 = (bf16[144,512]{1,0:T(8,128)(2,1)S(1)}, bf16[144,512]{1,0:T(8,128)(2,1)S(1)}, u32[]{:S(2)}, u32[]{:S(2)}) collective-permute-start(bf16[144,512]{1,0:T(8,128)(2,1)S(1)} %shard_map.193), channel_id=1, source_target_pairs={{0,8},{8,0},{16,24},{24,16},{1,9},{9,1},{17,25},{25,17},{2,10},{10... | collective-permute-start | bytes 442376 | tf_op jit(solution)/shard_map/ppermute | solution.py:28
  3.4 9.4 %collective-permute-start.5 = (bf16[144,512]{1,0:T(8,128)(2,1)S(1)}, bf16[144,512]{1,0:T(8,128)(2,1)S(1)}, u32[]{:S(2)}, u32[]{:S(2)}) collective-permute-start(bf16[144,512]{1,0:T(8,128)(2,1)S(1)} %shard_map.193), channel_id=1, source_target_pairs={{0,16},{8,24},{16,0},{24,8},{1,17},{9,25},{17,1},{25,9},{2,18},{10... | collective-permute-start | bytes 442376 | tf_op jit(solution)/shard_map/ppermute | solution.py:28
  10.5 5.0 %collective-permute-start.14 = (bf16[2,128,256]{2,1,0:T(8,128)(2,1)S(1)}, bf16[2,128,256]{2,1,0:T(8,128)(2,1)S(1)}, u32[]{:S(2)}, u32[]{:S(2)}) collective-permute-start(bf16[2,128,256]{2,1,0:T(8,128)(2,1)S(1)} %pad_maximum_fusion.9), channel_id=1, source_target_pairs={{0,2},{1,3},{2,0},{3,1},{4,6},{5,7},{6,4},{7,5},{8,10},{9,11},{10,... | collective-permute-start | bytes 393224 | tf_op jit(solution)/shard_map/ppermute | solution.py:28
  12.8 5.1 %collective-permute-start.6 = (bf16[144,512]{1,0:T(8,128)(2,1)S(1)}, bf16[144,512]{1,0:T(8,128)(2,1)S(1)}, u32[]{:S(2)}, u32[]{:S(2)}) collective-permute-start(bf16[144,512]{1,0:T(8,128)(2,1)S(1)} %collective-permute-done.5), channel_id=1, source_target_pairs={{0,8},{8,0},{16,24},{24,16},{1,9},{9,1},{17,25},{25,17},{2,10},{10... | collective-permute-start | bytes 442376 | tf_op jit(solution)/shard_map/ppermute | solution.py:28
  12.8 8.3 %collective-permute-start.4 = (bf16[2,144,256]{2,1,0:T(8,128)(2,1)S(1)}, bf16[2,144,256]{2,1,0:T(8,128)(2,1)S(1)}, u32[]{:S(2)}, u32[]{:S(2)}) collective-permute-start(bf16[2,144,256]{2,1,0:T(8,128)(2,1)S(1)} %fusion.20), channel_id=1, source_target_pairs={{0,4},{4,0},{1,5},{5,1},{2,6},{6,2},{3,7},{7,3},{8,12},{12,8},{9,1... | collective-permute-start | bytes 442376 | tf_op jit(solution)/shard_map/ppermute | solution.py:28
  15.6 12.5 %collective-permute-start.15 = (bf16[2,2,128,256]{3,2,1,0:T(8,128)(2,1)S(1)}, bf16[2,2,128,256]{3,2,1,0:T(8,128)(2,1)S(1)}, u32[]{:S(2)}, u32[]{:S(2)}) collective-permute-start(bf16[2,2,128,256]{3,2,1,0:T(8,128)(2,1)S(1)} %pad_maximum_fusion.6.refs_7_), channel_id=1, source_target_pairs={{0,4},{4,0},{1,5},{5,1},{2,6},{6,2},{3,7},{7,3},{8,12},{12,8},{9,1... | collective-permute-start | bytes 786440 | tf_op jit(solution)/shard_map/ppermute | solution.py:28
  17.1 12.6 %collective-permute-start.16 = (bf16[2,2,128,256]{3,2,1,0:T(8,128)(2,1)S(1)}, bf16[2,2,128,256]{3,2,1,0:T(8,128)(2,1)S(1)}, u32[]{:S(2)}, u32[]{:S(2)}) collective-permute-start(bf16[2,2,128,256]{3,2,1,0:T(8,128)(2,1)S(1)} %pad_maximum_fusion.6.refs_7_), channel_id=1, source_target_pairs={{0,1},{1,0},{2,3},{3,2},{4,5},{5,4},{6,7},{7,6},{8,9},{9,8},{10,11... | collective-permute-start | bytes 786440 | tf_op jit(solution)/shard_map/ppermute | solution.py:28
  18.0 8.4 %collective-permute-start.7 = (bf16[2,144,256]{2,1,0:T(8,128)(2,1)S(1)}, bf16[2,144,256]{2,1,0:T(8,128)(2,1)S(1)}, u32[]{:S(2)}, u32[]{:S(2)}) collective-permute-start(bf16[2,144,256]{2,1,0:T(8,128)(2,1)S(1)} %fusion.19), channel_id=1, source_target_pairs={{0,4},{4,0},{1,5},{5,1},{2,6},{6,2},{3,7},{7,3},{8,12},{12,8},{9,1... | collective-permute-start | bytes 442376 | tf_op jit(solution)/shard_map/ppermute | solution.py:28
  19.6 6.9 %collective-permute-start.21 = (bf16[2,128,256]{2,1,0:T(8,128)(2,1)S(1)}, bf16[2,128,256]{2,1,0:T(8,128)(2,1)S(1)}, u32[]{:S(2)}, u32[]{:S(2)}) collective-permute-start(bf16[2,128,256]{2,1,0:T(8,128)(2,1)S(1)} %pad_maximum_fusion.8), channel_id=1, source_target_pairs={{0,2},{1,3},{2,0},{3,1},{4,6},{5,7},{6,4},{7,5},{8,10},{9,11},{10,... | collective-permute-start | bytes 393224 | tf_op jit(solution)/shard_map/ppermute | solution.py:28
  21.2 8.6 %collective-permute-start.11 = (bf16[2,2,144,256]{3,2,1,0:T(8,128)(2,1)S(1)}, bf16[2,2,144,256]{3,2,1,0:T(8,128)(2,1)S(1)}, u32[]{:S(2)}, u32[]{:S(2)}) collective-permute-start(bf16[2,2,144,256]{3,2,1,0:T(8,128)(2,1)S(1)} %pad_maximum_fusion.1.refs_3_), channel_id=1, source_target_pairs={{0,2},{1,3},{2,0},{3,1},{4,6},{5,7},{6,4},{7,5},{8,10},{9,11},{10,... | collective-permute-start | bytes 884744 | tf_op jit(solution)/shard_map/ppermute | solution.py:28
  26.4 3.8 %collective-permute-start.12 = (bf16[2,2,144,256]{3,2,1,0:T(8,128)(2,1)S(1)}, bf16[2,2,144,256]{3,2,1,0:T(8,128)(2,1)S(1)}, u32[]{:S(2)}, u32[]{:S(2)}) collective-permute-start(bf16[2,2,144,256]{3,2,1,0:T(8,128)(2,1)S(1)} %pad_maximum_fusion.1.refs_3_), channel_id=1, source_target_pairs={{0,1},{1,0},{2,3},{3,2},{4,5},{5,4},{6,7},{7,6},{8,9},{9,8},{10,11... | collective-permute-start | bytes 884744 | tf_op jit(solution)/shard_map/ppermute | solution.py:28
  26.5 9.6 %collective-permute-start.18 = (bf16[2,2,144,256]{3,2,1,0:T(8,128)(2,1)S(1)}, bf16[2,2,144,256]{3,2,1,0:T(8,128)(2,1)S(1)}, u32[]{:S(2)}, u32[]{:S(2)}) collective-permute-start(bf16[2,2,144,256]{3,2,1,0:T(8,128)(2,1)S(1)} %pad_maximum_fusion.2.refs_11_), channel_id=1, source_target_pairs={{0,2},{1,3},{2,0},{3,1},{4,6},{5,7},{6,4},{7,5},{8,10},{9,11},{10,... | collective-permute-start | bytes 884744 | tf_op jit(solution)/shard_map/ppermute | solution.py:28
  28.1 28.2 %copy-start.1 = (bf16[128,2,128]{2,1,0:T(2,128)(2,1)S(1)}, bf16[128,2,128]{2,1,0:T(2,128)(2,1)}, u32[]{:S(2)}) copy-start(bf16[128,2,128]{2,1,0:T(2,128)(2,1)} %param.20) | copy-start | bytes 196612
  28.1 28.2 %copy-start.2 = (bf16[128,2,128]{2,1,0:T(2,128)(2,1)S(1)}, bf16[128,2,128]{2,1,0:T(2,128)(2,1)}, u32[]{:S(2)}) copy-start(bf16[128,2,128]{2,1,0:T(2,128)(2,1)} %param.19) | copy-start | bytes 196612
  28.1 8.5 %collective-permute-start.22 = (bf16[2,2,128,256]{3,2,1,0:T(8,128)(2,1)S(1)}, bf16[2,2,128,256]{3,2,1,0:T(8,128)(2,1)S(1)}, u32[]{:S(2)}, u32[]{:S(2)}) collective-permute-start(bf16[2,2,128,256]{3,2,1,0:T(8,128)(2,1)S(1)} %pad_maximum_fusion.7.refs_15_), channel_id=1, source_target_pairs={{0,4},{4,0},{1,5},{5,1},{2,6},{6,2},{3,7},{7,3},{8,12},{12,8},{9,1... | collective-permute-start | bytes 786440 | tf_op jit(solution)/shard_map/ppermute | solution.py:28
  29.7 6.9 %collective-permute-start.23 = (bf16[2,2,128,256]{3,2,1,0:T(8,128)(2,1)S(1)}, bf16[2,2,128,256]{3,2,1,0:T(8,128)(2,1)S(1)}, u32[]{:S(2)}, u32[]{:S(2)}) collective-permute-start(bf16[2,2,128,256]{3,2,1,0:T(8,128)(2,1)S(1)} %pad_maximum_fusion.7.refs_15_), channel_id=1, source_target_pairs={{0,1},{1,0},{2,3},{3,2},{4,5},{5,4},{6,7},{7,6},{8,9},{9,8},{10,11... | collective-permute-start | bytes 786440 | tf_op jit(solution)/shard_map/ppermute | solution.py:28
  29.8 7.3 %collective-permute-start.19 = (bf16[2,2,144,256]{3,2,1,0:T(8,128)(2,1)S(1)}, bf16[2,2,144,256]{3,2,1,0:T(8,128)(2,1)S(1)}, u32[]{:S(2)}, u32[]{:S(2)}) collective-permute-start(bf16[2,2,144,256]{3,2,1,0:T(8,128)(2,1)S(1)} %pad_maximum_fusion.2.refs_11_), channel_id=1, source_target_pairs={{0,1},{1,0},{2,3},{3,2},{4,5},{5,4},{6,7},{7,6},{8,9},{9,8},{10,11... | collective-permute-start | bytes 884744 | tf_op jit(solution)/shard_map/ppermute | solution.py:28
  30.2 8.0 %collective-permute-start.13 = (bf16[2,2,144,256]{3,2,1,0:T(8,128)(2,1)S(1)}, bf16[2,2,144,256]{3,2,1,0:T(8,128)(2,1)S(1)}, u32[]{:S(2)}, u32[]{:S(2)}) collective-permute-start(bf16[2,2,144,256]{3,2,1,0:T(8,128)(2,1)S(1)} %collective-permute-done.11.refs_4_), channel_id=1, source_target_pairs={{0,1},{1,0},{2,3},{3,2},{4,5},{5,4},{6,7},{7,6},{8,9},{9,8},{10,11... | collective-permute-start | bytes 884744 | tf_op jit(solution)/shard_map/ppermute | solution.py:28
  36.0 2.5 %collective-permute-start.20 = (bf16[2,2,144,256]{3,2,1,0:T(8,128)(2,1)S(1)}, bf16[2,2,144,256]{3,2,1,0:T(8,128)(2,1)S(1)}, u32[]{:S(2)}, u32[]{:S(2)}) collective-permute-start(bf16[2,2,144,256]{3,2,1,0:T(8,128)(2,1)S(1)} %collective-permute-done.18.refs_12_), channel_id=1, source_target_pairs={{0,1},{1,0},{2,3},{3,2},{4,5},{5,4},{6,7},{7,6},{8,9},{9,8},{10,11... | collective-permute-start | bytes 884744 | tf_op jit(solution)/shard_map/ppermute | solution.py:28
  36.6 1.5 %collective-permute-start.17 = (bf16[2,2,128,256]{3,2,1,0:T(8,128)(2,1)S(1)}, bf16[2,2,128,256]{3,2,1,0:T(8,128)(2,1)S(1)}, u32[]{:S(2)}, u32[]{:S(2)}) collective-permute-start(bf16[2,2,128,256]{3,2,1,0:T(8,128)(2,1)S(1)} %collective-permute-done.15.refs_8_), channel_id=1, source_target_pairs={{0,1},{1,0},{2,3},{3,2},{4,5},{5,4},{6,7},{7,6},{8,9},{9,8},{10,11... | collective-permute-start | bytes 786440 | tf_op jit(solution)/shard_map/ppermute | solution.py:28
  36.6 1.9 %collective-permute-start.24 = (bf16[2,2,128,256]{3,2,1,0:T(8,128)(2,1)S(1)}, bf16[2,2,128,256]{3,2,1,0:T(8,128)(2,1)S(1)}, u32[]{:S(2)}, u32[]{:S(2)}) collective-permute-start(bf16[2,2,128,256]{3,2,1,0:T(8,128)(2,1)S(1)} %collective-permute-done.22.refs_16_), channel_id=1, source_target_pairs={{0,1},{1,0},{2,3},{3,2},{4,5},{5,4},{6,7},{7,6},{8,9},{9,8},{10,11... | collective-permute-start | bytes 786440 | tf_op jit(solution)/shard_map/ppermute | solution.py:28
  56.1 29.2 %collective-permute-start.25 = (bf16[2,2,2,2,128,256]{5,4,3,2,1,0:T(8,128)(2,1)S(1)}, bf16[2,2,2,2,128,256]{5,4,3,2,1,0:T(8,128)(2,1)S(1)}, u32[]{:S(2)}, u32[]{:S(2)}) collective-permute-start(bf16[2,2,2,2,128,256]{5,4,3,2,1,0:T(8,128)(2,1)S(1)} %get-tuple-element.24), channel_id=1, source_target_pairs={{0,1},{1,0},{2,3},{3,2},{4,5},{5,4},{6,7},{7,6},{8,9},{9,8},{10,11... | collective-permute-start | bytes 3145736 | tf_op jit(solution)/shard_map/ppermute | solution.py:28
  56.3 5.8 %collective-permute-start = (bf16[512,128]{1,0:T(8,128)(2,1)S(1)}, bf16[512,128]{1,0:T(8,128)(2,1)S(1)}, u32[]{:S(2)}, u32[]{:S(2)}) collective-permute-start(bf16[512,128]{1,0:T(8,128)(2,1)S(1)} %get-tuple-element.42), channel_id=1, source_target_pairs={{0,4},{4,0},{1,5},{5,1},{2,6},{6,2},{3,7},{7,3},{8,12},{12,8},{9,1... | collective-permute-start | bytes 393224 | tf_op jit(solution)/shard_map/ppermute | solution.py:28
  60.5 8.4 %collective-permute-start.8 = (bf16[128,1024]{1,0:T(8,128)(2,1)S(1)}, bf16[128,1024]{1,0:T(8,128)(2,1)S(1)}, u32[]{:S(2)}, u32[]{:S(2)}) collective-permute-start(bf16[128,1024]{1,0:T(8,128)(2,1)S(1)} %get-tuple-element.15), channel_id=1, source_target_pairs={{0,4},{4,0},{1,5},{5,1},{2,6},{6,2},{3,7},{7,3},{8,12},{12,8},{9,1... | collective-permute-start | bytes 786440 | tf_op jit(solution)/shard_map/ppermute | solution.py:927
  62.2 14.4 %collective-permute-start.1 = (bf16[2,512,128]{2,1,0:T(8,128)(2,1)S(1)}, bf16[2,512,128]{2,1,0:T(8,128)(2,1)S(1)}, u32[]{:S(2)}, u32[]{:S(2)}) collective-permute-start(bf16[2,512,128]{2,1,0:T(8,128)(2,1)S(1)} %get-tuple-element.40), channel_id=1, source_target_pairs={{0,16},{8,24},{16,0},{24,8},{1,17},{9,25},{17,1},{25,9},{2,18},{10... | collective-permute-start | bytes 786440 | tf_op jit(solution)/shard_map/ppermute | solution.py:28
  62.9 25.2 %collective-permute-start.31 = (bf16[2,2,2,2,128,256]{5,4,3,2,1,0:T(8,128)(2,1)S(1)}, bf16[2,2,2,2,128,256]{5,4,3,2,1,0:T(8,128)(2,1)S(1)}, u32[]{:S(2)}, u32[]{:S(2)}) collective-permute-start(bf16[2,2,2,2,128,256]{5,4,3,2,1,0:T(8,128)(2,1)S(1)} %get-tuple-element.26), channel_id=1, source_target_pairs={{0,1},{1,0},{2,3},{3,2},{4,5},{5,4},{6,7},{7,6},{8,9},{9,8},{10,11... | collective-permute-start | bytes 3145736 | tf_op jit(solution)/shard_map/ppermute | solution.py:28
  69.6 12.6 %collective-permute-start.9 = (bf16[128,1024]{1,0:T(8,128)(2,1)S(1)}, bf16[128,1024]{1,0:T(8,128)(2,1)S(1)}, u32[]{:S(2)}, u32[]{:S(2)}) collective-permute-start(bf16[128,1024]{1,0:T(8,128)(2,1)S(1)} %get-tuple-element.17), channel_id=1, source_target_pairs={{0,8},{8,0},{16,24},{24,16},{1,9},{9,1},{17,25},{25,17},{2,10},{10... | collective-permute-start | bytes 786440 | tf_op jit(solution)/shard_map/ppermute | solution.py:929
  76.7 45.5 %collective-permute-start.2 = (bf16[2,2,512,128]{3,2,1,0:T(8,128)(2,1)S(1)}, bf16[2,2,512,128]{3,2,1,0:T(8,128)(2,1)S(1)}, u32[]{:S(2)}, u32[]{:S(2)}) collective-permute-start(bf16[2,2,512,128]{3,2,1,0:T(8,128)(2,1)S(1)} %pad_maximum_fusion), channel_id=1, source_target_pairs={{0,8},{8,0},{16,24},{24,16},{1,9},{9,1},{17,25},{25,17},{2,10},{10... | collective-permute-start | bytes 1572872 | tf_op jit(solution)/shard_map/ppermute | solution.py:28
  83.8 46.8 %collective-permute-start.10 = (bf16[128,1024]{1,0:T(8,128)(2,1)S(1)}, bf16[128,1024]{1,0:T(8,128)(2,1)S(1)}, u32[]{:S(2)}, u32[]{:S(2)}) collective-permute-start(bf16[128,1024]{1,0:T(8,128)(2,1)S(1)} %get-tuple-element.20), channel_id=1, source_target_pairs={{0,16},{8,24},{1,17},{9,25},{2,18},{10,26},{3,19},{11,27},{4,20},{... | collective-permute-start | bytes 786440 | tf_op jit(solution)/shard_map/ppermute | solution.py:940
  85.7 9.2 %collective-permute-start.28 = (bf16[2,2,128,256]{3,2,1,0:T(8,128)(2,1)S(1)}, bf16[2,2,128,256]{3,2,1,0:T(8,128)(2,1)S(1)}, u32[]{:S(2)}, u32[]{:S(2)}) collective-permute-start(bf16[2,2,128,256]{3,2,1,0:T(8,128)(2,1)S(1)} %get-tuple-element.37), channel_id=1, source_target_pairs={{0,4},{4,0},{1,5},{5,1},{2,6},{6,2},{3,7},{7,3},{8,12},{12,8},{9,1... | collective-permute-start | bytes 786440 | tf_op jit(solution)/shard_map/ppermute | solution.py:28
  86.6 9.7 %collective-permute-start.26 = (bf16[2,2,128,256]{3,2,1,0:T(8,128)(2,1)S(1)}, bf16[2,2,128,256]{3,2,1,0:T(8,128)(2,1)S(1)}, u32[]{:S(2)}, u32[]{:S(2)}) collective-permute-start(bf16[2,2,128,256]{3,2,1,0:T(8,128)(2,1)S(1)} %get-tuple-element.38), channel_id=1, source_target_pairs={{0,2},{1,3},{2,0},{3,1},{4,6},{5,7},{6,4},{7,5},{8,10},{9,11},{10,... | collective-permute-start | bytes 786440 | tf_op jit(solution)/shard_map/ppermute | solution.py:28
  88.5 11.0 %collective-permute-start.34 = (bf16[2,2,128,256]{3,2,1,0:T(8,128)(2,1)S(1)}, bf16[2,2,128,256]{3,2,1,0:T(8,128)(2,1)S(1)}, u32[]{:S(2)}, u32[]{:S(2)}) collective-permute-start(bf16[2,2,128,256]{3,2,1,0:T(8,128)(2,1)S(1)} %get-tuple-element.35), channel_id=1, source_target_pairs={{0,4},{4,0},{1,5},{5,1},{2,6},{6,2},{3,7},{7,3},{8,12},{12,8},{9,1... | collective-permute-start | bytes 786440 | tf_op jit(solution)/shard_map/ppermute | solution.py:28
  95.0 7.5 %collective-permute-start.32 = (bf16[2,2,128,256]{3,2,1,0:T(8,128)(2,1)S(1)}, bf16[2,2,128,256]{3,2,1,0:T(8,128)(2,1)S(1)}, u32[]{:S(2)}, u32[]{:S(2)}) collective-permute-start(bf16[2,2,128,256]{3,2,1,0:T(8,128)(2,1)S(1)} %get-tuple-element.36), channel_id=1, source_target_pairs={{0,2},{1,3},{2,0},{3,1},{4,6},{5,7},{6,4},{7,5},{8,10},{9,11},{10,... | collective-permute-start | bytes 786440 | tf_op jit(solution)/shard_map/ppermute | solution.py:28
  96.5 16.3 %collective-permute-start.27 = (bf16[2,128,256]{2,1,0:T(8,128)(2,1)S(1)}, bf16[2,128,256]{2,1,0:T(8,128)(2,1)S(1)}, u32[]{:S(2)}, u32[]{:S(2)}) collective-permute-start(bf16[2,128,256]{2,1,0:T(8,128)(2,1)S(1)} %fusion.21), channel_id=1, source_target_pairs={{0,4},{4,0},{1,5},{5,1},{2,6},{6,2},{3,7},{7,3},{8,12},{12,8},{9,1... | collective-permute-start | bytes 393224 | tf_op jit(solution)/shard_map/ppermute | solution.py:28
  99.5 13.3 %collective-permute-start.29 = (bf16[2,128,256]{2,1,0:T(8,128)(2,1)S(1)}, bf16[2,128,256]{2,1,0:T(8,128)(2,1)S(1)}, u32[]{:S(2)}, u32[]{:S(2)}) collective-permute-start(bf16[2,128,256]{2,1,0:T(8,128)(2,1)S(1)} %fusion.22), channel_id=1, source_target_pairs={{0,2},{1,3},{2,0},{3,1},{4,6},{5,7},{6,4},{7,5},{8,10},{9,11},{10,... | collective-permute-start | bytes 393224 | tf_op jit(solution)/shard_map/ppermute | solution.py:28
  102.6 5.0 %collective-permute-start.33 = (bf16[2,128,256]{2,1,0:T(8,128)(2,1)S(1)}, bf16[2,128,256]{2,1,0:T(8,128)(2,1)S(1)}, u32[]{:S(2)}, u32[]{:S(2)}) collective-permute-start(bf16[2,128,256]{2,1,0:T(8,128)(2,1)S(1)} %fusion.24), channel_id=1, source_target_pairs={{0,4},{4,0},{1,5},{5,1},{2,6},{6,2},{3,7},{7,3},{8,12},{12,8},{9,1... | collective-permute-start | bytes 393224 | tf_op jit(solution)/shard_map/ppermute | solution.py:28
  107.6 5.0 %collective-permute-start.35 = (bf16[2,128,256]{2,1,0:T(8,128)(2,1)S(1)}, bf16[2,128,256]{2,1,0:T(8,128)(2,1)S(1)}, u32[]{:S(2)}, u32[]{:S(2)}) collective-permute-start(bf16[2,128,256]{2,1,0:T(8,128)(2,1)S(1)} %fusion.25), channel_id=1, source_target_pairs={{0,2},{1,3},{2,0},{3,1},{4,6},{5,7},{6,4},{7,5},{8,10},{9,11},{10,... | collective-permute-start | bytes 393224 | tf_op jit(solution)/shard_map/ppermute | solution.py:28
  109.2 12.2 %copy-start.3 = (f32[16]{0:T(128)S(1)}, f32[16]{0:T(128)}, u32[]{:S(2)}) copy-start(f32[16]{0:T(128)} %param.27) | copy-start | bytes 196
  109.2 12.9 %copy-start = (bf16[128,8,128]{2,1,0:T(8,128)(2,1)S(1)}, bf16[128,8,128]{2,1,0:T(8,128)(2,1)}, u32[]{:S(2)}) copy-start(bf16[128,8,128]{2,1,0:T(8,128)(2,1)} %param.18) | copy-start | bytes 786436
  112.7 5.7 %collective-permute-start.36 = (bf16[128,512]{1,0:T(8,128)(2,1)S(1)}, bf16[128,512]{1,0:T(8,128)(2,1)S(1)}, u32[]{:S(2)}, u32[]{:S(2)}) collective-permute-start(bf16[128,512]{1,0:T(8,128)(2,1)S(1)} %fusion.26), channel_id=1, source_target_pairs={{0,8},{8,0},{16,24},{24,16},{1,9},{9,1},{17,25},{25,17},{2,10},{10... | collective-permute-start | bytes 393224 | tf_op jit(solution)/shard_map/ppermute | solution.py:28
  113.5 20.6 %collective-permute-start.30 = (bf16[128,512]{1,0:T(8,128)(2,1)}, bf16[128,512]{1,0:T(8,128)(2,1)}, u32[]{:S(2)}, u32[]{:S(2)}) collective-permute-start(bf16[128,512]{1,0:T(8,128)(2,1)} %fusion.23), channel_id=1, source_target_pairs={{0,8},{8,0},{16,24},{24,16},{1,9},{9,1},{17,25},{25,17},{2,10},{10... | collective-permute-start | bytes 393224 | tf_op jit(solution)/shard_map/ppermute | solution.py:28
  119.1 15.0 %collective-permute-start.37 = (bf16[128,512]{1,0:T(8,128)(2,1)}, bf16[128,512]{1,0:T(8,128)(2,1)}, u32[]{:S(2)}, u32[]{:S(2)}) collective-permute-start(bf16[128,512]{1,0:T(8,128)(2,1)} %fusion.7), channel_id=1, source_target_pairs={{0,16},{8,24},{16,0},{24,8},{1,17},{9,25},{17,1},{25,9},{2,18},{10... | collective-permute-start | bytes 393224 | tf_op jit(solution)/shard_map/ppermute | solution.py:28

commit v3 on v2

--- a/solution.py
+++ b/solution.py
@@ -81,40 +81,37 @@
     )(*scalars, *near, *[pltpu.with_memory_space_constraint(a, pltpu.HBM) for a in arrays])
 
 
-def attention_kernel(offsets, where_ref, query_ref, *refs):
-    kv_refs, (out_ref, score_ref, top_ref, sum_ref, acc_ref) = refs[:-5], refs[-5:]
+def attention_kernel(offsets, begins, ends, where_ref, query_ref, *refs):
+    count = len(refs) - (5 if ends else 4) - (0 if begins else 3)
+    kv_refs, refs = refs[:count], refs[count:]
+    if not begins:
+        old_top_ref, old_sum_ref, old_acc_ref, *refs = refs
+    if ends:
+        out_ref, *refs = refs
+        score_ref, top_ref, sum_ref, acc_ref = refs
+    else:
+        top_ref, sum_ref, acc_ref, score_ref = refs
     total, size = query_ref.shape
-    shared = 2
     wide = kv_refs[0].shape[1] // 2
-    keys = wide // shared
+    keys = wide // 2
     heads = total // keys
     mine = where_ref[2]
-    scale = 1.0 / math.sqrt(size)
+    scale = math.log2(math.e) / math.sqrt(size)
     row = lax.broadcasted_iota(jnp.int32, (total, keys), 0)
     column = lax.broadcasted_iota(jnp.int32, (total, keys), 1)
-    lower = lax.rem(row, heads) < heads // shared
+    lower = lax.rem(row, heads) < heads // 2
     behind = row // heads - column
-    source = lax.broadcasted_iota(jnp.int32, (wide, wide), 0)
-    target = lax.broadcasted_iota(jnp.int32, (wide, wide), 1)
-    apart = target == lax.rem(source, keys) * shared + source // keys
-    apart = apart.astype(F32).astype(BF16)
-    part = lambda rows: jnp.dot(apart, rows, preferred_element_type=F32).astype(BF16)
     blocks = [(kv_ref, b) for kv_ref in kv_refs for b in range(kv_ref.shape[0])]
     gaps = [(mine - (mine ^ offset)) * keys for offset in offsets]
     seen = [(gap >= 0) & (gap - (keys - 1) < WINDOW) for gap in gaps]
-    top_ref[...] = jnp.full_like(top_ref, -jnp.inf)
-    sum_ref[...] = jnp.zeros_like(sum_ref)
-    acc_ref[...] = jnp.zeros_like(acc_ref)
+    top_ref[...] = jnp.full_like(top_ref, -jnp.inf) if begins else old_top_ref[...]
 
     def scores(at):
         kv_ref, b = blocks[at]
         score = lax.dot_general(
-            query_ref[...],
-            part(kv_ref[b, :wide]),
-            (((1,), (1,)), ((), ())),
-            preferred_element_type=F32,
+            query_ref[...], kv_ref[b, :wide], (((1,), (1,)), ((), ())), preferred_element_type=F32
         )
-        return jnp.where(lower, score[:, :keys], score[:, keys:]) * scale
+        return jnp.where(lower, score[:, :keys], score[:, keys:])
 
     for at, gap in enumerate(gaps):
         inside = (gap >= keys - 1) & (gap + keys - 1 < WINDOW)
@@ -134,42 +131,51 @@
 
     top = jnp.max(top_ref[...], axis=1, keepdims=True)
     top_ref[...] = jnp.broadcast_to(top, (total, keys))
+    if begins:
+        sum_ref[...] = jnp.zeros_like(sum_ref)
+        acc_ref[...] = jnp.zeros_like(acc_ref)
+    else:
+        shrink = jnp.exp2((old_top_ref[...] - top_ref[...]) * scale)
+        sum_ref[...] = old_sum_ref[...] * shrink
+        acc_ref[...] = old_acc_ref[...] * shrink
 
     for at, (kv_ref, b) in enumerate(blocks):
 
         @pl.when(seen[at])
         def _(at=at, kv_ref=kv_ref, b=b):
-            weight = jnp.exp(score_ref[at] - top_ref[...])
+            weight = jnp.exp2((score_ref[at] - top_ref[...]) * scale)
             sum_ref[...] += weight
             weight = jnp.concatenate(
                 [jnp.where(lower, weight, 0.0), jnp.where(lower, 0.0, weight)], axis=1
             )
             acc_ref[...] += jnp.dot(
-                weight.astype(BF16), part(kv_ref[b, wide:]), preferred_element_type=F32
+                weight.astype(BF16), kv_ref[b, wide:], preferred_element_type=F32
             )
 
-    out_ref[...] = (acc_ref[...] / jnp.sum(sum_ref[...], axis=1, keepdims=True)).astype(BF16)
-
-
-def attention(query, kv_parts, offsets, where):
+    if ends:
+        out_ref[...] = (acc_ref[...] / jnp.sum(sum_ref[...], axis=1, keepdims=True)).astype(BF16)
+
+
+def attention(query, kv_parts, offsets, where, carried=None, ends=True):
     rows, heads, size = query.shape
     assert kv_parts[0].shape[1] == 4 * rows and size == rows
     total = rows * heads
+    begins = carried is None
     vmem = pl.BlockSpec(memory_space=pltpu.VMEM)
+    state = [jax.ShapeDtypeStruct((total, rows), F32)] * 3
+    scores = [pltpu.VMEM((len(offsets), total, rows), F32)]
     out = pl.pallas_call(
-        functools.partial(attention_kernel, offsets),
-        out_shape=jax.ShapeDtypeStruct((total, size), BF16),
-        in_specs=[pl.BlockSpec(memory_space=pltpu.SMEM), vmem] + [vmem] * len(kv_parts),
-        out_specs=vmem,
-        scratch_shapes=[pltpu.VMEM((len(offsets), total, rows), F32)]
-        + [pltpu.VMEM((total, rows), F32)] * 2
-        + [pltpu.VMEM((total, size), F32)],
+        functools.partial(attention_kernel, offsets, begins, ends),
+        out_shape=jax.ShapeDtypeStruct((total, size), BF16) if ends else state,
+        in_specs=[pl.BlockSpec(memory_space=pltpu.SMEM), vmem]
+        + [vmem] * (len(kv_parts) + (0 if begins else 3)),
+        out_specs=vmem if ends else [vmem] * 3,
+        scratch_shapes=scores + [pltpu.VMEM((total, rows), F32)] * 3 if ends else scores,
         compiler_params=pltpu.CompilerParams(
             vmem_limit_bytes=(len(offsets) + 40) * total * rows * 4
         ),
-        name="attention",
-    )(where, query.reshape(total, size), *kv_parts)
-    return out.reshape(rows, heads, size)
+    )(where, query.reshape(total, size), *kv_parts, *(carried or ()))
+    return out.reshape(rows, heads, size) if ends else out
 
 
 def norm_kernel(
@@ -613,7 +619,24 @@
     return jnp.dot(pick, ref[...], preferred_element_type=F32)
 
 
-def state_kernel(input_ref, inflow_ref, readout_ref, step_ref, log_ref, intra_ref, state_ref, sent_ref):
+def state_kernel(
+    input_ref,
+    inflow_ref,
+    readout_ref,
+    step_ref,
+    log_ref,
+    key_ref,
+    value_ref,
+    intra_ref,
+    state_ref,
+    sent_ref,
+    kv_ref,
+):
+    shared = key_ref.shape[0] // input_ref.shape[0]
+    for n, ref in enumerate((key_ref, value_ref)):
+        for h in range(shared):
+            start = (n * shared + h) * input_ref.shape[0]
+            kv_ref[start : start + input_ref.shape[0]] = group_rows(ref, h, shared).astype(BF16)
     rows = input_ref.shape[0]
     heads = step_ref.shape[0]
     groups = inflow_ref.shape[0] // rows
@@ -657,18 +680,19 @@
             sent_ref[:, columns] = block.astype(BF16)
 
 
-def state_local(inputs, inflow, readout, step, log_decay):
+def state_local(inputs, inflow, readout, step, log_decay, keys, values):
     rows, channels = inputs.shape
     assert rows == STRETCH
     return staged_call(
         state_kernel,
         (),
         (),
-        (inputs, inflow, readout, step, log_decay),
+        (inputs, inflow, readout, step, log_decay, keys, values),
         [
             jax.ShapeDtypeStruct((rows, channels), F32),
             jax.ShapeDtypeStruct((NS, channels), F32),
             jax.ShapeDtypeStruct((NS, channels), BF16),
+            jax.ShapeDtypeStruct((2 * keys.shape[0], keys.shape[1]), BF16),
         ],
     )
 
@@ -871,8 +895,15 @@
     flat = lambda a: a.reshape(-1, a.shape[2])
     heads = step_size.shape[1]
     inflow, readout = flat(state_inflow), flat(state_readout)
-    intra, state, sent = state_local(state_input, inflow, readout, step_size.T, log_decay.T)
-    kv = jnp.concatenate([flat(key_heads), flat(value_head_rows)], axis=0)
+    intra, state, sent, kv = state_local(
+        state_input,
+        inflow,
+        readout,
+        step_size.T,
+        log_decay.T,
+        flat(key_heads),
+        flat(value_head_rows),
+    )
     finish_args = (
         intra,
         readout,
@@ -916,8 +947,8 @@
     beyond = swap(own, SEQ, far)
     beside = swap(own, SEQ, near)
     here = jnp.stack([own, beside])
-    kv_own = jnp.stack([kv, swap(kv, EXP, side)])
-    kv_own = jnp.stack([kv_own, swap(kv_own, SEQ, far)])
+    kv_own = jnp.stack([kv, swap(kv, SEQ, far)])
+    kv_own = jnp.stack([kv_own, swap(kv_own, SEQ, near)])
     there = jnp.stack([beyond, swap(beyond, SEQ, near)])
     pieces_a = spread_near(here)
     pieces_b = spread_near(there)
@@ -927,7 +958,7 @@
     other = lax.ppermute(sent, *span_route(1))
     *entering, state, sent = scan_step(order, 1, heads, where, info_all, other, state)
     other2 = lax.ppermute(sent, *span_route(2))
-    kv_other = swap(kv_own, SEQ, near)
+    kv_other = swap(kv_own, EXP, side)
 
     offsets = ((0, high), (core, core ^ high))
     keep_a, send_a, keep_b, send_b = experts_gather(
@@ -943,9 +974,10 @@
         left = fold(kept[0, 0], kept[0, 1], TP, high)
         right = fold(kept[1, 0], kept[1, 1], EXP, side)
         firsts.append((name, left, right))
-    kv_parts = [a.reshape(-1, *kv.shape) for a in (kv_own, kv_other)]
-    kv_offsets = [n * nx ^ f * nx ^ i for n in (0, near) for f in (0, far) for i in (0, side)]
-    window_out = attention(query_heads, kv_parts, kv_offsets, where)
+    kv_own, kv_other = [a.reshape(-1, *kv.shape) for a in (kv_own, kv_other)]
+    offsets = [n * nx ^ f * nx for n in (0, near) for f in (0, far)]
+    carried = attention(query_heads, [kv_own], offsets, where, ends=False)
+    window_out = attention(query_heads, [kv_other], [o ^ side for o in offsets], where, carried)
     state_out = state_finish(order, 4, where, info_all, other4, *entering, *finish_args)
     for name, left, right in firsts:
         left = fold(left[0], left[1], EXP, side)

time: 136 us -> 143 us (1.051)
  the two profiles are of different devices: /device:TPU:24 before, /device:TPU:0 now
where the time goes in v3:
time: 143 us; the launch traced here: 141 us
  waiting for transfers between devices  57.5 us (40%)
  starting transfers between devices  45.5 us (32%)
  Pallas kernels  31.4 us (22%)
  other arithmetic  4.48 us (3%)
    ppermute x35, waiting for transfers between devices, swap(): lax.ppermute(block, axis, [(i, i ^ bit) for i in range(lax.axis_size(axis...  53.7 us
    ppermute x35, starting transfers between devices, swap(): lax.ppermute(block, axis, [(i, i ^ bit) for i in range(lax.axis_size(axis...  40.6 us
    pallas_call x1, Pallas kernels, experts_gather(): pl.pallas_call(functools.partial(gather_kernel, offsets), out_shape=[resu...  17.6 us
    pallas_call x3, Pallas kernels, staged_call(): pl.pallas_call(kernel, out_shape=out_shape, in_specs=[smem] * len(scalars...  8.29 us
    ppermute x1, starting transfers between devices, in_groups(): other4 = lax.ppermute(sent, *span_route(4))  3.42 us
    pallas_call x2, Pallas kernels, attention(): pl.pallas_call(functools.partial(attention_kernel, offsets, begins, ends)...  3.1 us
  transfers between devices with their start and end apart: 38, of which 18 were waited for; matrix products, arithmetic and copies ran while one was open for 3% of the time, Pallas kernels for 8%

profile of v3, /device:TPU:0, one launch (start us, length us, event | category | flops | bytes accessed | tf_op | source)
XLA Modules:
  0.0 140.8 jit_solution(16327037818790698466)
XLA Ops:
  0.7 2.2 %shard_map.196 = bf16[144,512]{1,0:T(8,128)(2,1)S(1)} custom-call(s32[3]{0:T(128)S(1)} %pad_add_fusion.where_ref.refs_0_, bf16[128,2048]{1,0:T(8,128)(2,1)} %refs_1_.2, f32[1,2048]{1,0:T(1,128)} %bitcast.148, bf16[8,2048]{1,0:T(8,128)(2,1)} %bitcast.147, s32[2,128]{1,0:T(2,128)} %bitcast.151, s32[2,128]{1,0:T(2,128)} %bitcast.152, f32[16,128]{1,0:T(8,128)} %bitcast.141), custom_call_target="tpu_custom_call" | custom-call | tf_op jit(solution)/shard_map/pallas_call | solution.py:70
  2.9 3.1 %collective-permute-start.3 = (bf16[144,512]{1,0:T(8,128)(2,1)S(1)}, bf16[144,512]{1,0:T(8,128)(2,1)S(1)}, u32[]{:S(2)}, u32[]{:S(2)}) collective-permute-start(bf16[144,512]{1,0:T(8,128)(2,1)S(1)} %shard_map.196), channel_id=1, source_target_pairs={{0,8},{8,0},{16,24},{24,16},{1,9},{9,1},{17,25},{25,17},{2,10},{10... | collective-permute-start | bytes 442376 | tf_op jit(solution)/shard_map/ppermute | solution.py:28
  6.0 2.6 %collective-permute-start.5 = (bf16[144,512]{1,0:T(8,128)(2,1)S(1)}, bf16[144,512]{1,0:T(8,128)(2,1)S(1)}, u32[]{:S(2)}, u32[]{:S(2)}) collective-permute-start(bf16[144,512]{1,0:T(8,128)(2,1)S(1)} %shard_map.196), channel_id=1, source_target_pairs={{0,16},{8,24},{16,0},{24,8},{1,17},{9,25},{17,1},{25,9},{2,18},{10... | collective-permute-start | bytes 442376 | tf_op jit(solution)/shard_map/ppermute | solution.py:28
  8.6 3.8 %collective-permute-done.3 = bf16[144,512]{1,0:T(8,128)(2,1)S(1)} collective-permute-done((bf16[144,512]{1,0:T(8,128)(2,1)S(1)}, bf16[144,512]{1,0:T(8,128)(2,1)S(1)}, u32[]{:S(2)}, u32[]{:S(2)}) %collective-permute-start.3) | collective-permute-done | bytes 147488 | tf_op jit(solution)/shard_map/ppermute | solution.py:28
  12.5 1.9 %collective-permute-start.14 = (bf16[2,128,256]{2,1,0:T(8,128)(2,1)S(1)}, bf16[2,128,256]{2,1,0:T(8,128)(2,1)S(1)}, u32[]{:S(2)}, u32[]{:S(2)}) collective-permute-start(bf16[2,128,256]{2,1,0:T(8,128)(2,1)S(1)} %pad_maximum_fusion.9), channel_id=1, source_target_pairs={{0,2},{1,3},{2,0},{3,1},{4,6},{5,7},{6,4},{7,5},{8,10},{9,11},{10,... | collective-permute-start | bytes 393224 | tf_op jit(solution)/shard_map/ppermute | solution.py:28
  14.4 1.0 collective-permute-done.5
  15.4 0.4 collective-permute-start.6
  15.9 1.6 %collective-permute-start.4 = (bf16[2,144,256]{2,1,0:T(8,128)(2,1)S(1)}, bf16[2,144,256]{2,1,0:T(8,128)(2,1)S(1)}, u32[]{:S(2)}, u32[]{:S(2)}) collective-permute-start(bf16[2,144,256]{2,1,0:T(8,128)(2,1)S(1)} %fusion.20), channel_id=1, source_target_pairs={{0,4},{4,0},{1,5},{5,1},{2,6},{6,2},{3,7},{7,3},{8,12},{12,8},{9,1... | collective-permute-start | bytes 442376 | tf_op jit(solution)/shard_map/ppermute | solution.py:28
  17.6 1.9 %collective-permute-start.15 = (bf16[2,2,128,256]{3,2,1,0:T(8,128)(2,1)S(1)}, bf16[2,2,128,256]{3,2,1,0:T(8,128)(2,1)S(1)}, u32[]{:S(2)}, u32[]{:S(2)}) collective-permute-start(bf16[2,2,128,256]{3,2,1,0:T(8,128)(2,1)S(1)} %pad_maximum_fusion.6.refs_7_), channel_id=1, source_target_pairs={{0,4},{4,0},{1,5},{5,1},{2,6},{6,2},{3,7},{7,3},{8,12},{12,8},{9,1... | collective-permute-start | bytes 786440 | tf_op jit(solution)/shard_map/ppermute | solution.py:28
  19.5 1.1 collective-permute-done.6
  20.6 1.6 %collective-permute-start.21 = (bf16[2,128,256]{2,1,0:T(8,128)(2,1)S(1)}, bf16[2,128,256]{2,1,0:T(8,128)(2,1)S(1)}, u32[]{:S(2)}, u32[]{:S(2)}) collective-permute-start(bf16[2,128,256]{2,1,0:T(8,128)(2,1)S(1)} %pad_maximum_fusion.8), channel_id=1, source_target_pairs={{0,2},{1,3},{2,0},{3,1},{4,6},{5,7},{6,4},{7,5},{8,10},{9,11},{10,... | collective-permute-start | bytes 393224 | tf_op jit(solution)/shard_map/ppermute | solution.py:28
  22.2 1.5 %collective-permute-start.7 = (bf16[2,144,256]{2,1,0:T(8,128)(2,1)S(1)}, bf16[2,144,256]{2,1,0:T(8,128)(2,1)S(1)}, u32[]{:S(2)}, u32[]{:S(2)}) collective-permute-start(bf16[2,144,256]{2,1,0:T(8,128)(2,1)S(1)} %fusion.19), channel_id=1, source_target_pairs={{0,4},{4,0},{1,5},{5,1},{2,6},{6,2},{3,7},{7,3},{8,12},{12,8},{9,1... | collective-permute-start | bytes 442376 | tf_op jit(solution)/shard_map/ppermute | solution.py:28
  23.9 6.0 %collective-permute-done.7 = bf16[2,144,256]{2,1,0:T(8,128)(2,1)S(1)} collective-permute-done((bf16[2,144,256]{2,1,0:T(8,128)(2,1)S(1)}, bf16[2,144,256]{2,1,0:T(8,128)(2,1)S(1)}, u32[]{:S(2)}, u32[]{:S(2)}) %collective-permute-start.7) | collective-permute-done | bytes 147488 | tf_op jit(solution)/shard_map/ppermute | solution.py:28
  29.9 1.5 %collective-permute-start.11 = (bf16[2,2,144,256]{3,2,1,0:T(8,128)(2,1)S(1)}, bf16[2,2,144,256]{3,2,1,0:T(8,128)(2,1)S(1)}, u32[]{:S(2)}, u32[]{:S(2)}) collective-permute-start(bf16[2,2,144,256]{3,2,1,0:T(8,128)(2,1)S(1)} %pad_maximum_fusion.1.refs_3_), channel_id=1, source_target_pairs={{0,2},{1,3},{2,0},{3,1},{4,6},{5,7},{6,4},{7,5},{8,10},{9,11},{10,... | collective-permute-start | bytes 884744 | tf_op jit(solution)/shard_map/ppermute | solution.py:28
  31.4 0.6 collective-permute-start.18
  32.1 1.6 %collective-permute-start.22 = (bf16[2,2,128,256]{3,2,1,0:T(8,128)(2,1)S(1)}, bf16[2,2,128,256]{3,2,1,0:T(8,128)(2,1)S(1)}, u32[]{:S(2)}, u32[]{:S(2)}) collective-permute-start(bf16[2,2,128,256]{3,2,1,0:T(8,128)(2,1)S(1)} %pad_maximum_fusion.7.refs_15_), channel_id=1, source_target_pairs={{0,4},{4,0},{1,5},{5,1},{2,6},{6,2},{3,7},{7,3},{8,12},{12,8},{9,1... | collective-permute-start | bytes 786440 | tf_op jit(solution)/shard_map/ppermute | solution.py:28
  33.7 0.1 collective-permute-start.19
  33.8 5.9 %collective-permute-done.11.refs_4_ = bf16[2,2,144,256]{3,2,1,0:T(8,128)(2,1)S(1)} collective-permute-done((bf16[2,2,144,256]{3,2,1,0:T(8,128)(2,1)S(1)}, bf16[2,2,144,256]{3,2,1,0:T(8,128)(2,1)S(1)}, u32[]{:S(2)}, u32[]{:S(2)}) %collective-permute-start.11) | collective-permute-done | bytes 294944 | tf_op jit(solution)/shard_map/ppermute | solution.py:28
  39.8 5.1 %collective-permute-done.18.refs_12_ = bf16[2,2,144,256]{3,2,1,0:T(8,128)(2,1)S(1)} collective-permute-done((bf16[2,2,144,256]{3,2,1,0:T(8,128)(2,1)S(1)}, bf16[2,2,144,256]{3,2,1,0:T(8,128)(2,1)S(1)}, u32[]{:S(2)}, u32[]{:S(2)}) %collective-permute-start.18) | collective-permute-done | bytes 294944 | tf_op jit(solution)/shard_map/ppermute | solution.py:28
  44.9 0.5 collective-permute-start.17
  45.5 1.4 collective-permute-done.17.refs_10_
  46.9 0.4 collective-permute-done.24.refs_18_
  47.2 17.6 %experts.1 = (bf16[2,2,2,2,128,256]{5,4,3,2,1,0:T(8,128)(2,1)S(1)}, bf16[2,2,2,2,128,256]{5,4,3,2,1,0:T(8,128)(2,1)S(1)}, bf16[2,2,2,2,128,256]{5,4,3,2,1,0:T(8,...) custom-call(s32[3]{0:T(128)S(1)} %pad_add_fusion.where_ref.refs_0_, bf16[4,448,2,2048]{3,2,1,0:T(2,128)(2,1)} %refs_1_.3, ...), custom_call_target="tpu_custom_call" | custom-call | tf_op jit(solution)/shard_map/experts/pallas_call | solution.py:551
  64.8 0.2 collective-permute-start.25
  65.0 2.7 %shard_map.193 = (f32[128,1024]{1,0:T(8,128)S(1)}, f32[128,1024]{1,0:T(8,128)S(1)}, bf16[128,1024]{1,0:T(8,128)(2,1)S(1)}, bf16[512,128]{1,0:T(8,128)(2,1)S(1)}) custom-call(bf16[128,1024]{1,0:T(8,128)(2,1)} %refs_7_.1, bf16[256,128]{1,0:T(8,128)(2,1)} %bitcast.144, bf16[256,128]{1,0:T(8,128)(2,1)} %bitcast.132, f32[16,128]{1,0:T(8,128)} %bitcast.149, ...), custom_call_target="tpu_custom_call" | custom-call | tf_op jit(solution)/shard_map/pallas_call | solution.py:70
  67.7 2.5 %collective-permute-start = (bf16[512,128]{1,0:T(8,128)(2,1)S(1)}, bf16[512,128]{1,0:T(8,128)(2,1)S(1)}, u32[]{:S(2)}, u32[]{:S(2)}) collective-permute-start(bf16[512,128]{1,0:T(8,128)(2,1)S(1)} %get-tuple-element.19), channel_id=1, source_target_pairs={{0,16},{8,24},{16,0},{24,8},{1,17},{9,25},{17,1},{25,9},{2,18},{10... | collective-permute-start | bytes 393224 | tf_op jit(solution)/shard_map/ppermute | solution.py:28
  70.2 0.5 collective-permute-start.8
  70.7 6.5 %collective-permute-done = bf16[512,128]{1,0:T(8,128)(2,1)S(1)} collective-permute-done((bf16[512,128]{1,0:T(8,128)(2,1)S(1)}, bf16[512,128]{1,0:T(8,128)(2,1)S(1)}, u32[]{:S(2)}, u32[]{:S(2)}) %collective-permute-start) | collective-permute-done | bytes 131104 | tf_op jit(solution)/shard_map/ppermute | solution.py:28
  77.5 1.0 collective-permute-done.8.other_ref
  78.5 0.8 shard_map.197
  79.3 1.0 collective-permute-start.9
  80.3 6.2 %collective-permute-done.1 = bf16[2,512,128]{2,1,0:T(8,128)(2,1)S(1)} collective-permute-done((bf16[2,512,128]{2,1,0:T(8,128)(2,1)S(1)}, bf16[2,512,128]{2,1,0:T(8,128)(2,1)S(1)}, u32[]{:S(2)}, u32[]{:S(2)}) %collective-permute-start.1) | collective-permute-done | bytes 262176 | tf_op jit(solution)/shard_map/ppermute | solution.py:28
  86.6 1.4 %collective-permute-start.2 = (bf16[2,2,512,128]{3,2,1,0:T(8,128)(2,1)S(1)}, bf16[2,2,512,128]{3,2,1,0:T(8,128)(2,1)S(1)}, u32[]{:S(2)}, u32[]{:S(2)}) collective-permute-start(bf16[2,2,512,128]{3,2,1,0:T(8,128)(2,1)S(1)} %pad_maximum_fusion), channel_id=1, source_target_pairs={{0,4},{4,0},{1,5},{5,1},{2,6},{6,2},{3,7},{7,3},{8,12},{12,8},{9,1... | collective-permute-start | bytes 1572872 | tf_op jit(solution)/shard_map/ppermute | solution.py:28
  88.0 2.7 %collective-permute-done.9.other_ref = bf16[128,1024]{1,0:T(8,128)(2,1)S(1)} collective-permute-done((bf16[128,1024]{1,0:T(8,128)(2,1)S(1)}, bf16[128,1024]{1,0:T(8,128)(2,1)S(1)}, u32[]{:S(2)}, u32[]{:S(2)}) %collective-permute-start.9) | collective-permute-done | bytes 262176 | tf_op jit(solution)/shard_map/ppermute | solution.py:960
  90.7 1.6 %shard_map.198 = (f32[128,1024]{1,0:T(8,128)S(1)}, f32[128,1024]{1,0:T(8,128)}, bf16[128,1024]{1,0:T(8,128)(2,1)S(1)}) custom-call(s32[3]{0:T(128)S(1)} %pad_add_fusion.where_ref.refs_0_, bf16[8,16,256]{2,1,0:T(8,128)(2,1)S(1)} %pad_maximum_fusion.10.total_ref.refs_1_, bf16[128,1024]{1,0:T(8,128)(2,1)S(1)} %collective-permute-done.9.other_ref, ...), custom_call_target="tpu_custom_call" | custom-call | tf_op jit(solution)/shard_map/pallas_call | solution.py:746
  92.3 3.4 %collective-permute-start.10 = (bf16[128,1024]{1,0:T(8,128)(2,1)S(1)}, bf16[128,1024]{1,0:T(8,128)(2,1)S(1)}, u32[]{:S(2)}, u32[]{:S(2)}) collective-permute-start(bf16[128,1024]{1,0:T(8,128)(2,1)S(1)} %get-tuple-element.28), channel_id=1, source_target_pairs={{0,16},{8,24},{1,17},{9,25},{2,18},{10,26},{3,19},{11,27},{4,20},{... | collective-permute-start | bytes 786440 | tf_op jit(solution)/shard_map/ppermute | solution.py:971
  95.7 0.3 fusion.30
  96.1 2.0 %collective-permute-start.28 = (bf16[2,2,128,256]{3,2,1,0:T(8,128)(2,1)S(1)}, bf16[2,2,128,256]{3,2,1,0:T(8,128)(2,1)S(1)}, u32[]{:S(2)}, u32[]{:S(2)}) collective-permute-start(bf16[2,2,128,256]{3,2,1,0:T(8,128)(2,1)S(1)} %get-tuple-element.45), channel_id=1, source_target_pairs={{0,4},{4,0},{1,5},{5,1},{2,6},{6,2},{3,7},{7,3},{8,12},{12,8},{9,1... | collective-permute-start | bytes 786440 | tf_op jit(solution)/shard_map/ppermute | solution.py:28
  98.1 1.5 %collective-permute-start.26 = (bf16[2,2,128,256]{3,2,1,0:T(8,128)(2,1)S(1)}, bf16[2,2,128,256]{3,2,1,0:T(8,128)(2,1)S(1)}, u32[]{:S(2)}, u32[]{:S(2)}) collective-permute-start(bf16[2,2,128,256]{3,2,1,0:T(8,128)(2,1)S(1)} %get-tuple-element.46), channel_id=1, source_target_pairs={{0,2},{1,3},{2,0},{3,1},{4,6},{5,7},{6,4},{7,5},{8,10},{9,11},{10,... | collective-permute-start | bytes 786440 | tf_op jit(solution)/shard_map/ppermute | solution.py:28
  99.7 0.3 fusion.31
  100.1 0.1 collective-permute-start.34
  100.2 5.2 %collective-permute-done.28 = bf16[2,2,128,256]{3,2,1,0:T(8,128)(2,1)S(1)} collective-permute-done((bf16[2,2,128,256]{3,2,1,0:T(8,128)(2,1)S(1)}, bf16[2,2,128,256]{3,2,1,0:T(8,128)(2,1)S(1)}, u32[]{:S(2)}, u32[]{:S(2)}) %collective-permute-start.28) | collective-permute-done | bytes 262176 | tf_op jit(solution)/shard_map/ppermute | solution.py:28
  105.4 1.5 %collective-permute-start.32 = (bf16[2,2,128,256]{3,2,1,0:T(8,128)(2,1)S(1)}, bf16[2,2,128,256]{3,2,1,0:T(8,128)(2,1)S(1)}, u32[]{:S(2)}, u32[]{:S(2)}) collective-permute-start(bf16[2,2,128,256]{3,2,1,0:T(8,128)(2,1)S(1)} %get-tuple-element.44), channel_id=1, source_target_pairs={{0,2},{1,3},{2,0},{3,1},{4,6},{5,7},{6,4},{7,5},{8,10},{9,11},{10,... | collective-permute-start | bytes 786440 | tf_op jit(solution)/shard_map/ppermute | solution.py:28
  106.9 0.1 fusion.2
  107.0 2.0 %collective-permute-start.27 = (bf16[2,128,256]{2,1,0:T(8,128)(2,1)S(1)}, bf16[2,128,256]{2,1,0:T(8,128)(2,1)S(1)}, u32[]{:S(2)}, u32[]{:S(2)}) collective-permute-start(bf16[2,128,256]{2,1,0:T(8,128)(2,1)S(1)} %fusion.21), channel_id=1, source_target_pairs={{0,4},{4,0},{1,5},{5,1},{2,6},{6,2},{3,7},{7,3},{8,12},{12,8},{9,1... | collective-permute-start | bytes 393224 | tf_op jit(solution)/shard_map/ppermute | solution.py:28
  109.1 1.8 %collective-permute-done.34 = bf16[2,2,128,256]{3,2,1,0:T(8,128)(2,1)S(1)} collective-permute-done((bf16[2,2,128,256]{3,2,1,0:T(8,128)(2,1)S(1)}, bf16[2,2,128,256]{3,2,1,0:T(8,128)(2,1)S(1)}, u32[]{:S(2)}, u32[]{:S(2)}) %collective-permute-start.34) | collective-permute-done | bytes 262176 | tf_op jit(solution)/shard_map/ppermute | solution.py:28
  110.8 1.5 %collective-permute-start.29 = (bf16[2,128,256]{2,1,0:T(8,128)(2,1)S(1)}, bf16[2,128,256]{2,1,0:T(8,128)(2,1)S(1)}, u32[]{:S(2)}, u32[]{:S(2)}) collective-permute-start(bf16[2,128,256]{2,1,0:T(8,128)(2,1)S(1)} %fusion.22), channel_id=1, source_target_pairs={{0,2},{1,3},{2,0},{3,1},{4,6},{5,7},{6,4},{7,5},{8,10},{9,11},{10,... | collective-permute-start | bytes 393224 | tf_op jit(solution)/shard_map/ppermute | solution.py:28
  112.4 0.6 collective-permute-done.32
  113.0 0.1 fusion
  113.1 2.2 %collective-permute-start.33 = (bf16[2,128,256]{2,1,0:T(8,128)(2,1)S(1)}, bf16[2,128,256]{2,1,0:T(8,128)(2,1)S(1)}, u32[]{:S(2)}, u32[]{:S(2)}) collective-permute-start(bf16[2,128,256]{2,1,0:T(8,128)(2,1)S(1)} %fusion.24), channel_id=1, source_target_pairs={{0,4},{4,0},{1,5},{5,1},{2,6},{6,2},{3,7},{7,3},{8,12},{12,8},{9,1... | collective-permute-start | bytes 393224 | tf_op jit(solution)/shard_map/ppermute | solution.py:28
  115.3 2.9 %collective-permute-done.33 = bf16[2,128,256]{2,1,0:T(8,128)(2,1)S(1)} collective-permute-done((bf16[2,128,256]{2,1,0:T(8,128)(2,1)S(1)}, bf16[2,128,256]{2,1,0:T(8,128)(2,1)S(1)}, u32[]{:S(2)}, u32[]{:S(2)}) %collective-permute-start.33) | collective-permute-done | bytes 131104 | tf_op jit(solution)/shard_map/ppermute | solution.py:28
  118.3 1.5 %collective-permute-start.35 = (bf16[2,128,256]{2,1,0:T(8,128)(2,1)S(1)}, bf16[2,128,256]{2,1,0:T(8,128)(2,1)S(1)}, u32[]{:S(2)}, u32[]{:S(2)}) collective-permute-start(bf16[2,128,256]{2,1,0:T(8,128)(2,1)S(1)} %fusion.25), channel_id=1, source_target_pairs={{0,2},{1,3},{2,0},{3,1},{4,6},{5,7},{6,4},{7,5},{8,10},{9,11},{10,... | collective-permute-start | bytes 393224 | tf_op jit(solution)/shard_map/ppermute | solution.py:28
  119.8 3.4 %collective-permute-done.35 = bf16[2,128,256]{2,1,0:T(8,128)(2,1)S(1)} collective-permute-done((bf16[2,128,256]{2,1,0:T(8,128)(2,1)S(1)}, bf16[2,128,256]{2,1,0:T(8,128)(2,1)S(1)}, u32[]{:S(2)}, u32[]{:S(2)}) %collective-permute-start.35) | collective-permute-done | bytes 131104 | tf_op jit(solution)/shard_map/ppermute | solution.py:28
  123.3 1.9 %collective-permute-start.36 = (bf16[128,512]{1,0:T(8,128)(2,1)S(1)}, bf16[128,512]{1,0:T(8,128)(2,1)S(1)}, u32[]{:S(2)}, u32[]{:S(2)}) collective-permute-start(bf16[128,512]{1,0:T(8,128)(2,1)S(1)} %fusion.26), channel_id=1, source_target_pairs={{0,8},{8,0},{16,24},{24,16},{1,9},{9,1},{17,25},{25,17},{2,10},{10... | collective-permute-start | bytes 393224 | tf_op jit(solution)/shard_map/ppermute | solution.py:28
  125.3 0.7 fusion.23
  125.9 0.2 collective-permute-start.30
  126.1 2.3 %collective-permute-done.36 = bf16[128,512]{1,0:T(8,128)(2,1)S(1)} collective-permute-done((bf16[128,512]{1,0:T(8,128)(2,1)S(1)}, bf16[128,512]{1,0:T(8,128)(2,1)S(1)}, u32[]{:S(2)}, u32[]{:S(2)}) %collective-permute-start.36) | collective-permute-done | bytes 131104 | tf_op jit(solution)/shard_map/ppermute | solution.py:28
  128.4 0.7 fusion.7
  129.1 2.7 %collective-permute-start.37 = (bf16[128,512]{1,0:T(8,128)(2,1)}, bf16[128,512]{1,0:T(8,128)(2,1)}, u32[]{:S(2)}, u32[]{:S(2)}) collective-permute-start(bf16[128,512]{1,0:T(8,128)(2,1)} %fusion.7), channel_id=1, source_target_pairs={{0,16},{8,24},{16,0},{24,8},{1,17},{9,25},{17,1},{25,9},{2,18},{10... | collective-permute-start | bytes 393224 | tf_op jit(solution)/shard_map/ppermute | solution.py:28
  131.8 0.7 broadcast_in_dim_reshape.3.refs_9_
  132.5 1.2 shard_map.194
  133.8 1.9 %shard_map.195 = bf16[1024,128]{1,0:T(8,128)(2,1)} custom-call(s32[3]{0:T(128)S(1)} %pad_add_fusion.where_ref.refs_0_, bf16[1024,128]{1,0:T(8,128)(2,1)S(1)} %bitcast.113, bf16[4,512,128]{2,1,0:T(8,128)(2,1)S(1)} %bitcast.114, f32[1024,128]{1,0:T(8,128)S(1)} %get-tuple-element.20.refs_1_, f32[1024,128]{1,0:T(8,128)S(1)} %get-tuple-element.21.refs_2_, ...), custom_call_target="tpu_custom_call" | custom-call | tf_op jit(solution)/shard_map/pallas_call | solution.py:167
  135.6 3.5 %shard_map.199 = bf16[128,1024]{1,0:T(8,128)(2,1)} custom-call(s32[3]{0:T(128)S(1)} %pad_add_fusion.where_ref.refs_0_, bf16[8,16,256]{2,1,0:T(8,128)(2,1)S(1)} %pad_maximum_fusion.10.total_ref.refs_1_, bf16[128,1024]{1,0:T(8,128)(2,1)S(1)} %collective-permute-done.10.refs_2_, f32[128,1024]{1,0:T(8,128)S(1)} %get-tuple-element.29.refs_3_, ...), custom_call_target="tpu_custom_call" | custom-call | tf_op jit(solution)/shard_map/pallas_call | solution.py:70
  139.1 1.7 %fusion.12 = bf16[128,512]{1,0:T(8,128)(2,1)} fusion(f32[2,128,256]{2,1,0:T(8,128)S(1)} %fusion.18, f32[2,128,256]{2,1,0:T(8,128)S(1)} %fusion.17, bf16[128,512]{1,0:T(8,128)(2,1)} %collective-permute-done.37, bf16[128,512]{1,0:T(8,128)(2,1)} %collective-permute-done.30), kind=kLoop, calls=%fused_computation.33 | loop fusion | flops 393216 | bytes 917504 | tf_op jit(solution)/shard_map/convert_element_type | solution.py:987
  (62 shorter events, 1.3 us)
Async XLA Ops:
  2.9 9.5 %collective-permute-start.3 = (bf16[144,512]{1,0:T(8,128)(2,1)S(1)}, bf16[144,512]{1,0:T(8,128)(2,1)S(1)}, u32[]{:S(2)}, u32[]{:S(2)}) collective-permute-start(bf16[144,512]{1,0:T(8,128)(2,1)S(1)} %shard_map.196), channel_id=1, source_target_pairs={{0,8},{8,0},{16,24},{24,16},{1,9},{9,1},{17,25},{25,17},{2,10},{10... | collective-permute-start | bytes 442376 | tf_op jit(solution)/shard_map/ppermute | solution.py:28
  6.0 9.4 %collective-permute-start.5 = (bf16[144,512]{1,0:T(8,128)(2,1)S(1)}, bf16[144,512]{1,0:T(8,128)(2,1)S(1)}, u32[]{:S(2)}, u32[]{:S(2)}) collective-permute-start(bf16[144,512]{1,0:T(8,128)(2,1)S(1)} %shard_map.196), channel_id=1, source_target_pairs={{0,16},{8,24},{16,0},{24,8},{1,17},{9,25},{17,1},{25,9},{2,18},{10... | collective-permute-start | bytes 442376 | tf_op jit(solution)/shard_map/ppermute | solution.py:28
  12.5 5.0 %collective-permute-start.14 = (bf16[2,128,256]{2,1,0:T(8,128)(2,1)S(1)}, bf16[2,128,256]{2,1,0:T(8,128)(2,1)S(1)}, u32[]{:S(2)}, u32[]{:S(2)}) collective-permute-start(bf16[2,128,256]{2,1,0:T(8,128)(2,1)S(1)} %pad_maximum_fusion.9), channel_id=1, source_target_pairs={{0,2},{1,3},{2,0},{3,1},{4,6},{5,7},{6,4},{7,5},{8,10},{9,11},{10,... | collective-permute-start | bytes 393224 | tf_op jit(solution)/shard_map/ppermute | solution.py:28
  15.4 5.1 %collective-permute-start.6 = (bf16[144,512]{1,0:T(8,128)(2,1)S(1)}, bf16[144,512]{1,0:T(8,128)(2,1)S(1)}, u32[]{:S(2)}, u32[]{:S(2)}) collective-permute-start(bf16[144,512]{1,0:T(8,128)(2,1)S(1)} %collective-permute-done.5), channel_id=1, source_target_pairs={{0,8},{8,0},{16,24},{24,16},{1,9},{9,1},{17,25},{25,17},{2,10},{10... | collective-permute-start | bytes 442376 | tf_op jit(solution)/shard_map/ppermute | solution.py:28
  15.9 7.8 %collective-permute-start.4 = (bf16[2,144,256]{2,1,0:T(8,128)(2,1)S(1)}, bf16[2,144,256]{2,1,0:T(8,128)(2,1)S(1)}, u32[]{:S(2)}, u32[]{:S(2)}) collective-permute-start(bf16[2,144,256]{2,1,0:T(8,128)(2,1)S(1)} %fusion.20), channel_id=1, source_target_pairs={{0,4},{4,0},{1,5},{5,1},{2,6},{6,2},{3,7},{7,3},{8,12},{12,8},{9,1... | collective-permute-start | bytes 442376 | tf_op jit(solution)/shard_map/ppermute | solution.py:28
  17.5 14.5 %collective-permute-start.16 = (bf16[2,2,128,256]{3,2,1,0:T(8,128)(2,1)S(1)}, bf16[2,2,128,256]{3,2,1,0:T(8,128)(2,1)S(1)}, u32[]{:S(2)}, u32[]{:S(2)}) collective-permute-start(bf16[2,2,128,256]{3,2,1,0:T(8,128)(2,1)S(1)} %pad_maximum_fusion.6.refs_7_), channel_id=1, source_target_pairs={{0,1},{1,0},{2,3},{3,2},{4,5},{5,4},{6,7},{7,6},{8,9},{9,8},{10,11... | collective-permute-start | bytes 786440 | tf_op jit(solution)/shard_map/ppermute | solution.py:28
  17.6 14.5 %collective-permute-start.15 = (bf16[2,2,128,256]{3,2,1,0:T(8,128)(2,1)S(1)}, bf16[2,2,128,256]{3,2,1,0:T(8,128)(2,1)S(1)}, u32[]{:S(2)}, u32[]{:S(2)}) collective-permute-start(bf16[2,2,128,256]{3,2,1,0:T(8,128)(2,1)S(1)} %pad_maximum_fusion.6.refs_7_), channel_id=1, source_target_pairs={{0,4},{4,0},{1,5},{5,1},{2,6},{6,2},{3,7},{7,3},{8,12},{12,8},{9,1... | collective-permute-start | bytes 786440 | tf_op jit(solution)/shard_map/ppermute | solution.py:28
  20.6 10.8 %collective-permute-start.21 = (bf16[2,128,256]{2,1,0:T(8,128)(2,1)S(1)}, bf16[2,128,256]{2,1,0:T(8,128)(2,1)S(1)}, u32[]{:S(2)}, u32[]{:S(2)}) collective-permute-start(bf16[2,128,256]{2,1,0:T(8,128)(2,1)S(1)} %pad_maximum_fusion.8), channel_id=1, source_target_pairs={{0,2},{1,3},{2,0},{3,1},{4,6},{5,7},{6,4},{7,5},{8,10},{9,11},{10,... | collective-permute-start | bytes 393224 | tf_op jit(solution)/shard_map/ppermute | solution.py:28
  22.2 7.7 %collective-permute-start.7 = (bf16[2,144,256]{2,1,0:T(8,128)(2,1)S(1)}, bf16[2,144,256]{2,1,0:T(8,128)(2,1)S(1)}, u32[]{:S(2)}, u32[]{:S(2)}) collective-permute-start(bf16[2,144,256]{2,1,0:T(8,128)(2,1)S(1)} %fusion.19), channel_id=1, source_target_pairs={{0,4},{4,0},{1,5},{5,1},{2,6},{6,2},{3,7},{7,3},{8,12},{12,8},{9,1... | collective-permute-start | bytes 442376 | tf_op jit(solution)/shard_map/ppermute | solution.py:28
  23.8 9.9 %collective-permute-start.12 = (bf16[2,2,144,256]{3,2,1,0:T(8,128)(2,1)S(1)}, bf16[2,2,144,256]{3,2,1,0:T(8,128)(2,1)S(1)}, u32[]{:S(2)}, u32[]{:S(2)}) collective-permute-start(bf16[2,2,144,256]{3,2,1,0:T(8,128)(2,1)S(1)} %pad_maximum_fusion.1.refs_3_), channel_id=1, source_target_pairs={{0,1},{1,0},{2,3},{3,2},{4,5},{5,4},{6,7},{7,6},{8,9},{9,8},{10,11... | collective-permute-start | bytes 884744 | tf_op jit(solution)/shard_map/ppermute | solution.py:28
  29.9 9.9 %collective-permute-start.11 = (bf16[2,2,144,256]{3,2,1,0:T(8,128)(2,1)S(1)}, bf16[2,2,144,256]{3,2,1,0:T(8,128)(2,1)S(1)}, u32[]{:S(2)}, u32[]{:S(2)}) collective-permute-start(bf16[2,2,144,256]{3,2,1,0:T(8,128)(2,1)S(1)} %pad_maximum_fusion.1.refs_3_), channel_id=1, source_target_pairs={{0,2},{1,3},{2,0},{3,1},{4,6},{5,7},{6,4},{7,5},{8,10},{9,11},{10,... | collective-permute-start | bytes 884744 | tf_op jit(solution)/shard_map/ppermute | solution.py:28
  31.4 13.5 %collective-permute-start.18 = (bf16[2,2,144,256]{3,2,1,0:T(8,128)(2,1)S(1)}, bf16[2,2,144,256]{3,2,1,0:T(8,128)(2,1)S(1)}, u32[]{:S(2)}, u32[]{:S(2)}) collective-permute-start(bf16[2,2,144,256]{3,2,1,0:T(8,128)(2,1)S(1)} %pad_maximum_fusion.2.refs_11_), channel_id=1, source_target_pairs={{0,2},{1,3},{2,0},{3,1},{4,6},{5,7},{6,4},{7,5},{8,10},{9,11},{10,... | collective-permute-start | bytes 884744 | tf_op jit(solution)/shard_map/ppermute | solution.py:28
  32.0 12.9 %collective-permute-start.23 = (bf16[2,2,128,256]{3,2,1,0:T(8,128)(2,1)S(1)}, bf16[2,2,128,256]{3,2,1,0:T(8,128)(2,1)S(1)}, u32[]{:S(2)}, u32[]{:S(2)}) collective-permute-start(bf16[2,2,128,256]{3,2,1,0:T(8,128)(2,1)S(1)} %pad_maximum_fusion.7.refs_15_), channel_id=1, source_target_pairs={{0,1},{1,0},{2,3},{3,2},{4,5},{5,4},{6,7},{7,6},{8,9},{9,8},{10,11... | collective-permute-start | bytes 786440 | tf_op jit(solution)/shard_map/ppermute | solution.py:28
  32.1 13.3 %collective-permute-start.22 = (bf16[2,2,128,256]{3,2,1,0:T(8,128)(2,1)S(1)}, bf16[2,2,128,256]{3,2,1,0:T(8,128)(2,1)S(1)}, u32[]{:S(2)}, u32[]{:S(2)}) collective-permute-start(bf16[2,2,128,256]{3,2,1,0:T(8,128)(2,1)S(1)} %pad_maximum_fusion.7.refs_15_), channel_id=1, source_target_pairs={{0,4},{4,0},{1,5},{5,1},{2,6},{6,2},{3,7},{7,3},{8,12},{12,8},{9,1... | collective-permute-start | bytes 786440 | tf_op jit(solution)/shard_map/ppermute | solution.py:28
  33.7 11.8 %collective-permute-start.19 = (bf16[2,2,144,256]{3,2,1,0:T(8,128)(2,1)S(1)}, bf16[2,2,144,256]{3,2,1,0:T(8,128)(2,1)S(1)}, u32[]{:S(2)}, u32[]{:S(2)}) collective-permute-start(bf16[2,2,144,256]{3,2,1,0:T(8,128)(2,1)S(1)} %pad_maximum_fusion.2.refs_11_), channel_id=1, source_target_pairs={{0,1},{1,0},{2,3},{3,2},{4,5},{5,4},{6,7},{7,6},{8,9},{9,8},{10,11... | collective-permute-start | bytes 884744 | tf_op jit(solution)/shard_map/ppermute | solution.py:28
  39.8 7.1 %collective-permute-start.13 = (bf16[2,2,144,256]{3,2,1,0:T(8,128)(2,1)S(1)}, bf16[2,2,144,256]{3,2,1,0:T(8,128)(2,1)S(1)}, u32[]{:S(2)}, u32[]{:S(2)}) collective-permute-start(bf16[2,2,144,256]{3,2,1,0:T(8,128)(2,1)S(1)} %collective-permute-done.11.refs_4_), channel_id=1, source_target_pairs={{0,1},{1,0},{2,3},{3,2},{4,5},{5,4},{6,7},{7,6},{8,9},{9,8},{10,11... | collective-permute-start | bytes 884744 | tf_op jit(solution)/shard_map/ppermute | solution.py:28
  44.9 2.3 %collective-permute-start.20 = (bf16[2,2,144,256]{3,2,1,0:T(8,128)(2,1)S(1)}, bf16[2,2,144,256]{3,2,1,0:T(8,128)(2,1)S(1)}, u32[]{:S(2)}, u32[]{:S(2)}) collective-permute-start(bf16[2,2,144,256]{3,2,1,0:T(8,128)(2,1)S(1)} %collective-permute-done.18.refs_12_), channel_id=1, source_target_pairs={{0,1},{1,0},{2,3},{3,2},{4,5},{5,4},{6,7},{7,6},{8,9},{9,8},{10,11... | collective-permute-start | bytes 884744 | tf_op jit(solution)/shard_map/ppermute | solution.py:28
  44.9 2.0 %collective-permute-start.17 = (bf16[2,2,128,256]{3,2,1,0:T(8,128)(2,1)S(1)}, bf16[2,2,128,256]{3,2,1,0:T(8,128)(2,1)S(1)}, u32[]{:S(2)}, u32[]{:S(2)}) collective-permute-start(bf16[2,2,128,256]{3,2,1,0:T(8,128)(2,1)S(1)} %collective-permute-done.15.refs_8_), channel_id=1, source_target_pairs={{0,1},{1,0},{2,3},{3,2},{4,5},{5,4},{6,7},{7,6},{8,9},{9,8},{10,11... | collective-permute-start | bytes 786440 | tf_op jit(solution)/shard_map/ppermute | solution.py:28
  45.4 1.8 %collective-permute-start.24 = (bf16[2,2,128,256]{3,2,1,0:T(8,128)(2,1)S(1)}, bf16[2,2,128,256]{3,2,1,0:T(8,128)(2,1)S(1)}, u32[]{:S(2)}, u32[]{:S(2)}) collective-permute-start(bf16[2,2,128,256]{3,2,1,0:T(8,128)(2,1)S(1)} %collective-permute-done.22.refs_16_), channel_id=1, source_target_pairs={{0,1},{1,0},{2,3},{3,2},{4,5},{5,4},{6,7},{7,6},{8,9},{9,8},{10,11... | collective-permute-start | bytes 786440 | tf_op jit(solution)/shard_map/ppermute | solution.py:28
  64.8 30.9 %collective-permute-start.25 = (bf16[2,2,2,2,128,256]{5,4,3,2,1,0:T(8,128)(2,1)S(1)}, bf16[2,2,2,2,128,256]{5,4,3,2,1,0:T(8,128)(2,1)S(1)}, u32[]{:S(2)}, u32[]{:S(2)}) collective-permute-start(bf16[2,2,2,2,128,256]{5,4,3,2,1,0:T(8,128)(2,1)S(1)} %get-tuple-element.32), channel_id=1, source_target_pairs={{0,1},{1,0},{2,3},{3,2},{4,5},{5,4},{6,7},{7,6},{8,9},{9,8},{10,11... | collective-permute-start | bytes 3145736 | tf_op jit(solution)/shard_map/ppermute | solution.py:28
  67.7 9.5 %collective-permute-start = (bf16[512,128]{1,0:T(8,128)(2,1)S(1)}, bf16[512,128]{1,0:T(8,128)(2,1)S(1)}, u32[]{:S(2)}, u32[]{:S(2)}) collective-permute-start(bf16[512,128]{1,0:T(8,128)(2,1)S(1)} %get-tuple-element.19), channel_id=1, source_target_pairs={{0,16},{8,24},{16,0},{24,8},{1,17},{9,25},{17,1},{25,9},{2,18},{10... | collective-permute-start | bytes 393224 | tf_op jit(solution)/shard_map/ppermute | solution.py:28
  70.2 8.3 %collective-permute-start.8 = (bf16[128,1024]{1,0:T(8,128)(2,1)S(1)}, bf16[128,1024]{1,0:T(8,128)(2,1)S(1)}, u32[]{:S(2)}, u32[]{:S(2)}) collective-permute-start(bf16[128,1024]{1,0:T(8,128)(2,1)S(1)} %get-tuple-element.23), channel_id=1, source_target_pairs={{0,4},{4,0},{1,5},{5,1},{2,6},{6,2},{3,7},{7,3},{8,12},{12,8},{9,1... | collective-permute-start | bytes 786440 | tf_op jit(solution)/shard_map/ppermute | solution.py:958
  77.3 9.2 %collective-permute-start.1 = (bf16[2,512,128]{2,1,0:T(8,128)(2,1)S(1)}, bf16[2,512,128]{2,1,0:T(8,128)(2,1)S(1)}, u32[]{:S(2)}, u32[]{:S(2)}) collective-permute-start(bf16[2,512,128]{2,1,0:T(8,128)(2,1)S(1)} %get-tuple-element.48), channel_id=1, source_target_pairs={{0,8},{8,0},{16,24},{24,16},{1,9},{9,1},{17,25},{25,17},{2,10},{10... | collective-permute-start | bytes 786440 | tf_op jit(solution)/shard_map/ppermute | solution.py:28
  77.4 22.3 %collective-permute-start.31 = (bf16[2,2,2,2,128,256]{5,4,3,2,1,0:T(8,128)(2,1)S(1)}, bf16[2,2,2,2,128,256]{5,4,3,2,1,0:T(8,128)(2,1)S(1)}, u32[]{:S(2)}, u32[]{:S(2)}) collective-permute-start(bf16[2,2,2,2,128,256]{5,4,3,2,1,0:T(8,128)(2,1)S(1)} %get-tuple-element.34), channel_id=1, source_target_pairs={{0,1},{1,0},{2,3},{3,2},{4,5},{5,4},{6,7},{7,6},{8,9},{9,8},{10,11... | collective-permute-start | bytes 3145736 | tf_op jit(solution)/shard_map/ppermute | solution.py:28
  79.3 11.4 %collective-permute-start.9 = (bf16[128,1024]{1,0:T(8,128)(2,1)S(1)}, bf16[128,1024]{1,0:T(8,128)(2,1)S(1)}, u32[]{:S(2)}, u32[]{:S(2)}) collective-permute-start(bf16[128,1024]{1,0:T(8,128)(2,1)S(1)} %get-tuple-element.25), channel_id=1, source_target_pairs={{0,8},{8,0},{16,24},{24,16},{1,9},{9,1},{17,25},{25,17},{2,10},{10... | collective-permute-start | bytes 786440 | tf_op jit(solution)/shard_map/ppermute | solution.py:960
  86.6 47.2 %collective-permute-start.2 = (bf16[2,2,512,128]{3,2,1,0:T(8,128)(2,1)S(1)}, bf16[2,2,512,128]{3,2,1,0:T(8,128)(2,1)S(1)}, u32[]{:S(2)}, u32[]{:S(2)}) collective-permute-start(bf16[2,2,512,128]{3,2,1,0:T(8,128)(2,1)S(1)} %pad_maximum_fusion), channel_id=1, source_target_pairs={{0,4},{4,0},{1,5},{5,1},{2,6},{6,2},{3,7},{7,3},{8,12},{12,8},{9,1... | collective-permute-start | bytes 1572872 | tf_op jit(solution)/shard_map/ppermute | solution.py:28
  92.3 43.3 %collective-permute-start.10 = (bf16[128,1024]{1,0:T(8,128)(2,1)S(1)}, bf16[128,1024]{1,0:T(8,128)(2,1)S(1)}, u32[]{:S(2)}, u32[]{:S(2)}) collective-permute-start(bf16[128,1024]{1,0:T(8,128)(2,1)S(1)} %get-tuple-element.28), channel_id=1, source_target_pairs={{0,16},{8,24},{1,17},{9,25},{2,18},{10,26},{3,19},{11,27},{4,20},{... | collective-permute-start | bytes 786440 | tf_op jit(solution)/shard_map/ppermute | solution.py:971
  96.1 9.2 %collective-permute-start.28 = (bf16[2,2,128,256]{3,2,1,0:T(8,128)(2,1)S(1)}, bf16[2,2,128,256]{3,2,1,0:T(8,128)(2,1)S(1)}, u32[]{:S(2)}, u32[]{:S(2)}) collective-permute-start(bf16[2,2,128,256]{3,2,1,0:T(8,128)(2,1)S(1)} %get-tuple-element.45), channel_id=1, source_target_pairs={{0,4},{4,0},{1,5},{5,1},{2,6},{6,2},{3,7},{7,3},{8,12},{12,8},{9,1... | collective-permute-start | bytes 786440 | tf_op jit(solution)/shard_map/ppermute | solution.py:28
  98.1 8.7 %collective-permute-start.26 = (bf16[2,2,128,256]{3,2,1,0:T(8,128)(2,1)S(1)}, bf16[2,2,128,256]{3,2,1,0:T(8,128)(2,1)S(1)}, u32[]{:S(2)}, u32[]{:S(2)}) collective-permute-start(bf16[2,2,128,256]{3,2,1,0:T(8,128)(2,1)S(1)} %get-tuple-element.46), channel_id=1, source_target_pairs={{0,2},{1,3},{2,0},{3,1},{4,6},{5,7},{6,4},{7,5},{8,10},{9,11},{10,... | collective-permute-start | bytes 786440 | tf_op jit(solution)/shard_map/ppermute | solution.py:28
  100.1 10.8 %collective-permute-start.34 = (bf16[2,2,128,256]{3,2,1,0:T(8,128)(2,1)S(1)}, bf16[2,2,128,256]{3,2,1,0:T(8,128)(2,1)S(1)}, u32[]{:S(2)}, u32[]{:S(2)}) collective-permute-start(bf16[2,2,128,256]{3,2,1,0:T(8,128)(2,1)S(1)} %get-tuple-element.43), channel_id=1, source_target_pairs={{0,4},{4,0},{1,5},{5,1},{2,6},{6,2},{3,7},{7,3},{8,12},{12,8},{9,1... | collective-permute-start | bytes 786440 | tf_op jit(solution)/shard_map/ppermute | solution.py:28
  105.4 7.6 %collective-permute-start.32 = (bf16[2,2,128,256]{3,2,1,0:T(8,128)(2,1)S(1)}, bf16[2,2,128,256]{3,2,1,0:T(8,128)(2,1)S(1)}, u32[]{:S(2)}, u32[]{:S(2)}) collective-permute-start(bf16[2,2,128,256]{3,2,1,0:T(8,128)(2,1)S(1)} %get-tuple-element.44), channel_id=1, source_target_pairs={{0,2},{1,3},{2,0},{3,1},{4,6},{5,7},{6,4},{7,5},{8,10},{9,11},{10,... | collective-permute-start | bytes 786440 | tf_op jit(solution)/shard_map/ppermute | solution.py:28
  107.0 18.1 %collective-permute-start.27 = (bf16[2,128,256]{2,1,0:T(8,128)(2,1)S(1)}, bf16[2,128,256]{2,1,0:T(8,128)(2,1)S(1)}, u32[]{:S(2)}, u32[]{:S(2)}) collective-permute-start(bf16[2,128,256]{2,1,0:T(8,128)(2,1)S(1)} %fusion.21), channel_id=1, source_target_pairs={{0,4},{4,0},{1,5},{5,1},{2,6},{6,2},{3,7},{7,3},{8,12},{12,8},{9,1... | collective-permute-start | bytes 393224 | tf_op jit(solution)/shard_map/ppermute | solution.py:28
  110.8 14.4 %collective-permute-start.29 = (bf16[2,128,256]{2,1,0:T(8,128)(2,1)S(1)}, bf16[2,128,256]{2,1,0:T(8,128)(2,1)S(1)}, u32[]{:S(2)}, u32[]{:S(2)}) collective-permute-start(bf16[2,128,256]{2,1,0:T(8,128)(2,1)S(1)} %fusion.22), channel_id=1, source_target_pairs={{0,2},{1,3},{2,0},{3,1},{4,6},{5,7},{6,4},{7,5},{8,10},{9,11},{10,... | collective-permute-start | bytes 393224 | tf_op jit(solution)/shard_map/ppermute | solution.py:28
  113.1 5.1 %collective-permute-start.33 = (bf16[2,128,256]{2,1,0:T(8,128)(2,1)S(1)}, bf16[2,128,256]{2,1,0:T(8,128)(2,1)S(1)}, u32[]{:S(2)}, u32[]{:S(2)}) collective-permute-start(bf16[2,128,256]{2,1,0:T(8,128)(2,1)S(1)} %fusion.24), channel_id=1, source_target_pairs={{0,4},{4,0},{1,5},{5,1},{2,6},{6,2},{3,7},{7,3},{8,12},{12,8},{9,1... | collective-permute-start | bytes 393224 | tf_op jit(solution)/shard_map/ppermute | solution.py:28
  118.3 5.0 %collective-permute-start.35 = (bf16[2,128,256]{2,1,0:T(8,128)(2,1)S(1)}, bf16[2,128,256]{2,1,0:T(8,128)(2,1)S(1)}, u32[]{:S(2)}, u32[]{:S(2)}) collective-permute-start(bf16[2,128,256]{2,1,0:T(8,128)(2,1)S(1)} %fusion.25), channel_id=1, source_target_pairs={{0,2},{1,3},{2,0},{3,1},{4,6},{5,7},{6,4},{7,5},{8,10},{9,11},{10,... | collective-permute-start | bytes 393224 | tf_op jit(solution)/shard_map/ppermute | solution.py:28
  119.8 11.9 %copy-start.1 = (f32[16]{0:T(128)S(1)}, f32[16]{0:T(128)}, u32[]{:S(2)}) copy-start(f32[16]{0:T(128)} %param.27) | copy-start | bytes 196
  119.8 12.7 %copy-start = (bf16[128,8,128]{2,1,0:T(8,128)(2,1)S(1)}, bf16[128,8,128]{2,1,0:T(8,128)(2,1)}, u32[]{:S(2)}) copy-start(bf16[128,8,128]{2,1,0:T(8,128)(2,1)} %param.18) | copy-start | bytes 786436
  123.3 5.1 %collective-permute-start.36 = (bf16[128,512]{1,0:T(8,128)(2,1)S(1)}, bf16[128,512]{1,0:T(8,128)(2,1)S(1)}, u32[]{:S(2)}, u32[]{:S(2)}) collective-permute-start(bf16[128,512]{1,0:T(8,128)(2,1)S(1)} %fusion.26), channel_id=1, source_target_pairs={{0,8},{8,0},{16,24},{24,16},{1,9},{9,1},{17,25},{25,17},{2,10},{10... | collective-permute-start | bytes 393224 | tf_op jit(solution)/shard_map/ppermute | solution.py:28
  125.9 13.2 %collective-permute-start.30 = (bf16[128,512]{1,0:T(8,128)(2,1)}, bf16[128,512]{1,0:T(8,128)(2,1)}, u32[]{:S(2)}, u32[]{:S(2)}) collective-permute-start(bf16[128,512]{1,0:T(8,128)(2,1)} %fusion.23), channel_id=1, source_target_pairs={{0,8},{8,0},{16,24},{24,16},{1,9},{9,1},{17,25},{25,17},{2,10},{10... | collective-permute-start | bytes 393224 | tf_op jit(solution)/shard_map/ppermute | solution.py:28
  129.1 10.0 %collective-permute-start.37 = (bf16[128,512]{1,0:T(8,128)(2,1)}, bf16[128,512]{1,0:T(8,128)(2,1)}, u32[]{:S(2)}, u32[]{:S(2)}) collective-permute-start(bf16[128,512]{1,0:T(8,128)(2,1)} %fusion.7), channel_id=1, source_target_pairs={{0,16},{8,24},{16,0},{24,8},{1,17},{9,25},{17,1},{25,9},{2,18},{10... | collective-permute-start | bytes 393224 | tf_op jit(solution)/shard_map/ppermute | solution.py:28

commit v4 on v3

--- a/solution.py
+++ b/solution.py
@@ -179,7 +179,17 @@
 
 
 def norm_kernel(
-    where_ref, hidden_ref, gain_ref, router_ref, id_ref, slot_ref, log_ref, own_ref, normed_ref
+    high,
+    where_ref,
+    hidden_ref,
+    gain_ref,
+    router_ref,
+    id_ref,
+    slot_ref,
+    log_ref,
+    own_ref,
+    known_ref,
+    normed_ref,
 ):
     rows, _ = hidden_ref.shape
     chunk = own_ref.shape[1]
@@ -189,6 +199,7 @@
     normed_ref[...] = normed
     start = pl.multiple_of(where_ref[0] * chunk, 128)
     own_ref[0:rows, :] = normed_ref[:, pl.ds(start, chunk)]
+    known_ref[...] = normed_ref[:, pl.ds(column_of(where_ref[0], high, 1, chunk // 2), chunk // 2)]
     logits = lax.dot_general(
         router_ref[...], normed, (((1,), (1,)), ((), ())), preferred_element_type=F32
     )
@@ -235,17 +246,20 @@
     return block[0:8, 0:128] + block[0:8, 128:256] + block[8:16, 0:128]
 
 
-def norm_share(where, chunk, hidden, gain, router, ids, slots, log_decay):
+def norm_share(where, high, chunk, hidden, gain, router, ids, slots, log_decay):
     rows, width = hidden.shape
     assert rows == 128 and chunk >= 512
     return staged_call(
-        norm_kernel,
+        functools.partial(norm_kernel, high),
         (where,),
         (),
         (hidden, gain, router, ids, slots, log_decay),
-        [jax.ShapeDtypeStruct((rows + 16, chunk), BF16)],
+        [
+            jax.ShapeDtypeStruct((rows + 16, chunk), BF16),
+            jax.ShapeDtypeStruct((rows, chunk // 2), BF16),
+        ],
         [pltpu.VMEM((rows, width), BF16)],
-    )[0]
+    )
 
 
 def expert_kernel(
@@ -440,11 +454,11 @@
 
 
 def gather_kernel(offsets, *refs):
-    where_ref, gate_up_ref, down_ref = refs[:3]
-    pieces = refs[3:19]
-    results = refs[19:23]
-    all_ref, rows_ref, hot_ref, weight_ref, wide_ref, tall_ref, info_ref = refs[23:30]
-    piece_sem, wide_sem, tall_sem, info_sem = refs[30:]
+    where_ref, info_ref, gate_up_ref, down_ref = refs[:4]
+    pieces = refs[4:20]
+    results = refs[20:24]
+    all_ref, rows_ref, hot_ref, weight_ref, wide_ref, tall_ref = refs[24:30]
+    piece_sem, wide_sem, tall_sem = refs[30:]
     me, first = where_ref[0], where_ref[1]
     pairs, local, places, width = rows_ref.shape
     tokens, half = all_ref.shape[2], pieces[0].shape[-1]
@@ -464,7 +478,7 @@
             for yi in range(2):
                 for h in range(2):
                     if h == 0:
-                        source = pieces[8 * g + 2 * core + yi].at[xo, :, 0:tokens]
+                        source = pieces[8 * g + 2 * core + yi].at[xo]
                     else:
                         source = pieces[8 * g + 4 + 2 * core + xo].at[yi]
                     column = column_of(me, offsets[core][yi], h, half)
@@ -475,22 +489,12 @@
                             piece_sem.at[len(copies)],
                         )
                     )
-    notes = [
-        pltpu.make_async_copy(
-            pieces[b // 4 * 8].at[b // 2 % 2, b % 2, tokens : tokens + 16],
-            info_ref.at[b],
-            info_sem.at[b],
-        )
-        for b in range(2 * pairs)
-    ]
-    for copy in notes + copies:
+    for copy in copies:
         copy.start()
     for slot in range(2):
         if slot < local:
             for copy in fetch(slot, slot):
                 copy.start()
-    for copy in notes:
-        copy.wait()
     for p in range(pairs):
         for e, (hot, weight) in enumerate(matches(info_ref, (2 * p, 2 * p + 1), first, local)):
             hot_ref[p, e] = hot
@@ -539,7 +543,7 @@
         )
 
 
-def experts_gather(offsets, where, pieces, gate_up, down):
+def experts_gather(offsets, where, info, pieces, gate_up, down):
     half = pieces[0].shape[-1]
     tokens = pieces[4].shape[-2]
     local, units, _, width = gate_up.shape
@@ -551,7 +555,7 @@
     return pl.pallas_call(
         functools.partial(gather_kernel, offsets),
         out_shape=[result] * 4,
-        in_specs=[smem, hbm, hbm] + [hbm] * len(pieces),
+        in_specs=[smem, vmem, hbm, hbm] + [hbm] * len(pieces),
         out_specs=[vmem] * 4,
         scratch_shapes=[
             pltpu.VMEM((pairs, 2, tokens, width), BF16),
@@ -560,15 +564,13 @@
             pltpu.VMEM((pairs, local, places, 128), F32),
             pltpu.VMEM((2, units, 2, width), BF16),
             pltpu.VMEM((2, units, width), BF16),
-            pltpu.VMEM((2 * pairs, 16, 2 * 128), BF16),
             pltpu.SemaphoreType.DMA((8 * pairs,)),
             pltpu.SemaphoreType.DMA((2,)),
             pltpu.SemaphoreType.DMA((2,)),
-            pltpu.SemaphoreType.DMA((2 * pairs,)),
         ],
         compiler_params=pltpu.CompilerParams(vmem_limit_bytes=44 * 1024 * 1024),
         name="experts",
-    )(where, gate_up, down, *pieces)
+    )(where, info, gate_up, down, *pieces)
 
 
 def group_bits():
@@ -578,17 +580,23 @@
     return far, near, side, high, core
 
 
-def spread_near(block):
+def spread_near(block, known=None):
     _, _, side, high, core = group_bits()
     half = block.shape[-1] // 2
     left, right = block[..., :half], block[..., :-16, half:]
-    left = jnp.stack([left, swap(left, EXP, side)])
-    right = jnp.stack([right, swap(right, TP, high)])
+    both = [left, swap(left, EXP, side)]
+    info = jnp.stack([b[..., -16:, :256] for b in both])
+    left = jnp.stack([b[..., :-16, :] for b in both])
+    if known is None:
+        other = swap(right, TP, high)
+    else:
+        other = jnp.concatenate([known[None], swap(right[1:], TP, high)])
+    right = jnp.stack([right, other])
     left2 = swap(left, TP, high)
     right2 = swap(right, EXP, side)
     first = [swap(left, TP, core), swap(right, TP, core)]
     second = [swap(left2, TP, core), swap(right2, TP, core)]
-    return [left, left2, first[0], second[0], right, right2, first[1], second[1]]
+    return [left, left2, first[0], second[0], right, right2, first[1], second[1]], info
 
 
 def fold(kept, sent, axis, bit):
@@ -882,8 +890,9 @@
     exp_stages = stages_of(EXP, bits_of(nx))
 
     where = jnp.stack([t, x * gate_up.shape[0], z * nx + x]).astype(jnp.int32)
-    own = norm_share(
+    own, known = norm_share(
         where,
+        bits_of(nt)[0],
         chunk,
         hidden_in,
         mlp_gain[None],
@@ -935,11 +944,11 @@
         return window_out, state_out, routed_out
 
     return in_groups(
-        where, own, kv, sent, state, query_heads, finish_args, gate_up, down_proj
-    )
-
-
-def in_groups(where, own, kv, sent, state, query_heads, finish_args, gate_up, down_proj):
+        where, own, known, kv, sent, state, query_heads, finish_args, gate_up, down_proj
+    )
+
+
+def in_groups(where, own, known, kv, sent, state, query_heads, finish_args, gate_up, down_proj):
     nz, nx = lax.axis_size(SEQ), lax.axis_size(EXP)
     heads = finish_args[2].shape[0]
     far, near, side, high, core = group_bits()
@@ -950,11 +959,9 @@
     kv_own = jnp.stack([kv, swap(kv, SEQ, far)])
     kv_own = jnp.stack([kv_own, swap(kv_own, SEQ, near)])
     there = jnp.stack([beyond, swap(beyond, SEQ, near)])
-    pieces_a = spread_near(here)
-    pieces_b = spread_near(there)
-    info_all = jnp.concatenate(
-        [p[0][..., -16:, :256].reshape(-1, 16, 256) for p in (pieces_a, pieces_b)], axis=0
-    )
+    pieces_a, info_a = spread_near(here, known)
+    pieces_b, info_b = spread_near(there)
+    info_all = jnp.stack([info_a, info_b]).reshape(-1, 16, 256)
     other = lax.ppermute(sent, *span_route(1))
     *entering, state, sent = scan_step(order, 1, heads, where, info_all, other, state)
     other2 = lax.ppermute(sent, *span_route(2))
@@ -962,7 +969,7 @@
 
     offsets = ((0, high), (core, core ^ high))
     keep_a, send_a, keep_b, send_b = experts_gather(
-        offsets, where, pieces_a + pieces_b, gate_up, down_proj
+        offsets, where, info_all, pieces_a + pieces_b, gate_up, down_proj
     )
 
     kept_b = fold(keep_b.astype(F32), send_b, TP, core)

time: 143 us -> 134 us (0.937)
  starting transfers between devices: 45.5 us -> 34.4 us
  waiting for transfers between devices: 57.5 us -> 59.4 us
    ppermute x35, starting transfers between devices: 40.6 us -> 28.3 us  [swap(): lax.ppermute(block, axis, [(i, i ^ bit) for i in range(lax.axis_size(axis...]
    ppermute x35, waiting for transfers between devices: 53.7 us -> 55.8 us  [swap(): lax.ppermute(block, axis, [(i, i ^ bit) for i in range(lax.axis_size(axis...]
  transfers between devices with their start and end apart: 38 -> 38, of which waited for: 18 -> 20; matrix products, arithmetic and copies ran while one was open for 3% -> 3% of each run, Pallas kernels for 8% -> 9%
where the time goes in v4:
time: 134 us; the launch traced here: 131 us
  waiting for transfers between devices  59.4 us (44%)
  starting transfers between devices  34.4 us (26%)
  Pallas kernels  31.2 us (23%)
  other arithmetic  4.46 us (3%)
    ppermute x35, waiting for transfers between devices, swap(): lax.ppermute(block, axis, [(i, i ^ bit) for i in range(lax.axis_size(axis...  55.8 us
    ppermute x35, starting transfers between devices, swap(): lax.ppermute(block, axis, [(i, i ^ bit) for i in range(lax.axis_size(axis...  28.3 us
    pallas_call x1, Pallas kernels, experts_gather(): pl.pallas_call(functools.partial(gather_kernel, offsets), out_shape=[resu...  17.4 us
    pallas_call x3, Pallas kernels, staged_call(): pl.pallas_call(kernel, out_shape=out_shape, in_specs=[smem] * len(scalars...  8.3 us
    ppermute x1, waiting for transfers between devices, in_groups(): other2 = lax.ppermute(sent, *span_route(2))  3.55 us
    ppermute x1, starting transfers between devices, in_groups(): other4 = lax.ppermute(sent, *span_route(4))  3.22 us
    pallas_call x2, Pallas kernels, attention(): pl.pallas_call(functools.partial(attention_kernel, offsets, begins, ends)...  3.1 us
  transfers between devices with their start and end apart: 38, of which 20 were waited for; matrix products, arithmetic and copies ran while one was open for 3% of the time, Pallas kernels for 9%

profile of v4, /device:TPU:0, one launch (start us, length us, event | category | flops | bytes accessed | tf_op | source)
XLA Modules:
  0.0 131.4 jit_solution(3061999585876652313)
XLA Ops:
  0.7 2.2 %shard_map.196 = (bf16[144,512]{1,0:T(8,128)(2,1)S(1)}, bf16[128,256]{1,0:T(8,128)(2,1)S(1)}) custom-call(s32[3]{0:T(128)S(1)} %pad_add_fusion.where_ref.refs_0_, bf16[128,2048]{1,0:T(8,128)(2,1)} %refs_1_.1, f32[1,2048]{1,0:T(1,128)} %bitcast.158, bf16[8,2048]{1,0:T(8,128)(2,1)} %bitcast.157, s32[2,128]{1,0:T(2,128)} %bitcast.161, s32[2,128]{1,0:T(2,128)} %bitcast.162, ...), custom_call_target="tpu_custom_call" | custom-call | tf_op jit(solution)/shard_map/pallas_call | solution.py:70
  2.9 3.1 %collective-permute-start.3 = (bf16[144,512]{1,0:T(8,128)(2,1)S(1)}, bf16[144,512]{1,0:T(8,128)(2,1)S(1)}, u32[]{:S(2)}, u32[]{:S(2)}) collective-permute-start(bf16[144,512]{1,0:T(8,128)(2,1)S(1)} %get-tuple-element.25), channel_id=1, source_target_pairs={{0,8},{8,0},{16,24},{24,16},{1,9},{9,1},{17,25},{25,17},{2,10},{10... | collective-permute-start | bytes 442376 | tf_op jit(solution)/shard_map/ppermute | solution.py:28
  6.0 2.6 %collective-permute-start.5 = (bf16[144,512]{1,0:T(8,128)(2,1)S(1)}, bf16[144,512]{1,0:T(8,128)(2,1)S(1)}, u32[]{:S(2)}, u32[]{:S(2)}) collective-permute-start(bf16[144,512]{1,0:T(8,128)(2,1)S(1)} %get-tuple-element.25), channel_id=1, source_target_pairs={{0,16},{8,24},{16,0},{24,8},{1,17},{9,25},{17,1},{25,9},{2,18},{10... | collective-permute-start | bytes 442376 | tf_op jit(solution)/shard_map/ppermute | solution.py:28
  8.6 3.8 %collective-permute-done.3 = bf16[144,512]{1,0:T(8,128)(2,1)S(1)} collective-permute-done((bf16[144,512]{1,0:T(8,128)(2,1)S(1)}, bf16[144,512]{1,0:T(8,128)(2,1)S(1)}, u32[]{:S(2)}, u32[]{:S(2)}) %collective-permute-start.3) | collective-permute-done | bytes 147488 | tf_op jit(solution)/shard_map/ppermute | solution.py:28
  12.5 1.9 %collective-permute-start.4 = (bf16[2,144,256]{2,1,0:T(8,128)(2,1)S(1)}, bf16[2,144,256]{2,1,0:T(8,128)(2,1)S(1)}, u32[]{:S(2)}, u32[]{:S(2)}) collective-permute-start(bf16[2,144,256]{2,1,0:T(8,128)(2,1)S(1)} %fusion.20), channel_id=1, source_target_pairs={{0,4},{4,0},{1,5},{5,1},{2,6},{6,2},{3,7},{7,3},{8,12},{12,8},{9,1... | collective-permute-start | bytes 442376 | tf_op jit(solution)/shard_map/ppermute | solution.py:28
  14.3 1.5 %collective-permute-start.14 = (bf16[1,128,256]{2,1,0:T(8,128)(2,1)S(1)}, bf16[1,128,256]{2,1,0:T(8,128)(2,1)S(1)}, u32[]{:S(2)}, u32[]{:S(2)}) collective-permute-start(bf16[1,128,256]{2,1,0:T(8,128)(2,1)S(1)} %slice.157), channel_id=1, source_target_pairs={{0,2},{1,3},{2,0},{3,1},{4,6},{5,7},{6,4},{7,5},{8,10},{9,11},{10,... | collective-permute-start | bytes 196616 | tf_op jit(solution)/shard_map/ppermute | solution.py:28
  16.0 2.6 %collective-permute-done.14 = bf16[1,128,256]{2,1,0:T(8,128)(2,1)S(1)} collective-permute-done((bf16[1,128,256]{2,1,0:T(8,128)(2,1)S(1)}, bf16[1,128,256]{2,1,0:T(8,128)(2,1)S(1)}, u32[]{:S(2)}, u32[]{:S(2)}) %collective-permute-start.14) | collective-permute-done | bytes 65568 | tf_op jit(solution)/shard_map/ppermute | solution.py:28
  18.7 0.3 collective-permute-start.15
  18.9 2.2 %collective-permute-done.6 = bf16[144,512]{1,0:T(8,128)(2,1)S(1)} collective-permute-done((bf16[144,512]{1,0:T(8,128)(2,1)S(1)}, bf16[144,512]{1,0:T(8,128)(2,1)S(1)}, u32[]{:S(2)}, u32[]{:S(2)}) %collective-permute-start.6) | collective-permute-done | bytes 147488 | tf_op jit(solution)/shard_map/ppermute | solution.py:28
  21.1 1.0 collective-permute-start.7
  22.2 1.6 %collective-permute-start.21 = (bf16[2,128,256]{2,1,0:T(8,128)(2,1)S(1)}, bf16[2,128,256]{2,1,0:T(8,128)(2,1)S(1)}, u32[]{:S(2)}, u32[]{:S(2)}) collective-permute-start(bf16[2,128,256]{2,1,0:T(8,128)(2,1)S(1)} %get-tuple-element.51), channel_id=1, source_target_pairs={{0,2},{1,3},{2,0},{3,1},{4,6},{5,7},{6,4},{7,5},{8,10},{9,11},{10,... | collective-permute-start | bytes 393224 | tf_op jit(solution)/shard_map/ppermute | solution.py:28
  23.8 0.6 collective-permute-start.11
  24.4 4.2 %collective-permute-done.21 = bf16[2,128,256]{2,1,0:T(8,128)(2,1)S(1)} collective-permute-done((bf16[2,128,256]{2,1,0:T(8,128)(2,1)S(1)}, bf16[2,128,256]{2,1,0:T(8,128)(2,1)S(1)}, u32[]{:S(2)}, u32[]{:S(2)}) %collective-permute-start.21) | collective-permute-done | bytes 131104 | tf_op jit(solution)/shard_map/ppermute | solution.py:28
  28.7 1.1 collective-permute-start.22
  29.8 0.3 collective-permute-start.23
  30.1 1.0 collective-permute-start.18
  31.1 1.0 collective-permute-done.11.refs_5_
  32.2 0.5 collective-permute-start.17
  32.7 4.7 %collective-permute-done.22.refs_17_ = bf16[2,2,128,256]{3,2,1,0:T(8,128)(2,1)S(1)} collective-permute-done((bf16[2,2,128,256]{3,2,1,0:T(8,128)(2,1)S(1)}, bf16[2,2,128,256]{3,2,1,0:T(8,128)(2,1)S(1)}, u32[]{:S(2)}, u32[]{:S(2)}) %collective-permute-start.22) | collective-permute-done | bytes 262176 | tf_op jit(solution)/shard_map/ppermute | solution.py:28
  37.4 0.5 collective-permute-start.24
  37.9 0.7 collective-permute-done.18.refs_13_
  38.7 0.3 collective-permute-done.13.refs_7_
  39.0 0.4 collective-permute-done.24.refs_19_
  39.3 0.8 collective-permute-done.20.refs_15_
  40.2 17.4 %experts.1 = (bf16[2,2,2,2,128,256]{5,4,3,2,1,0:T(8,128)(2,1)S(1)}, bf16[2,2,2,2,128,256]{5,4,3,2,1,0:T(8,128)(2,1)S(1)}, bf16[2,2,2,2,128,256]{5,4,3,2,1,0:T(8,...) custom-call(s32[3]{0:T(128)S(1)} %pad_add_fusion.where_ref.refs_0_, bf16[8,16,256]{2,1,0:T(8,128)(2,1)S(1)} %bitcast.122, ...), custom_call_target="tpu_custom_call" | custom-call | tf_op jit(solution)/shard_map/experts/pallas_call | solution.py:555
  57.6 0.2 collective-permute-start.25
  57.8 2.7 %shard_map.193 = (f32[128,1024]{1,0:T(8,128)S(1)}, f32[128,1024]{1,0:T(8,128)S(1)}, bf16[128,1024]{1,0:T(8,128)(2,1)S(1)}, bf16[512,128]{1,0:T(8,128)(2,1)S(1)}) custom-call(bf16[128,1024]{1,0:T(8,128)(2,1)} %refs_7_.1, bf16[256,128]{1,0:T(8,128)(2,1)} %bitcast.154, bf16[256,128]{1,0:T(8,128)(2,1)} %bitcast.145, f32[16,128]{1,0:T(8,128)} %bitcast.159, ...), custom_call_target="tpu_custom_call" | custom-call | tf_op jit(solution)/shard_map/pallas_call | solution.py:70
  60.4 1.3 collective-permute-start
  61.8 0.7 collective-permute-start.8
  62.5 7.5 %collective-permute-done = bf16[512,128]{1,0:T(8,128)(2,1)S(1)} collective-permute-done((bf16[512,128]{1,0:T(8,128)(2,1)S(1)}, bf16[512,128]{1,0:T(8,128)(2,1)S(1)}, u32[]{:S(2)}, u32[]{:S(2)}) %collective-permute-start) | collective-permute-done | bytes 131104 | tf_op jit(solution)/shard_map/ppermute | solution.py:28
  70.1 0.8 shard_map.197
  70.9 2.1 %collective-permute-start.9 = (bf16[128,1024]{1,0:T(8,128)(2,1)S(1)}, bf16[128,1024]{1,0:T(8,128)(2,1)S(1)}, u32[]{:S(2)}, u32[]{:S(2)}) collective-permute-start(bf16[128,1024]{1,0:T(8,128)(2,1)S(1)} %get-tuple-element.28), channel_id=1, source_target_pairs={{0,8},{8,0},{16,24},{24,16},{1,9},{9,1},{17,25},{25,17},{2,10},{10... | collective-permute-start | bytes 786440 | tf_op jit(solution)/shard_map/ppermute | solution.py:967
  73.0 6.3 %collective-permute-done.1 = bf16[2,512,128]{2,1,0:T(8,128)(2,1)S(1)} collective-permute-done((bf16[2,512,128]{2,1,0:T(8,128)(2,1)S(1)}, bf16[2,512,128]{2,1,0:T(8,128)(2,1)S(1)}, u32[]{:S(2)}, u32[]{:S(2)}) %collective-permute-start.1) | collective-permute-done | bytes 262176 | tf_op jit(solution)/shard_map/ppermute | solution.py:28
  79.3 0.9 collective-permute-start.2
  80.2 3.6 %collective-permute-done.9.other_ref = bf16[128,1024]{1,0:T(8,128)(2,1)S(1)} collective-permute-done((bf16[128,1024]{1,0:T(8,128)(2,1)S(1)}, bf16[128,1024]{1,0:T(8,128)(2,1)S(1)}, u32[]{:S(2)}, u32[]{:S(2)}) %collective-permute-start.9) | collective-permute-done | bytes 262176 | tf_op jit(solution)/shard_map/ppermute | solution.py:967
  83.8 1.6 %shard_map.198 = (f32[128,1024]{1,0:T(8,128)S(1)}, f32[128,1024]{1,0:T(8,128)}, bf16[128,1024]{1,0:T(8,128)(2,1)S(1)}) custom-call(s32[3]{0:T(128)S(1)} %pad_add_fusion.where_ref.refs_0_, bf16[8,16,256]{2,1,0:T(8,128)(2,1)S(1)} %bitcast.124, bf16[128,1024]{1,0:T(8,128)(2,1)S(1)} %collective-permute-done.9.other_ref, ...), custom_call_target="tpu_custom_call" | custom-call | tf_op jit(solution)/shard_map/pallas_call | solution.py:754
  85.4 3.2 %collective-permute-start.10 = (bf16[128,1024]{1,0:T(8,128)(2,1)S(1)}, bf16[128,1024]{1,0:T(8,128)(2,1)S(1)}, u32[]{:S(2)}, u32[]{:S(2)}) collective-permute-start(bf16[128,1024]{1,0:T(8,128)(2,1)S(1)} %get-tuple-element.31), channel_id=1, source_target_pairs={{0,16},{8,24},{1,17},{9,25},{2,18},{10,26},{3,19},{11,27},{4,20},{... | collective-permute-start | bytes 786440 | tf_op jit(solution)/shard_map/ppermute | solution.py:978
  88.7 0.3 fusion.33
  89.1 0.9 collective-permute-start.26
  90.0 1.4 %collective-permute-start.28 = (bf16[2,2,128,256]{3,2,1,0:T(8,128)(2,1)S(1)}, bf16[2,2,128,256]{3,2,1,0:T(8,128)(2,1)S(1)}, u32[]{:S(2)}, u32[]{:S(2)}) collective-permute-start(bf16[2,2,128,256]{3,2,1,0:T(8,128)(2,1)S(1)} %get-tuple-element.49), channel_id=1, source_target_pairs={{0,4},{4,0},{1,5},{5,1},{2,6},{6,2},{3,7},{7,3},{8,12},{12,8},{9,1... | collective-permute-start | bytes 786440 | tf_op jit(solution)/shard_map/ppermute | solution.py:28
  91.4 0.3 fusion.34
  91.8 0.6 collective-permute-start.32
  92.4 5.9 %collective-permute-done.26 = bf16[2,2,128,256]{3,2,1,0:T(8,128)(2,1)S(1)} collective-permute-done((bf16[2,2,128,256]{3,2,1,0:T(8,128)(2,1)S(1)}, bf16[2,2,128,256]{3,2,1,0:T(8,128)(2,1)S(1)}, u32[]{:S(2)}, u32[]{:S(2)}) %collective-permute-start.26) | collective-permute-done | bytes 262176 | tf_op jit(solution)/shard_map/ppermute | solution.py:28
  98.3 0.8 collective-permute-start.34
  99.2 1.6 %collective-permute-start.29 = (bf16[2,128,256]{2,1,0:T(8,128)(2,1)S(1)}, bf16[2,128,256]{2,1,0:T(8,128)(2,1)S(1)}, u32[]{:S(2)}, u32[]{:S(2)}) collective-permute-start(bf16[2,128,256]{2,1,0:T(8,128)(2,1)S(1)} %fusion.22), channel_id=1, source_target_pairs={{0,2},{1,3},{2,0},{3,1},{4,6},{5,7},{6,4},{7,5},{8,10},{9,11},{10,... | collective-permute-start | bytes 393224 | tf_op jit(solution)/shard_map/ppermute | solution.py:28
  100.8 2.8 %collective-permute-done.32 = bf16[2,2,128,256]{3,2,1,0:T(8,128)(2,1)S(1)} collective-permute-done((bf16[2,2,128,256]{3,2,1,0:T(8,128)(2,1)S(1)}, bf16[2,2,128,256]{3,2,1,0:T(8,128)(2,1)S(1)}, u32[]{:S(2)}, u32[]{:S(2)}) %collective-permute-start.32) | collective-permute-done | bytes 262176 | tf_op jit(solution)/shard_map/ppermute | solution.py:28
  103.6 0.8 collective-permute-start.27
  104.3 1.8 %collective-permute-done.34 = bf16[2,2,128,256]{3,2,1,0:T(8,128)(2,1)S(1)} collective-permute-done((bf16[2,2,128,256]{3,2,1,0:T(8,128)(2,1)S(1)}, bf16[2,2,128,256]{3,2,1,0:T(8,128)(2,1)S(1)}, u32[]{:S(2)}, u32[]{:S(2)}) %collective-permute-start.34) | collective-permute-done | bytes 262176 | tf_op jit(solution)/shard_map/ppermute | solution.py:28
  106.1 0.1 fusion
  106.2 0.9 collective-permute-start.35
  107.2 4.1 %collective-permute-done.35 = bf16[2,128,256]{2,1,0:T(8,128)(2,1)S(1)} collective-permute-done((bf16[2,128,256]{2,1,0:T(8,128)(2,1)S(1)}, bf16[2,128,256]{2,1,0:T(8,128)(2,1)S(1)}, u32[]{:S(2)}, u32[]{:S(2)}) %collective-permute-start.35) | collective-permute-done | bytes 131104 | tf_op jit(solution)/shard_map/ppermute | solution.py:28
  111.3 0.8 collective-permute-start.33
  112.1 4.2 %collective-permute-done.33 = bf16[2,128,256]{2,1,0:T(8,128)(2,1)S(1)} collective-permute-done((bf16[2,128,256]{2,1,0:T(8,128)(2,1)S(1)}, bf16[2,128,256]{2,1,0:T(8,128)(2,1)S(1)}, u32[]{:S(2)}, u32[]{:S(2)}) %collective-permute-start.33) | collective-permute-done | bytes 131104 | tf_op jit(solution)/shard_map/ppermute | solution.py:28
  116.3 1.8 %collective-permute-start.36 = (bf16[128,512]{1,0:T(8,128)(2,1)S(1)}, bf16[128,512]{1,0:T(8,128)(2,1)S(1)}, u32[]{:S(2)}, u32[]{:S(2)}) collective-permute-start(bf16[128,512]{1,0:T(8,128)(2,1)S(1)} %fusion.26), channel_id=1, source_target_pairs={{0,8},{8,0},{16,24},{24,16},{1,9},{9,1},{17,25},{25,17},{2,10},{10... | collective-permute-start | bytes 393224 | tf_op jit(solution)/shard_map/ppermute | solution.py:28
  118.2 0.7 fusion.23
  118.9 0.3 collective-permute-start.30
  119.1 2.3 %collective-permute-done.36 = bf16[128,512]{1,0:T(8,128)(2,1)S(1)} collective-permute-done((bf16[128,512]{1,0:T(8,128)(2,1)S(1)}, bf16[128,512]{1,0:T(8,128)(2,1)S(1)}, u32[]{:S(2)}, u32[]{:S(2)}) %collective-permute-start.36) | collective-permute-done | bytes 131104 | tf_op jit(solution)/shard_map/ppermute | solution.py:28
  121.5 0.7 fusion.7
  122.2 0.7 broadcast_in_dim_reshape.3.refs_9_
  122.9 1.2 shard_map.194
  124.1 1.9 %shard_map.195 = bf16[1024,128]{1,0:T(8,128)(2,1)} custom-call(s32[3]{0:T(128)S(1)} %pad_add_fusion.where_ref.refs_0_, bf16[1024,128]{1,0:T(8,128)(2,1)S(1)} %bitcast.130, bf16[4,512,128]{2,1,0:T(8,128)(2,1)S(1)} %bitcast.131, f32[1024,128]{1,0:T(8,128)S(1)} %get-tuple-element.22.refs_1_, f32[1024,128]{1,0:T(8,128)S(1)} %get-tuple-element.23.refs_2_, ...), custom_call_target="tpu_custom_call" | custom-call | tf_op jit(solution)/shard_map/pallas_call | solution.py:167
  126.0 3.5 %shard_map.199 = bf16[128,1024]{1,0:T(8,128)(2,1)} custom-call(s32[3]{0:T(128)S(1)} %pad_add_fusion.where_ref.refs_0_, bf16[8,16,256]{2,1,0:T(8,128)(2,1)S(1)} %bitcast.125, bf16[128,1024]{1,0:T(8,128)(2,1)S(1)} %collective-permute-done.10.refs_2_, f32[128,1024]{1,0:T(8,128)S(1)} %get-tuple-element.32.refs_3_, f32[128,1024]{1,0:T(8,128)S(1)} %get-tuple-element.33.refs_4_, ...), custom_call_target="tpu_custom_call" | custom-call | tf_op jit(solution)/shard_map/pallas_call | solution.py:70
  129.5 0.2 collective-permute-done.37
  129.7 1.7 %fusion.12 = bf16[128,512]{1,0:T(8,128)(2,1)} fusion(f32[2,128,256]{2,1,0:T(8,128)S(1)} %fusion.18, f32[2,128,256]{2,1,0:T(8,128)S(1)} %fusion.17, bf16[128,512]{1,0:T(8,128)(2,1)} %collective-permute-done.37, bf16[128,512]{1,0:T(8,128)(2,1)} %collective-permute-done.30), kind=kLoop, calls=%fused_computation.31 | loop fusion | flops 393216 | bytes 917504 | tf_op jit(solution)/shard_map/convert_element_type | solution.py:994
  (66 shorter events, 1.1 us)
Async XLA Ops:
  2.9 9.5 %collective-permute-start.3 = (bf16[144,512]{1,0:T(8,128)(2,1)S(1)}, bf16[144,512]{1,0:T(8,128)(2,1)S(1)}, u32[]{:S(2)}, u32[]{:S(2)}) collective-permute-start(bf16[144,512]{1,0:T(8,128)(2,1)S(1)} %get-tuple-element.25), channel_id=1, source_target_pairs={{0,8},{8,0},{16,24},{24,16},{1,9},{9,1},{17,25},{25,17},{2,10},{10... | collective-permute-start | bytes 442376 | tf_op jit(solution)/shard_map/ppermute | solution.py:28
  6.0 9.9 %collective-permute-start.5 = (bf16[144,512]{1,0:T(8,128)(2,1)S(1)}, bf16[144,512]{1,0:T(8,128)(2,1)S(1)}, u32[]{:S(2)}, u32[]{:S(2)}) collective-permute-start(bf16[144,512]{1,0:T(8,128)(2,1)S(1)} %get-tuple-element.25), channel_id=1, source_target_pairs={{0,16},{8,24},{16,0},{24,8},{1,17},{9,25},{17,1},{25,9},{2,18},{10... | collective-permute-start | bytes 442376 | tf_op jit(solution)/shard_map/ppermute | solution.py:28
  12.5 11.3 %collective-permute-start.4 = (bf16[2,144,256]{2,1,0:T(8,128)(2,1)S(1)}, bf16[2,144,256]{2,1,0:T(8,128)(2,1)S(1)}, u32[]{:S(2)}, u32[]{:S(2)}) collective-permute-start(bf16[2,144,256]{2,1,0:T(8,128)(2,1)S(1)} %fusion.20), channel_id=1, source_target_pairs={{0,4},{4,0},{1,5},{5,1},{2,6},{6,2},{3,7},{7,3},{8,12},{12,8},{9,1... | collective-permute-start | bytes 442376 | tf_op jit(solution)/shard_map/ppermute | solution.py:28
  14.3 4.3 %collective-permute-start.14 = (bf16[1,128,256]{2,1,0:T(8,128)(2,1)S(1)}, bf16[1,128,256]{2,1,0:T(8,128)(2,1)S(1)}, u32[]{:S(2)}, u32[]{:S(2)}) collective-permute-start(bf16[1,128,256]{2,1,0:T(8,128)(2,1)S(1)} %slice.157), channel_id=1, source_target_pairs={{0,2},{1,3},{2,0},{3,1},{4,6},{5,7},{6,4},{7,5},{8,10},{9,11},{10,... | collective-permute-start | bytes 196616 | tf_op jit(solution)/shard_map/ppermute | solution.py:28
  15.9 5.2 %collective-permute-start.6 = (bf16[144,512]{1,0:T(8,128)(2,1)S(1)}, bf16[144,512]{1,0:T(8,128)(2,1)S(1)}, u32[]{:S(2)}, u32[]{:S(2)}) collective-permute-start(bf16[144,512]{1,0:T(8,128)(2,1)S(1)} %collective-permute-done.5), channel_id=1, source_target_pairs={{0,8},{8,0},{16,24},{24,16},{1,9},{9,1},{17,25},{25,17},{2,10},{10... | collective-permute-start | bytes 442376 | tf_op jit(solution)/shard_map/ppermute | solution.py:28
  18.7 11.2 %collective-permute-start.15 = (bf16[2,2,128,256]{3,2,1,0:T(8,128)(2,1)S(1)}, bf16[2,2,128,256]{3,2,1,0:T(8,128)(2,1)S(1)}, u32[]{:S(2)}, u32[]{:S(2)}) collective-permute-start(bf16[2,2,128,256]{3,2,1,0:T(8,128)(2,1)S(1)} %pad_maximum_fusion.5.refs_8_), channel_id=1, source_target_pairs={{0,4},{4,0},{1,5},{5,1},{2,6},{6,2},{3,7},{7,3},{8,12},{12,8},{9,1... | collective-permute-start | bytes 786440 | tf_op jit(solution)/shard_map/ppermute | solution.py:28
  18.9 11.2 %collective-permute-start.16 = (bf16[2,2,128,256]{3,2,1,0:T(8,128)(2,1)S(1)}, bf16[2,2,128,256]{3,2,1,0:T(8,128)(2,1)S(1)}, u32[]{:S(2)}, u32[]{:S(2)}) collective-permute-start(bf16[2,2,128,256]{3,2,1,0:T(8,128)(2,1)S(1)} %pad_maximum_fusion.5.refs_8_), channel_id=1, source_target_pairs={{0,1},{1,0},{2,3},{3,2},{4,5},{5,4},{6,7},{7,6},{8,9},{9,8},{10,11... | collective-permute-start | bytes 786440 | tf_op jit(solution)/shard_map/ppermute | solution.py:28
  21.1 7.5 %collective-permute-start.7 = (bf16[2,144,256]{2,1,0:T(8,128)(2,1)S(1)}, bf16[2,144,256]{2,1,0:T(8,128)(2,1)S(1)}, u32[]{:S(2)}, u32[]{:S(2)}) collective-permute-start(bf16[2,144,256]{2,1,0:T(8,128)(2,1)S(1)} %fusion.19), channel_id=1, source_target_pairs={{0,4},{4,0},{1,5},{5,1},{2,6},{6,2},{3,7},{7,3},{8,12},{12,8},{9,1... | collective-permute-start | bytes 442376 | tf_op jit(solution)/shard_map/ppermute | solution.py:28
  22.2 6.4 %collective-permute-start.21 = (bf16[2,128,256]{2,1,0:T(8,128)(2,1)S(1)}, bf16[2,128,256]{2,1,0:T(8,128)(2,1)S(1)}, u32[]{:S(2)}, u32[]{:S(2)}) collective-permute-start(bf16[2,128,256]{2,1,0:T(8,128)(2,1)S(1)} %get-tuple-element.51), channel_id=1, source_target_pairs={{0,2},{1,3},{2,0},{3,1},{4,6},{5,7},{6,4},{7,5},{8,10},{9,11},{10,... | collective-permute-start | bytes 393224 | tf_op jit(solution)/shard_map/ppermute | solution.py:28
  23.8 8.4 %collective-permute-start.11 = (bf16[2,2,128,256]{3,2,1,0:T(8,128)(2,1)S(1)}, bf16[2,2,128,256]{3,2,1,0:T(8,128)(2,1)S(1)}, u32[]{:S(2)}, u32[]{:S(2)}) collective-permute-start(bf16[2,2,128,256]{3,2,1,0:T(8,128)(2,1)S(1)} %pad_maximum_fusion.4.refs_4_), channel_id=1, source_target_pairs={{0,2},{1,3},{2,0},{3,1},{4,6},{5,7},{6,4},{7,5},{8,10},{9,11},{10,... | collective-permute-start | bytes 786440 | tf_op jit(solution)/shard_map/ppermute | solution.py:28
  28.6 3.6 %collective-permute-start.12 = (bf16[2,2,128,256]{3,2,1,0:T(8,128)(2,1)S(1)}, bf16[2,2,128,256]{3,2,1,0:T(8,128)(2,1)S(1)}, u32[]{:S(2)}, u32[]{:S(2)}) collective-permute-start(bf16[2,2,128,256]{3,2,1,0:T(8,128)(2,1)S(1)} %pad_maximum_fusion.4.refs_4_), channel_id=1, source_target_pairs={{0,1},{1,0},{2,3},{3,2},{4,5},{5,4},{6,7},{7,6},{8,9},{9,8},{10,11... | collective-permute-start | bytes 786440 | tf_op jit(solution)/shard_map/ppermute | solution.py:28
  28.7 8.8 %collective-permute-start.22 = (bf16[2,2,128,256]{3,2,1,0:T(8,128)(2,1)S(1)}, bf16[2,2,128,256]{3,2,1,0:T(8,128)(2,1)S(1)}, u32[]{:S(2)}, u32[]{:S(2)}) collective-permute-start(bf16[2,2,128,256]{3,2,1,0:T(8,128)(2,1)S(1)} %pad_maximum_fusion.7.refs_16_), channel_id=1, source_target_pairs={{0,4},{4,0},{1,5},{5,1},{2,6},{6,2},{3,7},{7,3},{8,12},{12,8},{9,1... | collective-permute-start | bytes 786440 | tf_op jit(solution)/shard_map/ppermute | solution.py:28
  29.8 7.6 %collective-permute-start.23 = (bf16[2,2,128,256]{3,2,1,0:T(8,128)(2,1)S(1)}, bf16[2,2,128,256]{3,2,1,0:T(8,128)(2,1)S(1)}, u32[]{:S(2)}, u32[]{:S(2)}) collective-permute-start(bf16[2,2,128,256]{3,2,1,0:T(8,128)(2,1)S(1)} %pad_maximum_fusion.7.refs_16_), channel_id=1, source_target_pairs={{0,1},{1,0},{2,3},{3,2},{4,5},{5,4},{6,7},{7,6},{8,9},{9,8},{10,11... | collective-permute-start | bytes 786440 | tf_op jit(solution)/shard_map/ppermute | solution.py:28
  30.1 8.5 %collective-permute-start.18 = (bf16[2,2,128,256]{3,2,1,0:T(8,128)(2,1)S(1)}, bf16[2,2,128,256]{3,2,1,0:T(8,128)(2,1)S(1)}, u32[]{:S(2)}, u32[]{:S(2)}) collective-permute-start(bf16[2,2,128,256]{3,2,1,0:T(8,128)(2,1)S(1)} %pad_maximum_fusion.6.refs_12_), channel_id=1, source_target_pairs={{0,2},{1,3},{2,0},{3,1},{4,6},{5,7},{6,4},{7,5},{8,10},{9,11},{10,... | collective-permute-start | bytes 786440 | tf_op jit(solution)/shard_map/ppermute | solution.py:28
  32.2 6.5 %collective-permute-start.19 = (bf16[2,2,128,256]{3,2,1,0:T(8,128)(2,1)S(1)}, bf16[2,2,128,256]{3,2,1,0:T(8,128)(2,1)S(1)}, u32[]{:S(2)}, u32[]{:S(2)}) collective-permute-start(bf16[2,2,128,256]{3,2,1,0:T(8,128)(2,1)S(1)} %pad_maximum_fusion.6.refs_12_), channel_id=1, source_target_pairs={{0,1},{1,0},{2,3},{3,2},{4,5},{5,4},{6,7},{7,6},{8,9},{9,8},{10,11... | collective-permute-start | bytes 786440 | tf_op jit(solution)/shard_map/ppermute | solution.py:28
  32.2 6.5 %collective-permute-start.17 = (bf16[2,2,128,256]{3,2,1,0:T(8,128)(2,1)S(1)}, bf16[2,2,128,256]{3,2,1,0:T(8,128)(2,1)S(1)}, u32[]{:S(2)}, u32[]{:S(2)}) collective-permute-start(bf16[2,2,128,256]{3,2,1,0:T(8,128)(2,1)S(1)} %collective-permute-done.15.refs_9_), channel_id=1, source_target_pairs={{0,1},{1,0},{2,3},{3,2},{4,5},{5,4},{6,7},{7,6},{8,9},{9,8},{10,11... | collective-permute-start | bytes 786440 | tf_op jit(solution)/shard_map/ppermute | solution.py:28
  37.4 1.5 %collective-permute-start.13 = (bf16[2,2,128,256]{3,2,1,0:T(8,128)(2,1)S(1)}, bf16[2,2,128,256]{3,2,1,0:T(8,128)(2,1)S(1)}, u32[]{:S(2)}, u32[]{:S(2)}) collective-permute-start(bf16[2,2,128,256]{3,2,1,0:T(8,128)(2,1)S(1)} %collective-permute-done.11.refs_5_), channel_id=1, source_target_pairs={{0,1},{1,0},{2,3},{3,2},{4,5},{5,4},{6,7},{7,6},{8,9},{9,8},{10,11... | collective-permute-start | bytes 786440 | tf_op jit(solution)/shard_map/ppermute | solution.py:28
  37.4 1.9 %collective-permute-start.24 = (bf16[2,2,128,256]{3,2,1,0:T(8,128)(2,1)S(1)}, bf16[2,2,128,256]{3,2,1,0:T(8,128)(2,1)S(1)}, u32[]{:S(2)}, u32[]{:S(2)}) collective-permute-start(bf16[2,2,128,256]{3,2,1,0:T(8,128)(2,1)S(1)} %collective-permute-done.22.refs_17_), channel_id=1, source_target_pairs={{0,1},{1,0},{2,3},{3,2},{4,5},{5,4},{6,7},{7,6},{8,9},{9,8},{10,11... | collective-permute-start | bytes 786440 | tf_op jit(solution)/shard_map/ppermute | solution.py:28
  38.6 1.5 %collective-permute-start.20 = (bf16[2,2,128,256]{3,2,1,0:T(8,128)(2,1)S(1)}, bf16[2,2,128,256]{3,2,1,0:T(8,128)(2,1)S(1)}, u32[]{:S(2)}, u32[]{:S(2)}) collective-permute-start(bf16[2,2,128,256]{3,2,1,0:T(8,128)(2,1)S(1)} %collective-permute-done.18.refs_13_), channel_id=1, source_target_pairs={{0,1},{1,0},{2,3},{3,2},{4,5},{5,4},{6,7},{7,6},{8,9},{9,8},{10,11... | collective-permute-start | bytes 786440 | tf_op jit(solution)/shard_map/ppermute | solution.py:28
  57.6 31.1 %collective-permute-start.25 = (bf16[2,2,2,2,128,256]{5,4,3,2,1,0:T(8,128)(2,1)S(1)}, bf16[2,2,2,2,128,256]{5,4,3,2,1,0:T(8,128)(2,1)S(1)}, u32[]{:S(2)}, u32[]{:S(2)}) collective-permute-start(bf16[2,2,2,2,128,256]{5,4,3,2,1,0:T(8,128)(2,1)S(1)} %get-tuple-element.36), channel_id=1, source_target_pairs={{0,1},{1,0},{2,3},{3,2},{4,5},{5,4},{6,7},{7,6},{8,9},{9,8},{10,11... | collective-permute-start | bytes 3145736 | tf_op jit(solution)/shard_map/ppermute | solution.py:28
  60.4 9.5 %collective-permute-start = (bf16[512,128]{1,0:T(8,128)(2,1)S(1)}, bf16[512,128]{1,0:T(8,128)(2,1)S(1)}, u32[]{:S(2)}, u32[]{:S(2)}) collective-permute-start(bf16[512,128]{1,0:T(8,128)(2,1)S(1)} %get-tuple-element.21), channel_id=1, source_target_pairs={{0,16},{8,24},{16,0},{24,8},{1,17},{9,25},{17,1},{25,9},{2,18},{10... | collective-permute-start | bytes 393224 | tf_op jit(solution)/shard_map/ppermute | solution.py:28
  61.8 8.4 %collective-permute-start.8 = (bf16[128,1024]{1,0:T(8,128)(2,1)S(1)}, bf16[128,1024]{1,0:T(8,128)(2,1)S(1)}, u32[]{:S(2)}, u32[]{:S(2)}) collective-permute-start(bf16[128,1024]{1,0:T(8,128)(2,1)S(1)} %get-tuple-element.26), channel_id=1, source_target_pairs={{0,4},{4,0},{1,5},{5,1},{2,6},{6,2},{3,7},{7,3},{8,12},{12,8},{9,1... | collective-permute-start | bytes 786440 | tf_op jit(solution)/shard_map/ppermute | solution.py:965
  62.5 28.9 %collective-permute-start.31 = (bf16[2,2,2,2,128,256]{5,4,3,2,1,0:T(8,128)(2,1)S(1)}, bf16[2,2,2,2,128,256]{5,4,3,2,1,0:T(8,128)(2,1)S(1)}, u32[]{:S(2)}, u32[]{:S(2)}) collective-permute-start(bf16[2,2,2,2,128,256]{5,4,3,2,1,0:T(8,128)(2,1)S(1)} %get-tuple-element.38), channel_id=1, source_target_pairs={{0,1},{1,0},{2,3},{3,2},{4,5},{5,4},{6,7},{7,6},{8,9},{9,8},{10,11... | collective-permute-start | bytes 3145736 | tf_op jit(solution)/shard_map/ppermute | solution.py:28
  70.0 9.2 %collective-permute-start.1 = (bf16[2,512,128]{2,1,0:T(8,128)(2,1)S(1)}, bf16[2,512,128]{2,1,0:T(8,128)(2,1)S(1)}, u32[]{:S(2)}, u32[]{:S(2)}) collective-permute-start(bf16[2,512,128]{2,1,0:T(8,128)(2,1)S(1)} %get-tuple-element.56), channel_id=1, source_target_pairs={{0,8},{8,0},{16,24},{24,16},{1,9},{9,1},{17,25},{25,17},{2,10},{10... | collective-permute-start | bytes 786440 | tf_op jit(solution)/shard_map/ppermute | solution.py:28
  70.9 12.9 %collective-permute-start.9 = (bf16[128,1024]{1,0:T(8,128)(2,1)S(1)}, bf16[128,1024]{1,0:T(8,128)(2,1)S(1)}, u32[]{:S(2)}, u32[]{:S(2)}) collective-permute-start(bf16[128,1024]{1,0:T(8,128)(2,1)S(1)} %get-tuple-element.28), channel_id=1, source_target_pairs={{0,8},{8,0},{16,24},{24,16},{1,9},{9,1},{17,25},{25,17},{2,10},{10... | collective-permute-start | bytes 786440 | tf_op jit(solution)/shard_map/ppermute | solution.py:967
  79.3 44.8 %collective-permute-start.2 = (bf16[2,2,512,128]{3,2,1,0:T(8,128)(2,1)S(1)}, bf16[2,2,512,128]{3,2,1,0:T(8,128)(2,1)S(1)}, u32[]{:S(2)}, u32[]{:S(2)}) collective-permute-start(bf16[2,2,512,128]{3,2,1,0:T(8,128)(2,1)S(1)} %pad_maximum_fusion), channel_id=1, source_target_pairs={{0,4},{4,0},{1,5},{5,1},{2,6},{6,2},{3,7},{7,3},{8,12},{12,8},{9,1... | collective-permute-start | bytes 1572872 | tf_op jit(solution)/shard_map/ppermute | solution.py:28
  85.4 40.6 %collective-permute-start.10 = (bf16[128,1024]{1,0:T(8,128)(2,1)S(1)}, bf16[128,1024]{1,0:T(8,128)(2,1)S(1)}, u32[]{:S(2)}, u32[]{:S(2)}) collective-permute-start(bf16[128,1024]{1,0:T(8,128)(2,1)S(1)} %get-tuple-element.31), channel_id=1, source_target_pairs={{0,16},{8,24},{1,17},{9,25},{2,18},{10,26},{3,19},{11,27},{4,20},{... | collective-permute-start | bytes 786440 | tf_op jit(solution)/shard_map/ppermute | solution.py:978
  89.1 9.2 %collective-permute-start.26 = (bf16[2,2,128,256]{3,2,1,0:T(8,128)(2,1)S(1)}, bf16[2,2,128,256]{3,2,1,0:T(8,128)(2,1)S(1)}, u32[]{:S(2)}, u32[]{:S(2)}) collective-permute-start(bf16[2,2,128,256]{3,2,1,0:T(8,128)(2,1)S(1)} %get-tuple-element.50), channel_id=1, source_target_pairs={{0,2},{1,3},{2,0},{3,1},{4,6},{5,7},{6,4},{7,5},{8,10},{9,11},{10,... | collective-permute-start | bytes 786440 | tf_op jit(solution)/shard_map/ppermute | solution.py:28
  90.0 9.1 %collective-permute-start.28 = (bf16[2,2,128,256]{3,2,1,0:T(8,128)(2,1)S(1)}, bf16[2,2,128,256]{3,2,1,0:T(8,128)(2,1)S(1)}, u32[]{:S(2)}, u32[]{:S(2)}) collective-permute-start(bf16[2,2,128,256]{3,2,1,0:T(8,128)(2,1)S(1)} %get-tuple-element.49), channel_id=1, source_target_pairs={{0,4},{4,0},{1,5},{5,1},{2,6},{6,2},{3,7},{7,3},{8,12},{12,8},{9,1... | collective-permute-start | bytes 786440 | tf_op jit(solution)/shard_map/ppermute | solution.py:28
  91.8 11.8 %collective-permute-start.32 = (bf16[2,2,128,256]{3,2,1,0:T(8,128)(2,1)S(1)}, bf16[2,2,128,256]{3,2,1,0:T(8,128)(2,1)S(1)}, u32[]{:S(2)}, u32[]{:S(2)}) collective-permute-start(bf16[2,2,128,256]{3,2,1,0:T(8,128)(2,1)S(1)} %get-tuple-element.48), channel_id=1, source_target_pairs={{0,2},{1,3},{2,0},{3,1},{4,6},{5,7},{6,4},{7,5},{8,10},{9,11},{10,... | collective-permute-start | bytes 786440 | tf_op jit(solution)/shard_map/ppermute | solution.py:28
  98.3 7.8 %collective-permute-start.34 = (bf16[2,2,128,256]{3,2,1,0:T(8,128)(2,1)S(1)}, bf16[2,2,128,256]{3,2,1,0:T(8,128)(2,1)S(1)}, u32[]{:S(2)}, u32[]{:S(2)}) collective-permute-start(bf16[2,2,128,256]{3,2,1,0:T(8,128)(2,1)S(1)} %get-tuple-element.47), channel_id=1, source_target_pairs={{0,4},{4,0},{1,5},{5,1},{2,6},{6,2},{3,7},{7,3},{8,12},{12,8},{9,1... | collective-permute-start | bytes 786440 | tf_op jit(solution)/shard_map/ppermute | solution.py:28
  99.2 18.9 %collective-permute-start.29 = (bf16[2,128,256]{2,1,0:T(8,128)(2,1)S(1)}, bf16[2,128,256]{2,1,0:T(8,128)(2,1)S(1)}, u32[]{:S(2)}, u32[]{:S(2)}) collective-permute-start(bf16[2,128,256]{2,1,0:T(8,128)(2,1)S(1)} %fusion.22), channel_id=1, source_target_pairs={{0,2},{1,3},{2,0},{3,1},{4,6},{5,7},{6,4},{7,5},{8,10},{9,11},{10,... | collective-permute-start | bytes 393224 | tf_op jit(solution)/shard_map/ppermute | solution.py:28
  103.6 14.6 %collective-permute-start.27 = (bf16[2,128,256]{2,1,0:T(8,128)(2,1)S(1)}, bf16[2,128,256]{2,1,0:T(8,128)(2,1)S(1)}, u32[]{:S(2)}, u32[]{:S(2)}) collective-permute-start(bf16[2,128,256]{2,1,0:T(8,128)(2,1)S(1)} %fusion.21), channel_id=1, source_target_pairs={{0,4},{4,0},{1,5},{5,1},{2,6},{6,2},{3,7},{7,3},{8,12},{12,8},{9,1... | collective-permute-start | bytes 393224 | tf_op jit(solution)/shard_map/ppermute | solution.py:28
  106.2 5.0 %collective-permute-start.35 = (bf16[2,128,256]{2,1,0:T(8,128)(2,1)S(1)}, bf16[2,128,256]{2,1,0:T(8,128)(2,1)S(1)}, u32[]{:S(2)}, u32[]{:S(2)}) collective-permute-start(bf16[2,128,256]{2,1,0:T(8,128)(2,1)S(1)} %fusion.25), channel_id=1, source_target_pairs={{0,2},{1,3},{2,0},{3,1},{4,6},{5,7},{6,4},{7,5},{8,10},{9,11},{10,... | collective-permute-start | bytes 393224 | tf_op jit(solution)/shard_map/ppermute | solution.py:28
  111.3 5.0 %collective-permute-start.33 = (bf16[2,128,256]{2,1,0:T(8,128)(2,1)S(1)}, bf16[2,128,256]{2,1,0:T(8,128)(2,1)S(1)}, u32[]{:S(2)}, u32[]{:S(2)}) collective-permute-start(bf16[2,128,256]{2,1,0:T(8,128)(2,1)S(1)} %fusion.24), channel_id=1, source_target_pairs={{0,4},{4,0},{1,5},{5,1},{2,6},{6,2},{3,7},{7,3},{8,12},{12,8},{9,1... | collective-permute-start | bytes 393224 | tf_op jit(solution)/shard_map/ppermute | solution.py:28
  112.1 10.1 %copy-start.1 = (f32[16]{0:T(128)S(1)}, f32[16]{0:T(128)}, u32[]{:S(2)}) copy-start(f32[16]{0:T(128)} %param.27) | copy-start | bytes 196
  112.1 10.8 %copy-start = (bf16[128,8,128]{2,1,0:T(8,128)(2,1)S(1)}, bf16[128,8,128]{2,1,0:T(8,128)(2,1)}, u32[]{:S(2)}) copy-start(bf16[128,8,128]{2,1,0:T(8,128)(2,1)} %param.18) | copy-start | bytes 786436
  116.3 5.1 %collective-permute-start.36 = (bf16[128,512]{1,0:T(8,128)(2,1)S(1)}, bf16[128,512]{1,0:T(8,128)(2,1)S(1)}, u32[]{:S(2)}, u32[]{:S(2)}) collective-permute-start(bf16[128,512]{1,0:T(8,128)(2,1)S(1)} %fusion.26), channel_id=1, source_target_pairs={{0,8},{8,0},{16,24},{24,16},{1,9},{9,1},{17,25},{25,17},{2,10},{10... | collective-permute-start | bytes 393224 | tf_op jit(solution)/shard_map/ppermute | solution.py:28
  118.9 10.6 %collective-permute-start.30 = (bf16[128,512]{1,0:T(8,128)(2,1)}, bf16[128,512]{1,0:T(8,128)(2,1)}, u32[]{:S(2)}, u32[]{:S(2)}) collective-permute-start(bf16[128,512]{1,0:T(8,128)(2,1)} %fusion.23), channel_id=1, source_target_pairs={{0,8},{8,0},{16,24},{24,16},{1,9},{9,1},{17,25},{25,17},{2,10},{10... | collective-permute-start | bytes 393224 | tf_op jit(solution)/shard_map/ppermute | solution.py:28
  122.1 7.6 %collective-permute-start.37 = (bf16[128,512]{1,0:T(8,128)(2,1)}, bf16[128,512]{1,0:T(8,128)(2,1)}, u32[]{:S(2)}, u32[]{:S(2)}) collective-permute-start(bf16[128,512]{1,0:T(8,128)(2,1)} %fusion.7), channel_id=1, source_target_pairs={{0,16},{8,24},{16,0},{24,8},{1,17},{9,25},{17,1},{25,9},{2,18},{10... | collective-permute-start | bytes 393224 | tf_op jit(solution)/shard_map/ppermute | solution.py:28

commit v5 on v4

--- a/solution.py
+++ b/solution.py
@@ -777,15 +777,17 @@
     width = channels // groups
     grown = jnp.exp(running_sum(log_ref, rows, True))
     lead, _, _ = decay_between(where_ref[2], total_ref, order, span, heads)
+    skip = lanes_of(skip_ref[...], heads)
     left = lax.broadcasted_iota(jnp.int32, (rows, 2 * HP), 1) < HP
     for g in range(groups):
         columns = slice(g * width, (g + 1) * width)
-        inter = jnp.dot(
-            group_rows(readout_ref, g, groups),
-            lead[:, columns] * other_ref[:, columns].astype(F32) + entering_ref[:, columns],
-            precision=HIGHEST,
-            preferred_element_type=F32,
-        )
+        reader = group_rows(readout_ref, g, groups).astype(BF16)
+        rest = lead[:, columns] * other_ref[:, columns].astype(F32) + entering_ref[:, columns]
+        inter = 0.0
+        for _ in range(3):
+            part = rest.astype(BF16)
+            rest = rest - part.astype(F32)
+            inter = inter + jnp.dot(reader, part, preferred_element_type=F32)
         first = g * (heads // groups)
         factor = jnp.concatenate(
             [
@@ -797,7 +799,7 @@
         mixed = (
             intra_ref[:, columns]
             + factor * inter
-            + skip_ref[:, columns] * input_ref[:, columns].astype(F32)
+            + skip[:, columns] * input_ref[:, columns].astype(F32)
         )
         gate = gate_ref[:, columns].astype(F32)
         gated = mixed * (gate / (1.0 + jnp.exp(-gate)))
@@ -919,7 +921,7 @@
         log_decay.T,
         state_input,
         state_gate,
-        jnp.repeat(skip_scale, HP)[None],
+        skip_scale[None],
         state_gain[None],
     )
 

time: 134 us -> 132 us (0.985); the launches traced: 131 us -> 131 us
  starting transfers between devices: 34.4 us -> 42 us
  waiting for transfers between devices: 59.4 us -> 55 us
  other arithmetic: 4.46 us -> 2.21 us
    ppermute x35, starting transfers between devices: 28.3 us -> 35.2 us  [swap(): lax.ppermute(block, axis, [(i, i ^ bit) for i in range(lax.axis_size(axis...]
    ppermute x35, waiting for transfers between devices: 55.8 us -> 51.1 us  [swap(): lax.ppermute(block, axis, [(i, i ^ bit) for i in range(lax.axis_size(axis...]
  transfers between devices with their start and end apart: 38 -> 38, of which waited for: 20 -> 19; matrix products, arithmetic and copies ran while one was open for 3% -> 1% of each run, Pallas kernels for 9% -> 9%
where the time goes in v5:
time: 132 us; the launch traced here: 131 us
  waiting for transfers between devices  55 us (42%)
  starting transfers between devices  42 us (32%)
  Pallas kernels  31.1 us (24%)
  other arithmetic  2.21 us (2%)
    ppermute x35, waiting for transfers between devices, swap(): lax.ppermute(block, axis, [(i, i ^ bit) for i in range(lax.axis_size(axis...  51.1 us
    ppermute x35, starting transfers between devices, swap(): lax.ppermute(block, axis, [(i, i ^ bit) for i in range(lax.axis_size(axis...  35.2 us
    pallas_call x1, Pallas kernels, experts_gather(): pl.pallas_call(functools.partial(gather_kernel, offsets), out_shape=[resu...  17.4 us
    pallas_call x3, Pallas kernels, staged_call(): pl.pallas_call(kernel, out_shape=out_shape, in_specs=[smem] * len(scalars...  8.19 us
    ppermute x1, waiting for transfers between devices, in_groups(): other2 = lax.ppermute(sent, *span_route(2))  3.74 us
    ppermute x1, starting transfers between devices, in_groups(): other4 = lax.ppermute(sent, *span_route(4))  3.47 us
    pallas_call x2, Pallas kernels, attention(): pl.pallas_call(functools.partial(attention_kernel, offsets, begins, ends)...  3.1 us
  transfers between devices with their start and end apart: 38, of which 19 were waited for; matrix products, arithmetic and copies ran while one was open for 1% of the time, Pallas kernels for 9%

profile of v5, /device:TPU:0, one launch (start us, length us, event | category | flops | bytes accessed | tf_op | source)
XLA Modules:
  0.0 131.5 jit_solution(5947921853425005928)
XLA Ops:
  0.6 0.1 pad_add_fusion.where_ref.refs_0_
  0.7 2.2 %shard_map.196 = (bf16[144,512]{1,0:T(8,128)(2,1)S(1)}, bf16[128,256]{1,0:T(8,128)(2,1)S(1)}) custom-call(s32[3]{0:T(128)S(1)} %pad_add_fusion.where_ref.refs_0_, bf16[128,2048]{1,0:T(8,128)(2,1)} %refs_1_.1, f32[1,2048]{1,0:T(1,128)} %bitcast.159, bf16[8,2048]{1,0:T(8,128)(2,1)} %bitcast.158, s32[2,128]{1,0:T(2,128)} %bitcast.162, s32[2,128]{1,0:T(2,128)} %bitcast.163, ...), custom_call_target="tpu_custom_call" | custom-call | tf_op jit(solution)/shard_map/pallas_call | solution.py:70
  2.9 3.1 %collective-permute-start.3 = (bf16[144,512]{1,0:T(8,128)(2,1)S(1)}, bf16[144,512]{1,0:T(8,128)(2,1)S(1)}, u32[]{:S(2)}, u32[]{:S(2)}) collective-permute-start(bf16[144,512]{1,0:T(8,128)(2,1)S(1)} %get-tuple-element.25), channel_id=1, source_target_pairs={{0,8},{8,0},{16,24},{24,16},{1,9},{9,1},{17,25},{25,17},{2,10},{10... | collective-permute-start | bytes 442376 | tf_op jit(solution)/shard_map/ppermute | solution.py:28
  6.0 2.6 %collective-permute-start.5 = (bf16[144,512]{1,0:T(8,128)(2,1)S(1)}, bf16[144,512]{1,0:T(8,128)(2,1)S(1)}, u32[]{:S(2)}, u32[]{:S(2)}) collective-permute-start(bf16[144,512]{1,0:T(8,128)(2,1)S(1)} %get-tuple-element.25), channel_id=1, source_target_pairs={{0,16},{8,24},{16,0},{24,8},{1,17},{9,25},{17,1},{25,9},{2,18},{10... | collective-permute-start | bytes 442376 | tf_op jit(solution)/shard_map/ppermute | solution.py:28
  8.6 3.8 %collective-permute-done.3 = bf16[144,512]{1,0:T(8,128)(2,1)S(1)} collective-permute-done((bf16[144,512]{1,0:T(8,128)(2,1)S(1)}, bf16[144,512]{1,0:T(8,128)(2,1)S(1)}, u32[]{:S(2)}, u32[]{:S(2)}) %collective-permute-start.3) | collective-permute-done | bytes 147488 | tf_op jit(solution)/shard_map/ppermute | solution.py:28
  12.4 1.8 %collective-permute-start.14 = (bf16[1,128,256]{2,1,0:T(8,128)(2,1)S(1)}, bf16[1,128,256]{2,1,0:T(8,128)(2,1)S(1)}, u32[]{:S(2)}, u32[]{:S(2)}) collective-permute-start(bf16[1,128,256]{2,1,0:T(8,128)(2,1)S(1)} %slice.157), channel_id=1, source_target_pairs={{0,2},{1,3},{2,0},{3,1},{4,6},{5,7},{6,4},{7,5},{8,10},{9,11},{10,... | collective-permute-start | bytes 196616 | tf_op jit(solution)/shard_map/ppermute | solution.py:28
  14.3 1.6 %collective-permute-start.4 = (bf16[2,144,256]{2,1,0:T(8,128)(2,1)S(1)}, bf16[2,144,256]{2,1,0:T(8,128)(2,1)S(1)}, u32[]{:S(2)}, u32[]{:S(2)}) collective-permute-start(bf16[2,144,256]{2,1,0:T(8,128)(2,1)S(1)} %fusion.20), channel_id=1, source_target_pairs={{0,4},{4,0},{1,5},{5,1},{2,6},{6,2},{3,7},{7,3},{8,12},{12,8},{9,1... | collective-permute-start | bytes 442376 | tf_op jit(solution)/shard_map/ppermute | solution.py:28
  16.0 0.7 collective-permute-done.14
  16.8 0.1 collective-permute-start.16
  16.8 1.9 %collective-permute-start.15 = (bf16[2,2,128,256]{3,2,1,0:T(8,128)(2,1)S(1)}, bf16[2,2,128,256]{3,2,1,0:T(8,128)(2,1)S(1)}, u32[]{:S(2)}, u32[]{:S(2)}) collective-permute-start(bf16[2,2,128,256]{3,2,1,0:T(8,128)(2,1)S(1)} %pad_maximum_fusion.5.refs_8_), channel_id=1, source_target_pairs={{0,4},{4,0},{1,5},{5,1},{2,6},{6,2},{3,7},{7,3},{8,12},{12,8},{9,1... | collective-permute-start | bytes 786440 | tf_op jit(solution)/shard_map/ppermute | solution.py:28
  18.7 2.4 %collective-permute-done.6 = bf16[144,512]{1,0:T(8,128)(2,1)S(1)} collective-permute-done((bf16[144,512]{1,0:T(8,128)(2,1)S(1)}, bf16[144,512]{1,0:T(8,128)(2,1)S(1)}, u32[]{:S(2)}, u32[]{:S(2)}) %collective-permute-start.6) | collective-permute-done | bytes 147488 | tf_op jit(solution)/shard_map/ppermute | solution.py:28
  21.1 1.1 collective-permute-start.21
  22.2 1.6 %collective-permute-start.7 = (bf16[2,144,256]{2,1,0:T(8,128)(2,1)S(1)}, bf16[2,144,256]{2,1,0:T(8,128)(2,1)S(1)}, u32[]{:S(2)}, u32[]{:S(2)}) collective-permute-start(bf16[2,144,256]{2,1,0:T(8,128)(2,1)S(1)} %fusion.19), channel_id=1, source_target_pairs={{0,4},{4,0},{1,5},{5,1},{2,6},{6,2},{3,7},{7,3},{8,12},{12,8},{9,1... | collective-permute-start | bytes 442376 | tf_op jit(solution)/shard_map/ppermute | solution.py:28
  23.9 2.3 %collective-permute-done.21 = bf16[2,128,256]{2,1,0:T(8,128)(2,1)S(1)} collective-permute-done((bf16[2,128,256]{2,1,0:T(8,128)(2,1)S(1)}, bf16[2,128,256]{2,1,0:T(8,128)(2,1)S(1)}, u32[]{:S(2)}, u32[]{:S(2)}) %collective-permute-start.21) | collective-permute-done | bytes 131104 | tf_op jit(solution)/shard_map/ppermute | solution.py:28
  26.2 1.0 collective-permute-start.11
  27.2 1.6 %collective-permute-done.7 = bf16[2,144,256]{2,1,0:T(8,128)(2,1)S(1)} collective-permute-done((bf16[2,144,256]{2,1,0:T(8,128)(2,1)S(1)}, bf16[2,144,256]{2,1,0:T(8,128)(2,1)S(1)}, u32[]{:S(2)}, u32[]{:S(2)}) %collective-permute-start.7) | collective-permute-done | bytes 147488 | tf_op jit(solution)/shard_map/ppermute | solution.py:28
  28.8 1.8 %collective-permute-start.22 = (bf16[2,2,128,256]{3,2,1,0:T(8,128)(2,1)S(1)}, bf16[2,2,128,256]{3,2,1,0:T(8,128)(2,1)S(1)}, u32[]{:S(2)}, u32[]{:S(2)}) collective-permute-start(bf16[2,2,128,256]{3,2,1,0:T(8,128)(2,1)S(1)} %pad_maximum_fusion.7.refs_16_), channel_id=1, source_target_pairs={{0,4},{4,0},{1,5},{5,1},{2,6},{6,2},{3,7},{7,3},{8,12},{12,8},{9,1... | collective-permute-start | bytes 786440 | tf_op jit(solution)/shard_map/ppermute | solution.py:28
  30.6 1.5 %collective-permute-start.18 = (bf16[2,2,128,256]{3,2,1,0:T(8,128)(2,1)S(1)}, bf16[2,2,128,256]{3,2,1,0:T(8,128)(2,1)S(1)}, u32[]{:S(2)}, u32[]{:S(2)}) collective-permute-start(bf16[2,2,128,256]{3,2,1,0:T(8,128)(2,1)S(1)} %pad_maximum_fusion.6.refs_12_), channel_id=1, source_target_pairs={{0,2},{1,3},{2,0},{3,1},{4,6},{5,7},{6,4},{7,5},{8,10},{9,11},{10,... | collective-permute-start | bytes 786440 | tf_op jit(solution)/shard_map/ppermute | solution.py:28
  32.3 0.3 collective-permute-done.11.refs_5_
  32.6 0.2 collective-permute-start.17
  32.8 0.3 collective-permute-start.13
  33.1 4.5 %collective-permute-done.22.refs_17_ = bf16[2,2,128,256]{3,2,1,0:T(8,128)(2,1)S(1)} collective-permute-done((bf16[2,2,128,256]{3,2,1,0:T(8,128)(2,1)S(1)}, bf16[2,2,128,256]{3,2,1,0:T(8,128)(2,1)S(1)}, u32[]{:S(2)}, u32[]{:S(2)}) %collective-permute-start.22) | collective-permute-done | bytes 262176 | tf_op jit(solution)/shard_map/ppermute | solution.py:28
  37.6 1.5 %collective-permute-done.18.refs_13_ = bf16[2,2,128,256]{3,2,1,0:T(8,128)(2,1)S(1)} collective-permute-done((bf16[2,2,128,256]{3,2,1,0:T(8,128)(2,1)S(1)}, bf16[2,2,128,256]{3,2,1,0:T(8,128)(2,1)S(1)}, u32[]{:S(2)}, u32[]{:S(2)}) %collective-permute-start.18) | collective-permute-done | bytes 262176 | tf_op jit(solution)/shard_map/ppermute | solution.py:28
  39.2 1.5 %collective-permute-done.20.refs_15_ = bf16[2,2,128,256]{3,2,1,0:T(8,128)(2,1)S(1)} collective-permute-done((bf16[2,2,128,256]{3,2,1,0:T(8,128)(2,1)S(1)}, bf16[2,2,128,256]{3,2,1,0:T(8,128)(2,1)S(1)}, u32[]{:S(2)}, u32[]{:S(2)}) %collective-permute-start.20) | collective-permute-done | bytes 262176 | tf_op jit(solution)/shard_map/ppermute | solution.py:28
  40.6 17.4 %experts.1 = (bf16[2,2,2,2,128,256]{5,4,3,2,1,0:T(8,128)(2,1)S(1)}, bf16[2,2,2,2,128,256]{5,4,3,2,1,0:T(8,128)(2,1)S(1)}, bf16[2,2,2,2,128,256]{5,4,3,2,1,0:T(8,...) custom-call(s32[3]{0:T(128)S(1)} %pad_add_fusion.where_ref.refs_0_, bf16[8,16,256]{2,1,0:T(8,128)(2,1)S(1)} %bitcast.123, ...), custom_call_target="tpu_custom_call" | custom-call | tf_op jit(solution)/shard_map/experts/pallas_call | solution.py:555
  58.0 0.2 collective-permute-start.25
  58.2 2.7 %shard_map.193 = (f32[128,1024]{1,0:T(8,128)S(1)}, f32[128,1024]{1,0:T(8,128)S(1)}, bf16[128,1024]{1,0:T(8,128)(2,1)S(1)}, bf16[512,128]{1,0:T(8,128)(2,1)S(1)}) custom-call(bf16[128,1024]{1,0:T(8,128)(2,1)} %refs_7_.1, bf16[256,128]{1,0:T(8,128)(2,1)} %bitcast.155, bf16[256,128]{1,0:T(8,128)(2,1)} %bitcast.146, f32[16,128]{1,0:T(8,128)} %bitcast.160, ...), custom_call_target="tpu_custom_call" | custom-call | tf_op jit(solution)/shard_map/pallas_call | solution.py:70
  60.9 1.5 %collective-permute-start = (bf16[512,128]{1,0:T(8,128)(2,1)S(1)}, bf16[512,128]{1,0:T(8,128)(2,1)S(1)}, u32[]{:S(2)}, u32[]{:S(2)}) collective-permute-start(bf16[512,128]{1,0:T(8,128)(2,1)S(1)} %get-tuple-element.21), channel_id=1, source_target_pairs={{0,16},{8,24},{16,0},{24,8},{1,17},{9,25},{17,1},{25,9},{2,18},{10... | collective-permute-start | bytes 393224 | tf_op jit(solution)/shard_map/ppermute | solution.py:28
  62.4 1.4 %collective-permute-start.8 = (bf16[128,1024]{1,0:T(8,128)(2,1)S(1)}, bf16[128,1024]{1,0:T(8,128)(2,1)S(1)}, u32[]{:S(2)}, u32[]{:S(2)}) collective-permute-start(bf16[128,1024]{1,0:T(8,128)(2,1)S(1)} %get-tuple-element.26), channel_id=1, source_target_pairs={{0,4},{4,0},{1,5},{5,1},{2,6},{6,2},{3,7},{7,3},{8,12},{12,8},{9,1... | collective-permute-start | bytes 786440 | tf_op jit(solution)/shard_map/ppermute | solution.py:967
  63.8 6.6 %collective-permute-done = bf16[512,128]{1,0:T(8,128)(2,1)S(1)} collective-permute-done((bf16[512,128]{1,0:T(8,128)(2,1)S(1)}, bf16[512,128]{1,0:T(8,128)(2,1)S(1)}, u32[]{:S(2)}, u32[]{:S(2)}) %collective-permute-start) | collective-permute-done | bytes 131104 | tf_op jit(solution)/shard_map/ppermute | solution.py:28
  70.5 0.1 collective-permute-start.1
  70.6 0.2 collective-permute-done.8.other_ref
  70.7 0.8 shard_map.197
  71.5 2.0 %collective-permute-start.9 = (bf16[128,1024]{1,0:T(8,128)(2,1)S(1)}, bf16[128,1024]{1,0:T(8,128)(2,1)S(1)}, u32[]{:S(2)}, u32[]{:S(2)}) collective-permute-start(bf16[128,1024]{1,0:T(8,128)(2,1)S(1)} %get-tuple-element.28), channel_id=1, source_target_pairs={{0,8},{8,0},{16,24},{24,16},{1,9},{9,1},{17,25},{25,17},{2,10},{10... | collective-permute-start | bytes 786440 | tf_op jit(solution)/shard_map/ppermute | solution.py:969
  73.5 6.3 %collective-permute-done.1 = bf16[2,512,128]{2,1,0:T(8,128)(2,1)S(1)} collective-permute-done((bf16[2,512,128]{2,1,0:T(8,128)(2,1)S(1)}, bf16[2,512,128]{2,1,0:T(8,128)(2,1)S(1)}, u32[]{:S(2)}, u32[]{:S(2)}) %collective-permute-start.1) | collective-permute-done | bytes 262176 | tf_op jit(solution)/shard_map/ppermute | solution.py:28
  79.8 0.7 collective-permute-start.2
  80.5 3.7 %collective-permute-done.9.other_ref = bf16[128,1024]{1,0:T(8,128)(2,1)S(1)} collective-permute-done((bf16[128,1024]{1,0:T(8,128)(2,1)S(1)}, bf16[128,1024]{1,0:T(8,128)(2,1)S(1)}, u32[]{:S(2)}, u32[]{:S(2)}) %collective-permute-start.9) | collective-permute-done | bytes 262176 | tf_op jit(solution)/shard_map/ppermute | solution.py:969
  84.2 1.6 %shard_map.198 = (f32[128,1024]{1,0:T(8,128)S(1)}, f32[128,1024]{1,0:T(8,128)}, bf16[128,1024]{1,0:T(8,128)(2,1)S(1)}) custom-call(s32[3]{0:T(128)S(1)} %pad_add_fusion.where_ref.refs_0_, bf16[8,16,256]{2,1,0:T(8,128)(2,1)S(1)} %bitcast.125, bf16[128,1024]{1,0:T(8,128)(2,1)S(1)} %collective-permute-done.9.other_ref, ...), custom_call_target="tpu_custom_call" | custom-call | tf_op jit(solution)/shard_map/pallas_call | solution.py:754
  85.9 3.5 %collective-permute-start.10 = (bf16[128,1024]{1,0:T(8,128)(2,1)S(1)}, bf16[128,1024]{1,0:T(8,128)(2,1)S(1)}, u32[]{:S(2)}, u32[]{:S(2)}) collective-permute-start(bf16[128,1024]{1,0:T(8,128)(2,1)S(1)} %get-tuple-element.31), channel_id=1, source_target_pairs={{0,16},{8,24},{1,17},{9,25},{2,18},{10,26},{3,19},{11,27},{4,20},{... | collective-permute-start | bytes 786440 | tf_op jit(solution)/shard_map/ppermute | solution.py:980
  89.4 0.3 fusion.33
  89.8 0.8 collective-permute-start.28
  90.6 1.4 %collective-permute-start.26 = (bf16[2,2,128,256]{3,2,1,0:T(8,128)(2,1)S(1)}, bf16[2,2,128,256]{3,2,1,0:T(8,128)(2,1)S(1)}, u32[]{:S(2)}, u32[]{:S(2)}) collective-permute-start(bf16[2,2,128,256]{3,2,1,0:T(8,128)(2,1)S(1)} %get-tuple-element.50), channel_id=1, source_target_pairs={{0,2},{1,3},{2,0},{3,1},{4,6},{5,7},{6,4},{7,5},{8,10},{9,11},{10,... | collective-permute-start | bytes 786440 | tf_op jit(solution)/shard_map/ppermute | solution.py:28
  92.0 0.4 fusion.34
  92.4 1.4 %collective-permute-start.34 = (bf16[2,2,128,256]{3,2,1,0:T(8,128)(2,1)S(1)}, bf16[2,2,128,256]{3,2,1,0:T(8,128)(2,1)S(1)}, u32[]{:S(2)}, u32[]{:S(2)}) collective-permute-start(bf16[2,2,128,256]{3,2,1,0:T(8,128)(2,1)S(1)} %get-tuple-element.47), channel_id=1, source_target_pairs={{0,4},{4,0},{1,5},{5,1},{2,6},{6,2},{3,7},{7,3},{8,12},{12,8},{9,1... | collective-permute-start | bytes 786440 | tf_op jit(solution)/shard_map/ppermute | solution.py:28
  93.8 5.2 %collective-permute-done.28 = bf16[2,2,128,256]{3,2,1,0:T(8,128)(2,1)S(1)} collective-permute-done((bf16[2,2,128,256]{3,2,1,0:T(8,128)(2,1)S(1)}, bf16[2,2,128,256]{3,2,1,0:T(8,128)(2,1)S(1)}, u32[]{:S(2)}, u32[]{:S(2)}) %collective-permute-start.28) | collective-permute-done | bytes 262176 | tf_op jit(solution)/shard_map/ppermute | solution.py:28
  99.0 1.5 %collective-permute-start.32 = (bf16[2,2,128,256]{3,2,1,0:T(8,128)(2,1)S(1)}, bf16[2,2,128,256]{3,2,1,0:T(8,128)(2,1)S(1)}, u32[]{:S(2)}, u32[]{:S(2)}) collective-permute-start(bf16[2,2,128,256]{3,2,1,0:T(8,128)(2,1)S(1)} %get-tuple-element.48), channel_id=1, source_target_pairs={{0,2},{1,3},{2,0},{3,1},{4,6},{5,7},{6,4},{7,5},{8,10},{9,11},{10,... | collective-permute-start | bytes 786440 | tf_op jit(solution)/shard_map/ppermute | solution.py:28
  100.5 0.1 fusion.2
  100.7 0.7 collective-permute-start.27
  101.4 2.9 %collective-permute-done.34 = bf16[2,2,128,256]{3,2,1,0:T(8,128)(2,1)S(1)} collective-permute-done((bf16[2,2,128,256]{3,2,1,0:T(8,128)(2,1)S(1)}, bf16[2,2,128,256]{3,2,1,0:T(8,128)(2,1)S(1)}, u32[]{:S(2)}, u32[]{:S(2)}) %collective-permute-start.34) | collective-permute-done | bytes 262176 | tf_op jit(solution)/shard_map/ppermute | solution.py:28
  104.3 1.5 %collective-permute-start.29 = (bf16[2,128,256]{2,1,0:T(8,128)(2,1)S(1)}, bf16[2,128,256]{2,1,0:T(8,128)(2,1)S(1)}, u32[]{:S(2)}, u32[]{:S(2)}) collective-permute-start(bf16[2,128,256]{2,1,0:T(8,128)(2,1)S(1)} %fusion.22), channel_id=1, source_target_pairs={{0,2},{1,3},{2,0},{3,1},{4,6},{5,7},{6,4},{7,5},{8,10},{9,11},{10,... | collective-permute-start | bytes 393224 | tf_op jit(solution)/shard_map/ppermute | solution.py:28
  105.8 1.0 collective-permute-done.32
  106.8 0.1 fusion
  106.9 0.8 collective-permute-start.33
  107.8 4.2 %collective-permute-done.33 = bf16[2,128,256]{2,1,0:T(8,128)(2,1)S(1)} collective-permute-done((bf16[2,128,256]{2,1,0:T(8,128)(2,1)S(1)}, bf16[2,128,256]{2,1,0:T(8,128)(2,1)S(1)}, u32[]{:S(2)}, u32[]{:S(2)}) %collective-permute-start.33) | collective-permute-done | bytes 131104 | tf_op jit(solution)/shard_map/ppermute | solution.py:28
  112.0 1.5 %collective-permute-start.35 = (bf16[2,128,256]{2,1,0:T(8,128)(2,1)S(1)}, bf16[2,128,256]{2,1,0:T(8,128)(2,1)S(1)}, u32[]{:S(2)}, u32[]{:S(2)}) collective-permute-start(bf16[2,128,256]{2,1,0:T(8,128)(2,1)S(1)} %fusion.25), channel_id=1, source_target_pairs={{0,2},{1,3},{2,0},{3,1},{4,6},{5,7},{6,4},{7,5},{8,10},{9,11},{10,... | collective-permute-start | bytes 393224 | tf_op jit(solution)/shard_map/ppermute | solution.py:28
  113.5 3.4 %collective-permute-done.35 = bf16[2,128,256]{2,1,0:T(8,128)(2,1)S(1)} collective-permute-done((bf16[2,128,256]{2,1,0:T(8,128)(2,1)S(1)}, bf16[2,128,256]{2,1,0:T(8,128)(2,1)S(1)}, u32[]{:S(2)}, u32[]{:S(2)}) %collective-permute-start.35) | collective-permute-done | bytes 131104 | tf_op jit(solution)/shard_map/ppermute | solution.py:28
  117.0 1.8 %collective-permute-start.36 = (bf16[128,512]{1,0:T(8,128)(2,1)S(1)}, bf16[128,512]{1,0:T(8,128)(2,1)S(1)}, u32[]{:S(2)}, u32[]{:S(2)}) collective-permute-start(bf16[128,512]{1,0:T(8,128)(2,1)S(1)} %fusion.26), channel_id=1, source_target_pairs={{0,8},{8,0},{16,24},{24,16},{1,9},{9,1},{17,25},{25,17},{2,10},{10... | collective-permute-start | bytes 393224 | tf_op jit(solution)/shard_map/ppermute | solution.py:28
  118.9 0.4 collective-permute-start.30
  119.2 2.9 %collective-permute-done.36 = bf16[128,512]{1,0:T(8,128)(2,1)S(1)} collective-permute-done((bf16[128,512]{1,0:T(8,128)(2,1)S(1)}, bf16[128,512]{1,0:T(8,128)(2,1)S(1)}, u32[]{:S(2)}, u32[]{:S(2)}) %collective-permute-start.36) | collective-permute-done | bytes 131104 | tf_op jit(solution)/shard_map/ppermute | solution.py:28
  122.2 2.1 %collective-permute-start.37 = (bf16[128,512]{1,0:T(8,128)(2,1)S(1)}, bf16[128,512]{1,0:T(8,128)(2,1)S(1)}, u32[]{:S(2)}, u32[]{:S(2)}) collective-permute-start(bf16[128,512]{1,0:T(8,128)(2,1)S(1)} %fusion.7), channel_id=1, source_target_pairs={{0,16},{8,24},{16,0},{24,8},{1,17},{9,25},{17,1},{25,9},{2,18},{10... | collective-permute-start | bytes 393224 | tf_op jit(solution)/shard_map/ppermute | solution.py:28
  124.3 1.2 shard_map.194
  125.5 1.9 %shard_map.195 = bf16[1024,128]{1,0:T(8,128)(2,1)} custom-call(s32[3]{0:T(128)S(1)} %pad_add_fusion.where_ref.refs_0_, bf16[1024,128]{1,0:T(8,128)(2,1)S(1)} %bitcast.131, bf16[4,512,128]{2,1,0:T(8,128)(2,1)S(1)} %bitcast.132, f32[1024,128]{1,0:T(8,128)S(1)} %get-tuple-element.22.refs_1_, f32[1024,128]{1,0:T(8,128)S(1)} %get-tuple-element.23.refs_2_, ...), custom_call_target="tpu_custom_call" | custom-call | tf_op jit(solution)/shard_map/pallas_call | solution.py:167
  127.4 3.3 %shard_map.199 = bf16[128,1024]{1,0:T(8,128)(2,1)} custom-call(s32[3]{0:T(128)S(1)} %pad_add_fusion.where_ref.refs_0_, bf16[8,16,256]{2,1,0:T(8,128)(2,1)S(1)} %bitcast.126, bf16[128,1024]{1,0:T(8,128)(2,1)S(1)} %collective-permute-done.10.refs_2_, f32[128,1024]{1,0:T(8,128)S(1)} %get-tuple-element.32.refs_3_, f32[128,1024]{1,0:T(8,128)S(1)} %get-tuple-element.33.refs_4_, ...), custom_call_target="tpu_custom_call" | custom-call | tf_op jit(solution)/shard_map/pallas_call | solution.py:70
  130.8 0.7 fusion.12
  (62 shorter events, 0.9 us)
Async XLA Ops:
  2.9 9.5 %collective-permute-start.3 = (bf16[144,512]{1,0:T(8,128)(2,1)S(1)}, bf16[144,512]{1,0:T(8,128)(2,1)S(1)}, u32[]{:S(2)}, u32[]{:S(2)}) collective-permute-start(bf16[144,512]{1,0:T(8,128)(2,1)S(1)} %get-tuple-element.25), channel_id=1, source_target_pairs={{0,8},{8,0},{16,24},{24,16},{1,9},{9,1},{17,25},{25,17},{2,10},{10... | collective-permute-start | bytes 442376 | tf_op jit(solution)/shard_map/ppermute | solution.py:28
  6.0 9.9 %collective-permute-start.5 = (bf16[144,512]{1,0:T(8,128)(2,1)S(1)}, bf16[144,512]{1,0:T(8,128)(2,1)S(1)}, u32[]{:S(2)}, u32[]{:S(2)}) collective-permute-start(bf16[144,512]{1,0:T(8,128)(2,1)S(1)} %get-tuple-element.25), channel_id=1, source_target_pairs={{0,16},{8,24},{16,0},{24,8},{1,17},{9,25},{17,1},{25,9},{2,18},{10... | collective-permute-start | bytes 442376 | tf_op jit(solution)/shard_map/ppermute | solution.py:28
  12.4 4.3 %collective-permute-start.14 = (bf16[1,128,256]{2,1,0:T(8,128)(2,1)S(1)}, bf16[1,128,256]{2,1,0:T(8,128)(2,1)S(1)}, u32[]{:S(2)}, u32[]{:S(2)}) collective-permute-start(bf16[1,128,256]{2,1,0:T(8,128)(2,1)S(1)} %slice.157), channel_id=1, source_target_pairs={{0,2},{1,3},{2,0},{3,1},{4,6},{5,7},{6,4},{7,5},{8,10},{9,11},{10,... | collective-permute-start | bytes 196616 | tf_op jit(solution)/shard_map/ppermute | solution.py:28
  14.3 9.5 %collective-permute-start.4 = (bf16[2,144,256]{2,1,0:T(8,128)(2,1)S(1)}, bf16[2,144,256]{2,1,0:T(8,128)(2,1)S(1)}, u32[]{:S(2)}, u32[]{:S(2)}) collective-permute-start(bf16[2,144,256]{2,1,0:T(8,128)(2,1)S(1)} %fusion.20), channel_id=1, source_target_pairs={{0,4},{4,0},{1,5},{5,1},{2,6},{6,2},{3,7},{7,3},{8,12},{12,8},{9,1... | collective-permute-start | bytes 442376 | tf_op jit(solution)/shard_map/ppermute | solution.py:28
  15.9 5.2 %collective-permute-start.6 = (bf16[144,512]{1,0:T(8,128)(2,1)S(1)}, bf16[144,512]{1,0:T(8,128)(2,1)S(1)}, u32[]{:S(2)}, u32[]{:S(2)}) collective-permute-start(bf16[144,512]{1,0:T(8,128)(2,1)S(1)} %collective-permute-done.5), channel_id=1, source_target_pairs={{0,8},{8,0},{16,24},{24,16},{1,9},{9,1},{17,25},{25,17},{2,10},{10... | collective-permute-start | bytes 442376 | tf_op jit(solution)/shard_map/ppermute | solution.py:28
  16.8 12.1 %collective-permute-start.16 = (bf16[2,2,128,256]{3,2,1,0:T(8,128)(2,1)S(1)}, bf16[2,2,128,256]{3,2,1,0:T(8,128)(2,1)S(1)}, u32[]{:S(2)}, u32[]{:S(2)}) collective-permute-start(bf16[2,2,128,256]{3,2,1,0:T(8,128)(2,1)S(1)} %pad_maximum_fusion.5.refs_8_), channel_id=1, source_target_pairs={{0,1},{1,0},{2,3},{3,2},{4,5},{5,4},{6,7},{7,6},{8,9},{9,8},{10,11... | collective-permute-start | bytes 786440 | tf_op jit(solution)/shard_map/ppermute | solution.py:28
  16.8 13.8 %collective-permute-start.15 = (bf16[2,2,128,256]{3,2,1,0:T(8,128)(2,1)S(1)}, bf16[2,2,128,256]{3,2,1,0:T(8,128)(2,1)S(1)}, u32[]{:S(2)}, u32[]{:S(2)}) collective-permute-start(bf16[2,2,128,256]{3,2,1,0:T(8,128)(2,1)S(1)} %pad_maximum_fusion.5.refs_8_), channel_id=1, source_target_pairs={{0,4},{4,0},{1,5},{5,1},{2,6},{6,2},{3,7},{7,3},{8,12},{12,8},{9,1... | collective-permute-start | bytes 786440 | tf_op jit(solution)/shard_map/ppermute | solution.py:28
  21.1 5.0 %collective-permute-start.21 = (bf16[2,128,256]{2,1,0:T(8,128)(2,1)S(1)}, bf16[2,128,256]{2,1,0:T(8,128)(2,1)S(1)}, u32[]{:S(2)}, u32[]{:S(2)}) collective-permute-start(bf16[2,128,256]{2,1,0:T(8,128)(2,1)S(1)} %get-tuple-element.51), channel_id=1, source_target_pairs={{0,2},{1,3},{2,0},{3,1},{4,6},{5,7},{6,4},{7,5},{8,10},{9,11},{10,... | collective-permute-start | bytes 393224 | tf_op jit(solution)/shard_map/ppermute | solution.py:28
  22.2 6.6 %collective-permute-start.7 = (bf16[2,144,256]{2,1,0:T(8,128)(2,1)S(1)}, bf16[2,144,256]{2,1,0:T(8,128)(2,1)S(1)}, u32[]{:S(2)}, u32[]{:S(2)}) collective-permute-start(bf16[2,144,256]{2,1,0:T(8,128)(2,1)S(1)} %fusion.19), channel_id=1, source_target_pairs={{0,4},{4,0},{1,5},{5,1},{2,6},{6,2},{3,7},{7,3},{8,12},{12,8},{9,1... | collective-permute-start | bytes 442376 | tf_op jit(solution)/shard_map/ppermute | solution.py:28
  23.8 8.4 %collective-permute-start.12 = (bf16[2,2,128,256]{3,2,1,0:T(8,128)(2,1)S(1)}, bf16[2,2,128,256]{3,2,1,0:T(8,128)(2,1)S(1)}, u32[]{:S(2)}, u32[]{:S(2)}) collective-permute-start(bf16[2,2,128,256]{3,2,1,0:T(8,128)(2,1)S(1)} %pad_maximum_fusion.4.refs_4_), channel_id=1, source_target_pairs={{0,1},{1,0},{2,3},{3,2},{4,5},{5,4},{6,7},{7,6},{8,9},{9,8},{10,11... | collective-permute-start | bytes 786440 | tf_op jit(solution)/shard_map/ppermute | solution.py:28
  26.2 6.4 %collective-permute-start.11 = (bf16[2,2,128,256]{3,2,1,0:T(8,128)(2,1)S(1)}, bf16[2,2,128,256]{3,2,1,0:T(8,128)(2,1)S(1)}, u32[]{:S(2)}, u32[]{:S(2)}) collective-permute-start(bf16[2,2,128,256]{3,2,1,0:T(8,128)(2,1)S(1)} %pad_maximum_fusion.4.refs_4_), channel_id=1, source_target_pairs={{0,2},{1,3},{2,0},{3,1},{4,6},{5,7},{6,4},{7,5},{8,10},{9,11},{10,... | collective-permute-start | bytes 786440 | tf_op jit(solution)/shard_map/ppermute | solution.py:28
  28.8 4.0 %collective-permute-start.23 = (bf16[2,2,128,256]{3,2,1,0:T(8,128)(2,1)S(1)}, bf16[2,2,128,256]{3,2,1,0:T(8,128)(2,1)S(1)}, u32[]{:S(2)}, u32[]{:S(2)}) collective-permute-start(bf16[2,2,128,256]{3,2,1,0:T(8,128)(2,1)S(1)} %pad_maximum_fusion.7.refs_16_), channel_id=1, source_target_pairs={{0,1},{1,0},{2,3},{3,2},{4,5},{5,4},{6,7},{7,6},{8,9},{9,8},{10,11... | collective-permute-start | bytes 786440 | tf_op jit(solution)/shard_map/ppermute | solution.py:28
  28.8 8.8 %collective-permute-start.22 = (bf16[2,2,128,256]{3,2,1,0:T(8,128)(2,1)S(1)}, bf16[2,2,128,256]{3,2,1,0:T(8,128)(2,1)S(1)}, u32[]{:S(2)}, u32[]{:S(2)}) collective-permute-start(bf16[2,2,128,256]{3,2,1,0:T(8,128)(2,1)S(1)} %pad_maximum_fusion.7.refs_16_), channel_id=1, source_target_pairs={{0,4},{4,0},{1,5},{5,1},{2,6},{6,2},{3,7},{7,3},{8,12},{12,8},{9,1... | collective-permute-start | bytes 786440 | tf_op jit(solution)/shard_map/ppermute | solution.py:28
  30.6 8.4 %collective-permute-start.18 = (bf16[2,2,128,256]{3,2,1,0:T(8,128)(2,1)S(1)}, bf16[2,2,128,256]{3,2,1,0:T(8,128)(2,1)S(1)}, u32[]{:S(2)}, u32[]{:S(2)}) collective-permute-start(bf16[2,2,128,256]{3,2,1,0:T(8,128)(2,1)S(1)} %pad_maximum_fusion.6.refs_12_), channel_id=1, source_target_pairs={{0,2},{1,3},{2,0},{3,1},{4,6},{5,7},{6,4},{7,5},{8,10},{9,11},{10,... | collective-permute-start | bytes 786440 | tf_op jit(solution)/shard_map/ppermute | solution.py:28
  32.2 6.9 %collective-permute-start.19 = (bf16[2,2,128,256]{3,2,1,0:T(8,128)(2,1)S(1)}, bf16[2,2,128,256]{3,2,1,0:T(8,128)(2,1)S(1)}, u32[]{:S(2)}, u32[]{:S(2)}) collective-permute-start(bf16[2,2,128,256]{3,2,1,0:T(8,128)(2,1)S(1)} %pad_maximum_fusion.6.refs_12_), channel_id=1, source_target_pairs={{0,1},{1,0},{2,3},{3,2},{4,5},{5,4},{6,7},{7,6},{8,9},{9,8},{10,11... | collective-permute-start | bytes 786440 | tf_op jit(solution)/shard_map/ppermute | solution.py:28
  32.6 6.5 %collective-permute-start.17 = (bf16[2,2,128,256]{3,2,1,0:T(8,128)(2,1)S(1)}, bf16[2,2,128,256]{3,2,1,0:T(8,128)(2,1)S(1)}, u32[]{:S(2)}, u32[]{:S(2)}) collective-permute-start(bf16[2,2,128,256]{3,2,1,0:T(8,128)(2,1)S(1)} %collective-permute-done.15.refs_9_), channel_id=1, source_target_pairs={{0,1},{1,0},{2,3},{3,2},{4,5},{5,4},{6,7},{7,6},{8,9},{9,8},{10,11... | collective-permute-start | bytes 786440 | tf_op jit(solution)/shard_map/ppermute | solution.py:28
  32.8 6.4 %collective-permute-start.13 = (bf16[2,2,128,256]{3,2,1,0:T(8,128)(2,1)S(1)}, bf16[2,2,128,256]{3,2,1,0:T(8,128)(2,1)S(1)}, u32[]{:S(2)}, u32[]{:S(2)}) collective-permute-start(bf16[2,2,128,256]{3,2,1,0:T(8,128)(2,1)S(1)} %collective-permute-done.11.refs_5_), channel_id=1, source_target_pairs={{0,1},{1,0},{2,3},{3,2},{4,5},{5,4},{6,7},{7,6},{8,9},{9,8},{10,11... | collective-permute-start | bytes 786440 | tf_op jit(solution)/shard_map/ppermute | solution.py:28
  37.6 1.5 %collective-permute-start.24 = (bf16[2,2,128,256]{3,2,1,0:T(8,128)(2,1)S(1)}, bf16[2,2,128,256]{3,2,1,0:T(8,128)(2,1)S(1)}, u32[]{:S(2)}, u32[]{:S(2)}) collective-permute-start(bf16[2,2,128,256]{3,2,1,0:T(8,128)(2,1)S(1)} %collective-permute-done.22.refs_17_), channel_id=1, source_target_pairs={{0,1},{1,0},{2,3},{3,2},{4,5},{5,4},{6,7},{7,6},{8,9},{9,8},{10,11... | collective-permute-start | bytes 786440 | tf_op jit(solution)/shard_map/ppermute | solution.py:28
  39.1 1.5 %collective-permute-start.20 = (bf16[2,2,128,256]{3,2,1,0:T(8,128)(2,1)S(1)}, bf16[2,2,128,256]{3,2,1,0:T(8,128)(2,1)S(1)}, u32[]{:S(2)}, u32[]{:S(2)}) collective-permute-start(bf16[2,2,128,256]{3,2,1,0:T(8,128)(2,1)S(1)} %collective-permute-done.18.refs_13_), channel_id=1, source_target_pairs={{0,1},{1,0},{2,3},{3,2},{4,5},{5,4},{6,7},{7,6},{8,9},{9,8},{10,11... | collective-permute-start | bytes 786440 | tf_op jit(solution)/shard_map/ppermute | solution.py:28
  58.0 31.3 %collective-permute-start.25 = (bf16[2,2,2,2,128,256]{5,4,3,2,1,0:T(8,128)(2,1)S(1)}, bf16[2,2,2,2,128,256]{5,4,3,2,1,0:T(8,128)(2,1)S(1)}, u32[]{:S(2)}, u32[]{:S(2)}) collective-permute-start(bf16[2,2,2,2,128,256]{5,4,3,2,1,0:T(8,128)(2,1)S(1)} %get-tuple-element.36), channel_id=1, source_target_pairs={{0,1},{1,0},{2,3},{3,2},{4,5},{5,4},{6,7},{7,6},{8,9},{9,8},{10,11... | collective-permute-start | bytes 3145736 | tf_op jit(solution)/shard_map/ppermute | solution.py:28
  60.9 9.5 %collective-permute-start = (bf16[512,128]{1,0:T(8,128)(2,1)S(1)}, bf16[512,128]{1,0:T(8,128)(2,1)S(1)}, u32[]{:S(2)}, u32[]{:S(2)}) collective-permute-start(bf16[512,128]{1,0:T(8,128)(2,1)S(1)} %get-tuple-element.21), channel_id=1, source_target_pairs={{0,16},{8,24},{16,0},{24,8},{1,17},{9,25},{17,1},{25,9},{2,18},{10... | collective-permute-start | bytes 393224 | tf_op jit(solution)/shard_map/ppermute | solution.py:28
  62.4 8.3 %collective-permute-start.8 = (bf16[128,1024]{1,0:T(8,128)(2,1)S(1)}, bf16[128,1024]{1,0:T(8,128)(2,1)S(1)}, u32[]{:S(2)}, u32[]{:S(2)}) collective-permute-start(bf16[128,1024]{1,0:T(8,128)(2,1)S(1)} %get-tuple-element.26), channel_id=1, source_target_pairs={{0,4},{4,0},{1,5},{5,1},{2,6},{6,2},{3,7},{7,3},{8,12},{12,8},{9,1... | collective-permute-start | bytes 786440 | tf_op jit(solution)/shard_map/ppermute | solution.py:967
  63.8 28.2 %collective-permute-start.31 = (bf16[2,2,2,2,128,256]{5,4,3,2,1,0:T(8,128)(2,1)S(1)}, bf16[2,2,2,2,128,256]{5,4,3,2,1,0:T(8,128)(2,1)S(1)}, u32[]{:S(2)}, u32[]{:S(2)}) collective-permute-start(bf16[2,2,2,2,128,256]{5,4,3,2,1,0:T(8,128)(2,1)S(1)} %get-tuple-element.38), channel_id=1, source_target_pairs={{0,1},{1,0},{2,3},{3,2},{4,5},{5,4},{6,7},{7,6},{8,9},{9,8},{10,11... | collective-permute-start | bytes 3145736 | tf_op jit(solution)/shard_map/ppermute | solution.py:28
  70.5 9.2 %collective-permute-start.1 = (bf16[2,512,128]{2,1,0:T(8,128)(2,1)S(1)}, bf16[2,512,128]{2,1,0:T(8,128)(2,1)S(1)}, u32[]{:S(2)}, u32[]{:S(2)}) collective-permute-start(bf16[2,512,128]{2,1,0:T(8,128)(2,1)S(1)} %get-tuple-element.56), channel_id=1, source_target_pairs={{0,8},{8,0},{16,24},{24,16},{1,9},{9,1},{17,25},{25,17},{2,10},{10... | collective-permute-start | bytes 786440 | tf_op jit(solution)/shard_map/ppermute | solution.py:28
  71.5 12.7 %collective-permute-start.9 = (bf16[128,1024]{1,0:T(8,128)(2,1)S(1)}, bf16[128,1024]{1,0:T(8,128)(2,1)S(1)}, u32[]{:S(2)}, u32[]{:S(2)}) collective-permute-start(bf16[128,1024]{1,0:T(8,128)(2,1)S(1)} %get-tuple-element.28), channel_id=1, source_target_pairs={{0,8},{8,0},{16,24},{24,16},{1,9},{9,1},{17,25},{25,17},{2,10},{10... | collective-permute-start | bytes 786440 | tf_op jit(solution)/shard_map/ppermute | solution.py:969
  79.8 45.7 %collective-permute-start.2 = (bf16[2,2,512,128]{3,2,1,0:T(8,128)(2,1)S(1)}, bf16[2,2,512,128]{3,2,1,0:T(8,128)(2,1)S(1)}, u32[]{:S(2)}, u32[]{:S(2)}) collective-permute-start(bf16[2,2,512,128]{3,2,1,0:T(8,128)(2,1)S(1)} %pad_maximum_fusion), channel_id=1, source_target_pairs={{0,4},{4,0},{1,5},{5,1},{2,6},{6,2},{3,7},{7,3},{8,12},{12,8},{9,1... | collective-permute-start | bytes 1572872 | tf_op jit(solution)/shard_map/ppermute | solution.py:28
  85.9 41.5 %collective-permute-start.10 = (bf16[128,1024]{1,0:T(8,128)(2,1)S(1)}, bf16[128,1024]{1,0:T(8,128)(2,1)S(1)}, u32[]{:S(2)}, u32[]{:S(2)}) collective-permute-start(bf16[128,1024]{1,0:T(8,128)(2,1)S(1)} %get-tuple-element.31), channel_id=1, source_target_pairs={{0,16},{8,24},{1,17},{9,25},{2,18},{10,26},{3,19},{11,27},{4,20},{... | collective-permute-start | bytes 786440 | tf_op jit(solution)/shard_map/ppermute | solution.py:980
  89.8 9.2 %collective-permute-start.28 = (bf16[2,2,128,256]{3,2,1,0:T(8,128)(2,1)S(1)}, bf16[2,2,128,256]{3,2,1,0:T(8,128)(2,1)S(1)}, u32[]{:S(2)}, u32[]{:S(2)}) collective-permute-start(bf16[2,2,128,256]{3,2,1,0:T(8,128)(2,1)S(1)} %get-tuple-element.49), channel_id=1, source_target_pairs={{0,4},{4,0},{1,5},{5,1},{2,6},{6,2},{3,7},{7,3},{8,12},{12,8},{9,1... | collective-permute-start | bytes 786440 | tf_op jit(solution)/shard_map/ppermute | solution.py:28
  90.6 9.9 %collective-permute-start.26 = (bf16[2,2,128,256]{3,2,1,0:T(8,128)(2,1)S(1)}, bf16[2,2,128,256]{3,2,1,0:T(8,128)(2,1)S(1)}, u32[]{:S(2)}, u32[]{:S(2)}) collective-permute-start(bf16[2,2,128,256]{3,2,1,0:T(8,128)(2,1)S(1)} %get-tuple-element.50), channel_id=1, source_target_pairs={{0,2},{1,3},{2,0},{3,1},{4,6},{5,7},{6,4},{7,5},{8,10},{9,11},{10,... | collective-permute-start | bytes 786440 | tf_op jit(solution)/shard_map/ppermute | solution.py:28
  92.4 11.9 %collective-permute-start.34 = (bf16[2,2,128,256]{3,2,1,0:T(8,128)(2,1)S(1)}, bf16[2,2,128,256]{3,2,1,0:T(8,128)(2,1)S(1)}, u32[]{:S(2)}, u32[]{:S(2)}) collective-permute-start(bf16[2,2,128,256]{3,2,1,0:T(8,128)(2,1)S(1)} %get-tuple-element.47), channel_id=1, source_target_pairs={{0,4},{4,0},{1,5},{5,1},{2,6},{6,2},{3,7},{7,3},{8,12},{12,8},{9,1... | collective-permute-start | bytes 786440 | tf_op jit(solution)/shard_map/ppermute | solution.py:28
  99.0 7.8 %collective-permute-start.32 = (bf16[2,2,128,256]{3,2,1,0:T(8,128)(2,1)S(1)}, bf16[2,2,128,256]{3,2,1,0:T(8,128)(2,1)S(1)}, u32[]{:S(2)}, u32[]{:S(2)}) collective-permute-start(bf16[2,2,128,256]{3,2,1,0:T(8,128)(2,1)S(1)} %get-tuple-element.48), channel_id=1, source_target_pairs={{0,2},{1,3},{2,0},{3,1},{4,6},{5,7},{6,4},{7,5},{8,10},{9,11},{10,... | collective-permute-start | bytes 786440 | tf_op jit(solution)/shard_map/ppermute | solution.py:28
  100.7 18.1 %collective-permute-start.27 = (bf16[2,128,256]{2,1,0:T(8,128)(2,1)S(1)}, bf16[2,128,256]{2,1,0:T(8,128)(2,1)S(1)}, u32[]{:S(2)}, u32[]{:S(2)}) collective-permute-start(bf16[2,128,256]{2,1,0:T(8,128)(2,1)S(1)} %fusion.21), channel_id=1, source_target_pairs={{0,4},{4,0},{1,5},{5,1},{2,6},{6,2},{3,7},{7,3},{8,12},{12,8},{9,1... | collective-permute-start | bytes 393224 | tf_op jit(solution)/shard_map/ppermute | solution.py:28
  104.3 14.6 %collective-permute-start.29 = (bf16[2,128,256]{2,1,0:T(8,128)(2,1)S(1)}, bf16[2,128,256]{2,1,0:T(8,128)(2,1)S(1)}, u32[]{:S(2)}, u32[]{:S(2)}) collective-permute-start(bf16[2,128,256]{2,1,0:T(8,128)(2,1)S(1)} %fusion.22), channel_id=1, source_target_pairs={{0,2},{1,3},{2,0},{3,1},{4,6},{5,7},{6,4},{7,5},{8,10},{9,11},{10,... | collective-permute-start | bytes 393224 | tf_op jit(solution)/shard_map/ppermute | solution.py:28
  106.9 5.0 %collective-permute-start.33 = (bf16[2,128,256]{2,1,0:T(8,128)(2,1)S(1)}, bf16[2,128,256]{2,1,0:T(8,128)(2,1)S(1)}, u32[]{:S(2)}, u32[]{:S(2)}) collective-permute-start(bf16[2,128,256]{2,1,0:T(8,128)(2,1)S(1)} %fusion.24), channel_id=1, source_target_pairs={{0,4},{4,0},{1,5},{5,1},{2,6},{6,2},{3,7},{7,3},{8,12},{12,8},{9,1... | collective-permute-start | bytes 393224 | tf_op jit(solution)/shard_map/ppermute | solution.py:28
  112.0 5.0 %collective-permute-start.35 = (bf16[2,128,256]{2,1,0:T(8,128)(2,1)S(1)}, bf16[2,128,256]{2,1,0:T(8,128)(2,1)S(1)}, u32[]{:S(2)}, u32[]{:S(2)}) collective-permute-start(bf16[2,128,256]{2,1,0:T(8,128)(2,1)S(1)} %fusion.25), channel_id=1, source_target_pairs={{0,2},{1,3},{2,0},{3,1},{4,6},{5,7},{6,4},{7,5},{8,10},{9,11},{10,... | collective-permute-start | bytes 393224 | tf_op jit(solution)/shard_map/ppermute | solution.py:28
  113.5 10.8 %copy-start = (bf16[128,8,128]{2,1,0:T(8,128)(2,1)S(1)}, bf16[128,8,128]{2,1,0:T(8,128)(2,1)}, u32[]{:S(2)}) copy-start(bf16[128,8,128]{2,1,0:T(8,128)(2,1)} %param.18) | copy-start | bytes 786436
  117.0 5.2 %collective-permute-start.36 = (bf16[128,512]{1,0:T(8,128)(2,1)S(1)}, bf16[128,512]{1,0:T(8,128)(2,1)S(1)}, u32[]{:S(2)}, u32[]{:S(2)}) collective-permute-start(bf16[128,512]{1,0:T(8,128)(2,1)S(1)} %fusion.26), channel_id=1, source_target_pairs={{0,8},{8,0},{16,24},{24,16},{1,9},{9,1},{17,25},{25,17},{2,10},{10... | collective-permute-start | bytes 393224 | tf_op jit(solution)/shard_map/ppermute | solution.py:28
  118.9 11.9 %collective-permute-start.30 = (bf16[128,512]{1,0:T(8,128)(2,1)S(1)}, bf16[128,512]{1,0:T(8,128)(2,1)S(1)}, u32[]{:S(2)}, u32[]{:S(2)}) collective-permute-start(bf16[128,512]{1,0:T(8,128)(2,1)S(1)} %fusion.23), channel_id=1, source_target_pairs={{0,8},{8,0},{16,24},{24,16},{1,9},{9,1},{17,25},{25,17},{2,10},{10... | collective-permute-start | bytes 393224 | tf_op jit(solution)/shard_map/ppermute | solution.py:28
  122.2 8.6 %collective-permute-start.37 = (bf16[128,512]{1,0:T(8,128)(2,1)S(1)}, bf16[128,512]{1,0:T(8,128)(2,1)S(1)}, u32[]{:S(2)}, u32[]{:S(2)}) collective-permute-start(bf16[128,512]{1,0:T(8,128)(2,1)S(1)} %fusion.7), channel_id=1, source_target_pairs={{0,16},{8,24},{16,0},{24,8},{1,17},{9,25},{17,1},{25,9},{2,18},{10... | collective-permute-start | bytes 393224 | tf_op jit(solution)/shard_map/ppermute | solution.py:28
